TPU v7x, 32 devices: a whole 2x2x4 slice. The times are simulated.
32 devices in a mesh: space: 8 (over z, y), scene: 4 (over x, core).
Axes of the slice: x: 2, y: 2, z: 4, core: 2. Of those that a mesh axis runs over, the one named last changes fastest.
Arguments:
- features: bfloat16 [4, 16, 64, 512], P('scene', 'space'), may hold values from -6 to 6
- cotangent: bfloat16 [4, 16, 64, 512], P('scene', 'space'), may hold values from -6 to 6
- weight: bfloat16 [27, 64, 64], replicated, may hold values from -0.15625 to 0.15625
- neighbours: int32 [4, 16, 27], P('scene', 'space'), may hold values from -1 to 15, as said below
- occupancy: int32 [4, 16, 512], P('scene', 'space'), may hold values 0 or 1
Outputs:
- conv_out: bfloat16 [4, 16, 64, 512], P('scene', 'space')
- grad_features: bfloat16 [4, 16, 64, 512], P('scene', 'space')
- grad_weight: float32 [27, 64, 64], replicated
Inputs may be any that keep to these rules, and one draw needn't show every extreme that they name: neighbours[s, b, 9 (a + 1) + 3 (c + 1) + (e + 1)] is the number within scene s of the active brick whose brick coordinates differ from brick b's by (a, c, e), each in -1, 0, 1, or -1 where no such brick is active; entry 13 is b itself and the relation is symmetric. Bricks 2 p to 2 (p + 1) - 1 form block p, a slab along the first brick coordinate: a neighbour at offset a = 0 lies in block p, a neighbour in block p - 1 has offset a = -1, a neighbour in block p + 1 has offset a = +1, and no neighbour lies in any other block.
All inputs are finite; a program needn't handle non-finite values. No bound on the sum of `occupancy` on one device may be relied on, other than what follows from the above.
Results may differ from a plain program's by a relative error of at most 0.001.
Values may be sent and summed in bfloat16 or wider, within the bound.
No kernel may reach another device: no remote copies, remote signals or barrier semaphores. Data moves between devices by JAX's collectives and lax.ppermute only.
A program may use at most 64 MiB of HBM per device.

v0:
```python
import math

import jax
import jax.numpy as jnp
from jax import lax
from jax.sharding import PartitionSpec as P


def with_halo(cells, sides, width):
    for axis, dim in sides:
        count = lax.axis_size(axis)
        ends = count - 1
        head = lax.slice_in_dim(cells, 0, width, axis=dim)
        tail = lax.slice_in_dim(cells, cells.shape[dim] - width, cells.shape[dim], axis=dim)
        cells = jnp.concatenate(
            [
                lax.ppermute(tail, axis, [(i, (i + 1) % count) for i in range(ends)]),
                cells,
                lax.ppermute(head, axis, [((i + 1) % count, i) for i in range(ends)]),
            ],
            axis=dim,
        )
    return cells


def bounds(offset):
    if offset == 0:
        return (7, 8)
    if offset == 1:
        return (0, 8)
    return (0, 1)


def assemble(lookup, places):
    plane_list = []
    for off_x in range(3):
        x_low, x_high = bounds(off_x)
        row_list = []
        for off_y in range(3):
            y_low, y_high = bounds(off_y)
            cell_list = []
            for off_z in range(3):
                z_low, z_high = bounds(off_z)
                section = lookup[:, :, x_low:x_high, y_low:y_high, z_low:z_high]
                cell_list.append(
                    jnp.take(section, places[:, 9 * off_x + 3 * off_y + off_z], axis=0)
                )
            row_list.append(jnp.concatenate(cell_list, axis=4))
        plane_list.append(jnp.concatenate(row_list, axis=3))
    return jnp.concatenate(plane_list, axis=2)


def window(volume, start_x, start_y, start_z):
    bricks, channels = (volume.shape[0], volume.shape[1])
    return volume[
        :, :, start_x : start_x + 8, start_y : start_y + 8, start_z : start_z + 8
    ].reshape(bricks, channels, 512)


def local(features, cotangent, weight, neighbours, occupancy):
    bricks, channels = (features.shape[1], features.shape[2])
    grad_scale = 1.0 / math.sqrt(lax.axis_size("scene") * bricks * lax.axis_size("space") * 512)
    present = occupancy[0].astype(jnp.bfloat16)[:, None, :]
    masked_x = features[0] * present
    masked_gradient = cotangent[0] * present
    stacked = jnp.stack([masked_x, masked_gradient])
    gathered = with_halo(stacked, (("space", 1),), bricks)
    zero_rows = jnp.zeros((2, 1, channels, 512), jnp.bfloat16)
    lookup = jnp.concatenate([gathered, zero_rows], axis=1).reshape(
        2, 3 * bricks + 1, channels, 8, 8, 8
    )
    offset_base = (lax.axis_index("space") - 1) * bricks
    places = jnp.where(neighbours[0] < 0, 3 * bricks, neighbours[0] - offset_base)
    volume_x = assemble(lookup[0], places)
    volume_g = assemble(lookup[1], places)
    acc_y = jnp.zeros((bricks, channels, 512), jnp.float32)
    acc_g = jnp.zeros((bricks, channels, 512), jnp.float32)
    partial_w = []
    for tap_x in range(3):
        fwd_list = []
        back_list = []
        back_weights = []
        for inner_tap in range(9):
            tap_y, tap_z = (inner_tap // 3, inner_tap % 3)
            fwd_list.append(window(volume_x, tap_x, tap_y, tap_z))
            back_list.append(window(volume_g, 2 - tap_x, 2 - tap_y, 2 - tap_z))
            back_weights.append(weight[9 * tap_x + inner_tap].T)
        forward_stacked_taps = jnp.concatenate(fwd_list, axis=1)
        backward_stacked_taps = jnp.concatenate(back_list, axis=1)
        forward_kernel_weight = weight[9 * tap_x : 9 * tap_x + 9].reshape(9 * channels, channels)
        backward_kernel_weight = jnp.concatenate(back_weights, axis=0)
        acc_y = acc_y + jnp.einsum(
            "hpo,ps->hso",
            forward_stacked_taps,
            forward_kernel_weight,
            preferred_element_type=jnp.float32,
        )
        acc_g = acc_g + jnp.einsum(
            "ish,sw->iwh",
            backward_stacked_taps,
            backward_kernel_weight,
            preferred_element_type=jnp.float32,
        )
        grouped_weight = jnp.einsum(
            "hgm,htm->gt", forward_stacked_taps, masked_gradient, preferred_element_type=jnp.float32
        )
        partial_w.append(grouped_weight.reshape(9, channels, channels))
    mask_wide = present.astype(jnp.float32)
    out_y = (acc_y * mask_wide).astype(jnp.bfloat16)[None]
    out_g = (acc_g * mask_wide).astype(jnp.bfloat16)[None]
    grad_w = jnp.concatenate(partial_w, axis=0) * grad_scale
    by_scene = lax.psum(grad_w, "scene")
    summed = lax.psum(by_scene, "space")
    return (out_y, out_g, summed)


def solution(mesh):
    in_specs = (
        P("scene", "space", None, None),
        P("scene", "space", None, None),
        P(),
        P("scene", "space", None),
        P("scene", "space", None),
    )
    out_specs = (P("scene", "space", None, None), P("scene", "space", None, None), P())
    return jax.shard_map(local, mesh=mesh, in_specs=in_specs, out_specs=out_specs, check_vma=False)
```

profile of v0, /device:TPU:0, one launch (start us, length us, event | category | flops | bytes accessed | tf_op | source)
XLA Modules:
  0.0 337.7 jit_solution(2646253069375196064)
XLA Ops:
  12.3 5.6 %collective-permute-start = (bf16[2,2,64,512]{2,3,1,0:T(8,128)(2,1)S(1)}, bf16[2,2,64,512]{2,3,1,0:T(8,128)(2,1)S(1)}, u32[]{:S(2)}, u32[]{:S(2)}) collective-permute-start(bf16[2,2,64,512]{2,3,1,0:T(8,128)(2,1)S(1)} %pad_maximum_fusion), channel_id=1, source_target_pairs={{0,4},{4,8},{8,12},{12,16},{16,20},{20,24},{24,28},{1,5},{5,9},{9,... | collective-permute-start | bytes 786440 | tf_op jit(solution)/shard_map/ppermute | solution.py:17
  88.5 1.7 copy.240
  90.2 1.7 copy.241
  91.9 1.7 copy.242
  93.7 1.7 copy.243
  95.4 1.7 copy.244
  97.1 1.7 copy.245
  100.6 1.7 copy.247
  103.3 1.8 copy.251
  113.3 1.8 copy.257
  137.1 1.7 copy.272
  140.4 1.7 copy.273
  142.1 1.7 copy.274
  157.9 1.7 copy.305
  159.6 1.7 copy.306
  164.8 1.7 copy.309
  170.0 1.8 copy.314
  173.4 1.7 copy.315
  189.1 1.7 copy.329
  205.0 1.8 convolution_bitcast_fusion
  219.7 29.3 %all-reduce.3.cloned.1.call-done = f32[27,64,64]{2,1,0:T(8,128)} async-done(((f32[27,64,64]{2,1,0:T(8,128)}), f32[27,64,64]{2,1,0:T(8,128)}) %all-reduce.3.cloned.1.call-update) | async-done | bytes 442384 | tf_op jit(solution)/shard_map/psum | solution.py:112
  249.9 2.3 fusion.5
  252.2 76.5 %all-reduce.5.cloned.1.call-done = f32[27,64,64]{2,1,0:T(8,128)} async-done(((f32[27,64,64]{2,1,0:T(8,128)}), f32[27,64,64]{2,1,0:T(8,128)}) %all-reduce.5.cloned.1.call-update) | async-done | bytes 442384 | tf_op jit(solution)/shard_map/psum | solution.py:113
  328.7 2.2 copy.476
  (660 shorter events, 172.4 us)
Async XLA Ops:
  7.2 241.8 %all-reduce.3.cloned.1.call-start = ((), (), s32[]{:S(2)}) async-start(), calls=%async_computation | async-start | bytes 1769472 | tf_op jit(solution)/shard_map/psum | solution.py:112
  10.7 16.3 %copy-start.1 = (bf16[27,64,64]{2,1,0:T(8,128)(2,1)S(1)}, bf16[27,64,64]{2,1,0:T(8,128)(2,1)}, u32[]{:S(2)}) copy-start(bf16[27,64,64]{2,1,0:T(8,128)(2,1)} %param.23) | copy-start | bytes 663556
  11.0 32.9 %collective-permute-start.1 = (bf16[2,2,64,512]{2,3,1,0:T(8,128)(2,1)S(1)}, bf16[2,2,64,512]{2,3,1,0:T(8,128)(2,1)S(1)}, u32[]{:S(2)}, u32[]{:S(2)}) collective-permute-start(bf16[2,2,64,512]{2,3,1,0:T(8,128)(2,1)S(1)} %pad_maximum_fusion), channel_id=1, source_target_pairs={{4,0},{8,4},{12,8},{16,12},{20,16},{24,20},{28,24},{5,1},{9,5},{13... | collective-permute-start | bytes 786440 | tf_op jit(solution)/shard_map/ppermute | solution.py:19
  12.3 31.6 %collective-permute-start = (bf16[2,2,64,512]{2,3,1,0:T(8,128)(2,1)S(1)}, bf16[2,2,64,512]{2,3,1,0:T(8,128)(2,1)S(1)}, u32[]{:S(2)}, u32[]{:S(2)}) collective-permute-start(bf16[2,2,64,512]{2,3,1,0:T(8,128)(2,1)S(1)} %pad_maximum_fusion), channel_id=1, source_target_pairs={{0,4},{4,8},{8,12},{12,16},{16,20},{20,24},{24,28},{1,5},{5,9},{9,... | collective-permute-start | bytes 786440 | tf_op jit(solution)/shard_map/ppermute | solution.py:17
  69.5 10.8 %copy-start.63 = (bf16[2,64,8]{1,2,0:T(8,128)(2,1)S(1)}, bf16[2,64,8]{1,2,0:T(8,128)(2,1)}, u32[]{:S(2)}) copy-start(bf16[2,64,8]{1,2,0:T(8,128)(2,1)} %gather_fusion.33) | copy-start | bytes 6148
  69.5 11.5 %copy-start.144 = (pred[2]{0:T(512)(128)(4,1)S(1)}, pred[2]{0:T(512)(128)(4,1)}, u32[]{:S(2)}) copy-start(pred[2]{0:T(512)(128)(4,1)} %get-tuple-element.248) | copy-start | bytes 10
  69.5 11.6 %copy-start.143 = (pred[2]{0:T(512)(128)(4,1)S(1)}, pred[2]{0:T(512)(128)(4,1)}, u32[]{:S(2)}) copy-start(pred[2]{0:T(512)(128)(4,1)} %get-tuple-element.249) | copy-start | bytes 10
  115.8 10.8 %copy-start.89 = (bf16[7,64,8]{1,0,2:T(8,128)(2,1)S(1)}, bf16[7,64,8]{1,0,2:T(8,128)(2,1)}, u32[]{:S(2)}) copy-start(bf16[7,64,8]{1,0,2:T(8,128)(2,1)} %get-tuple-element.50) | copy-start | bytes 21508
  115.8 10.8 %copy-start.70 = (bf16[7,64,8]{1,2,0:T(8,128)(2,1)S(1)}, bf16[7,64,8]{1,2,0:T(8,128)(2,1)}, u32[]{:S(2)}) copy-start(bf16[7,64,8]{1,2,0:T(8,128)(2,1)} %get-tuple-element.78) | copy-start | bytes 21508
  115.8 12.9 %copy-start.103 = (bf16[7,64]{1,0:T(8,128)(2,1)S(1)}, bf16[7,64]{1,0:T(8,128)(2,1)}, u32[]{:S(2)}) copy-start(bf16[7,64]{1,0:T(8,128)(2,1)} %get-tuple-element.42) | copy-start | bytes 2692
  115.9 13.6 %copy-start.155 = (pred[2]{0:T(512)(128)(4,1)S(1)}, pred[2]{0:T(512)(128)(4,1)}, u32[]{:S(2)}) copy-start(pred[2]{0:T(512)(128)(4,1)} %get-tuple-element.236) | copy-start | bytes 10
  115.9 14.2 %copy-start.153 = (pred[2]{0:T(512)(128)(4,1)S(1)}, pred[2]{0:T(512)(128)(4,1)}, u32[]{:S(2)}) copy-start(pred[2]{0:T(512)(128)(4,1)} %get-tuple-element.237) | copy-start | bytes 10
  116.7 14.1 %copy-start.154 = (pred[2]{0:T(512)(128)(4,1)S(1)}, pred[2]{0:T(512)(128)(4,1)}, u32[]{:S(2)}) copy-start(pred[2]{0:T(512)(128)(4,1)} %get-tuple-element.238) | copy-start | bytes 10
  116.7 14.7 %copy-start.152 = (pred[2]{0:T(512)(128)(4,1)S(1)}, pred[2]{0:T(512)(128)(4,1)}, u32[]{:S(2)}) copy-start(pred[2]{0:T(512)(128)(4,1)} %get-tuple-element.239) | copy-start | bytes 10
  116.7 15.4 %copy-start.142 = (pred[2]{0:T(512)(128)(4,1)S(1)}, pred[2]{0:T(512)(128)(4,1)}, u32[]{:S(2)}) copy-start(pred[2]{0:T(512)(128)(4,1)} %get-tuple-element.240) | copy-start | bytes 10
  116.7 16.1 %copy-start.151 = (pred[2]{0:T(512)(128)(4,1)S(1)}, pred[2]{0:T(512)(128)(4,1)}, u32[]{:S(2)}) copy-start(pred[2]{0:T(512)(128)(4,1)} %get-tuple-element.241) | copy-start | bytes 10
  117.4 16.0 %copy-start.150 = (pred[2]{0:T(512)(128)(4,1)S(1)}, pred[2]{0:T(512)(128)(4,1)}, u32[]{:S(2)}) copy-start(pred[2]{0:T(512)(128)(4,1)} %get-tuple-element.242) | copy-start | bytes 10
  118.1 16.0 %copy-start.149 = (pred[2]{0:T(512)(128)(4,1)S(1)}, pred[2]{0:T(512)(128)(4,1)}, u32[]{:S(2)}) copy-start(pred[2]{0:T(512)(128)(4,1)} %get-tuple-element.243) | copy-start | bytes 10
  118.1 16.6 %copy-start.148 = (pred[2]{0:T(512)(128)(4,1)S(1)}, pred[2]{0:T(512)(128)(4,1)}, u32[]{:S(2)}) copy-start(pred[2]{0:T(512)(128)(4,1)} %get-tuple-element.244) | copy-start | bytes 10
  118.1 17.2 %copy-start.60 = (bf16[2,64,8,1,8]{1,4,3,2,0:T(8,128)(2,1)S(1)}, bf16[2,64,8,1,8]{1,4,3,2,0:T(8,128)(2,1)}, u32[]{:S(2)}) copy-start(bf16[2,64,8,1,8]{1,4,3,2,0:T(8,128)(2,1)} %copy-done.59) | copy-start | bytes 49156
  118.2 17.2 %copy-start.80 = (bf16[2,64,8,1,1]{1,4,3,2,0:T(2,128)(2,1)S(1)}, bf16[2,64,8,1,1]{1,4,3,2,0:T(2,128)(2,1)}, u32[]{:S(2)}) copy-start(bf16[2,64,8,1,1]{1,4,3,2,0:T(2,128)(2,1)} %copy-done.79) | copy-start | bytes 6148
  118.2 17.2 %copy-start.82 = (bf16[2,64,8,1,1]{1,4,3,2,0:T(2,128)(2,1)S(1)}, bf16[2,64,8,1,1]{1,4,3,2,0:T(2,128)(2,1)}, u32[]{:S(2)}) copy-start(bf16[2,64,8,1,1]{1,4,3,2,0:T(2,128)(2,1)} %copy-done.81) | copy-start | bytes 6148
  211.6 117.1 %all-reduce.5.cloned.1.call-start = ((), (), s32[]{:S(2)}) async-start(), calls=%async_computation.1 | async-start | bytes 1769472 | tf_op jit(solution)/shard_map/psum | solution.py:113
  218.7 30.3 %copy-start.10 = (bf16[9,64,64]{2,1,0:T(8,128)(2,1)S(1)}, bf16[9,64,64]{2,1,0:T(8,128)(2,1)}, u32[]{:S(2)}) copy-start(bf16[9,64,64]{2,1,0:T(8,128)(2,1)} %get-tuple-element.170) | copy-start | bytes 221188
  (143 other events, 670.1 us)
Sparse Core Ops, SparseCore 0:
  211.7 37.2 all-reduce.2
  252.4 76.2 all-reduce.4
where the time goes:
time: 340 us; the launch traced here: 338 us
  local copies, waits for them, and re-layouts  158 us (46%)
  waiting for transfers between devices  106 us (31%)
  other arithmetic  42.7 us (13%)
  between operations  16.4 us (5%)
  matrix products  7.51 us (2%)
  starting transfers between devices  6.93 us (2%)
    psum x1, waiting for transfers between devices, local(): summed = lax.psum(by_scene, 'space')  76.5 us
    reshape x54, local copies, waits for them, and re-layouts, window(): return volume[:, :, start_x:start_x + 8, start_y:start_y + 8, start_z:sta...  67.4 us
    gather x54, local copies, waits for them, and re-layouts, assemble(): jnp.take(section, places[:, 9 * off_x + 3 * off_y + off_z], axis=0)  39.8 us
    psum x1, waiting for transfers between devices, local(): by_scene = lax.psum(grad_w, 'scene')  29.3 us
    unnamed x383, local copies, waits for them, and re-layouts  26.9 us
    gather x23, other arithmetic  13.7 us
    select_n x54, other arithmetic, assemble(): jnp.take(section, places[:, 9 * off_x + 3 * off_y + off_z], axis=0)  11.8 us
    slice x8, local copies, waits for them, and re-layouts, window(): volume[:, :, start_x:start_x + 8, start_y:start_y + 8, start_z:start_z + 8]  8.44 us
  transfers between devices with their start and end apart: 4, of which 2 were waited for; matrix products, arithmetic and copies ran while one was open for 10% of the time, Pallas kernels for 0%

commit v1 on v0

v1 whole, which is shorter than its diff:
```python
import functools
import math

import jax
import jax.numpy as jnp
from jax import lax
from jax.experimental import pallas as pl
from jax.experimental.pallas import tpu as pltpu
from jax.sharding import PartitionSpec as P


TILE = 128
TILES = 4
AXES = ("space", "scene")
SMEM = pl.BlockSpec(memory_space=pltpu.SMEM)
VMEM = pl.BlockSpec(memory_space=pltpu.VMEM)
HBM = pl.BlockSpec(memory_space=pltpu.HBM)
SIDES = [(c, e) for c in (-1, 0, 1) for e in (-1, 0, 1)]


def set_selection(select_y, select_z):
    row = lax.broadcasted_iota(jnp.int32, (TILE, TILE), 0)
    lane = lax.broadcasted_iota(jnp.int32, (TILE, TILE), 1)
    for select, step in ((select_y, 8), (select_z, 1)):
        now = lane // step % 8
        for t in range(3):
            moved = now + t - 1
            wanted = lane + step * (jnp.bitwise_and(moved, 7) - now)
            beyond = jnp.where(moved == jnp.bitwise_and(moved, 7), 0, 1)
            for source in range(2):
                hit = jnp.where(beyond == source, wanted, -1) == row
                select[source * TILE : (source + 1) * TILE, t * TILE : (t + 1) * TILE] = jnp.where(
                    hit, 1.0, 0.0
                ).astype(jnp.bfloat16)


def lane_of(shape):
    return lax.broadcasted_iota(jnp.int32, shape, len(shape) - 1)


def swap_halves(x):
    return pltpu.roll(x, 64, x.ndim - 1)


def on_even():
    return lax.axis_index("space") % 2 == 0


def set_groups(parts, row, pick):
    channels, rows = pick(0, 0).shape[0], parts.shape[0] // 2
    lane = lane_of((channels, TILE))
    j_high, k_high = lane % 64 >= 32, lane % 8 >= 4
    parts[row : row + channels, :TILE] = pick(0, 0)
    parts[row : row + channels, TILE:] = jnp.where(j_high, pick(-1, 0), pick(1, 0))
    row = rows + row
    parts[row : row + channels, :TILE] = jnp.where(k_high, pick(0, -1), pick(0, 1))
    parts[row : row + channels, TILE:] = jnp.where(
        j_high,
        jnp.where(k_high, pick(-1, -1), pick(-1, 1)),
        jnp.where(k_high, pick(1, -1), pick(1, 1)),
    )


def index_of(near, b, a, c, e, start, none):
    number = near[0, b, 9 * (a + 1) + 3 * (c + 1) + e + 1]
    return jnp.where(number < 0, none, number - start)


def shift_all(parts, select_y, select_z, middle, shifted, tiles):
    bricks, channels, rows = shifted.shape[0], shifted.shape[1] // 9, parts.shape[0] // 2
    for side in range(2):
        moved = jnp.dot(
            parts[side * rows : (side + 1) * rows, :], select_y[...], preferred_element_type=jnp.float32
        ).astype(jnp.bfloat16)
        for t in range(3):
            middle[t * rows : (t + 1) * rows, side * TILE : (side + 1) * TILE] = moved[:, t * TILE : (t + 1) * TILE]
    for ty in range(3):
        moved = jnp.dot(
            middle[ty * rows : (ty + 1) * rows, :], select_z[...], preferred_element_type=jnp.float32
        ).astype(jnp.bfloat16)
        for b in range(bricks):
            for q in range(tiles):
                row = (b * tiles + q) * channels
                for tz in range(3):
                    tap = 3 * ty + tz
                    shifted[b, tap * channels : (tap + 1) * channels, q * TILE : (q + 1) * TILE] = moved[
                        row : row + channels, tz * TILE : (tz + 1) * TILE
                    ]


def inner_parts(near, own, parts):
    bricks, channels = own.shape[0] - 1, own.shape[1]
    base = lax.axis_index("space") * bricks
    for b in range(bricks):
        here = {s: index_of(near, b, 0, *s, base, bricks) for s in SIDES}
        for q in range(TILES):
            set_groups(
                parts, (b * TILES + q) * channels, lambda c, e: own[here[c, e], :, q * TILE : (q + 1) * TILE]
            )


def outer_parts(near, side, first, second, from_first, from_second, low, high, parts):
    bricks, channels = first.shape[0], first.shape[1]
    even = on_even()
    zero = jnp.zeros((channels, TILE), jnp.bfloat16)

    def placed(x):
        return swap_halves(x.astype(jnp.float32)).astype(jnp.bfloat16) if side else x

    for b in range(bricks):
        high[b] = placed(jnp.where(even, from_second[b], from_first[b]))
        high[bricks + b] = placed(jnp.where(even, first[b], second[b]))
        low[b] = placed(jnp.where(even, second[b], first[b]))
        low[bricks + b] = placed(jnp.where(even, from_first[b], from_second[b]))
    high[2 * bricks] = zero
    low[2 * bricks] = zero
    base = lax.axis_index("space") * bricks
    lower = lane_of((channels, TILE)) < 64
    for b in range(bricks):
        up = {s: index_of(near, b, 1, *s, base, 2 * bricks) for s in SIDES}
        down = {s: index_of(near, b, -1, *s, base - bricks, 2 * bricks) for s in SIDES}
        set_groups(parts, b * channels, lambda c, e: jnp.where(lower, low[up[c, e]], high[down[c, e]]))


def faces_kernel(features, cotangent, mask, near, first, second, own_x, own_g, present, near_out, *rest):
    buffers, sems = rest[:3], rest[3]
    copies = [pltpu.make_async_copy(a, b, sems.at[n]) for n, (a, b) in enumerate(zip((mask, features, cotangent), buffers))]
    copies.append(pltpu.make_async_copy(near, near_out, sems.at[3]))
    for copy in copies:
        copy.start()
    even = on_even()
    bricks, channels = own_x.shape[0] - 1, own_x.shape[1]
    lower = lane_of((channels, TILE)) < 64
    copies[0].wait()
    present[...] = buffers[0][0].astype(jnp.float32)
    for side, own in enumerate((own_x, own_g)):
        copies[1 + side].wait()
        for b in range(bricks):
            own[b] = buffers[1 + side][0, b] * jnp.broadcast_to(present[b : b + 1, :], (channels, 512)).astype(
                jnp.bfloat16
            )
        own[bricks] = jnp.zeros((channels, 512), jnp.bfloat16)
    for b in range(bricks):
        x, g = own_x[b].astype(jnp.float32), own_g[b].astype(jnp.float32)
        head = jnp.where(lower, x[:, :TILE], swap_halves(g[:, :TILE])).astype(jnp.bfloat16)
        tail = jnp.where(lower, swap_halves(g[:, 3 * TILE :]), x[:, 3 * TILE :]).astype(jnp.bfloat16)
        first[b] = jnp.where(even, tail, head)
        second[b] = jnp.where(even, head, tail)
    copies[3].wait()


def inner_kernel(scale, near, own, gradient, shifted, grad, parts, middle, select_y, select_z, placed):
    rows, bricks, channels = grad.shape[0], own.shape[0] - 1, own.shape[1]
    set_selection(select_y, select_z)
    inner_parts(near, own, parts)
    lower = lane_of((channels, TILE)) < 64
    zero = jnp.zeros((channels, TILE), jnp.float32)
    for b in range(bricks):
        masked = gradient[b].astype(jnp.float32)
        tile = [zero] + [masked[:, q * TILE : (q + 1) * TILE] for q in range(TILES)] + [zero]
        for q in range(TILES):
            at = slice(q * TILE, (q + 1) * TILE)
            placed[b, :channels, at] = swap_halves(jnp.where(lower, tile[q + 2], tile[q + 1])).astype(jnp.bfloat16)
            placed[b, channels : 2 * channels, at] = swap_halves(jnp.where(lower, tile[q + 1], tile[q])).astype(
                jnp.bfloat16
            )
            placed[b, 2 * channels :, at] = tile[q + 1].astype(jnp.bfloat16)
    shift_all(parts, select_y, select_z, middle, shifted, TILES)
    total = None
    for b in range(bricks):
        term = lax.dot_general(
            shifted[b], placed[b], (((1,), (1,)), ((), ())), preferred_element_type=jnp.float32
        )
        total = term if total is None else total + term
    total = total * scale
    count, half = 9 * channels, 9 * channels // 2
    grad[:count, :] = total[:, : 2 * channels]
    grad[count : count + half, :channels] = total[:half, 2 * channels :]
    grad[count : count + half, channels:] = total[half:, 2 * channels :]
    if rows > count + half:
        grad[count + half :, :] = jnp.zeros((rows - count - half, 2 * channels), jnp.float32)


def outer_kernel(
    scale, near, first, second, from_first, from_second, inner, shifted, grad,
    low, high, parts, middle, select_y, select_z,
):
    bricks, channels = first.shape[0], first.shape[1]
    set_selection(select_y, select_z)
    outer_parts(near, 0, first, second, from_first, from_second, low, high, parts)
    shift_all(parts, select_y, select_z, middle, shifted, 1)
    even = on_even()
    lower = lane_of((channels, TILE)) < 64
    total = None
    for b in range(bricks):
        head = jnp.where(even, second[b], first[b])
        tail = jnp.where(even, first[b], second[b])
        ends = jnp.concatenate([jnp.where(lower, 0, head), jnp.where(lower, tail, 0)], axis=0)
        term = lax.dot_general(shifted[b], ends, (((1,), (1,)), ((), ())), preferred_element_type=jnp.float32)
        total = term if total is None else total + term
    count = 9 * channels
    grad[:count, :] = inner[:count, :] + total * scale
    grad[count:, :] = inner[count:, :]


def tables_kernel(weight, table_y, table_g):
    channels = weight.shape[1]
    for tx in range(3):
        for yz in range(9):
            at = (slice(tx * channels, (tx + 1) * channels), slice(yz * channels, (yz + 1) * channels))
            table_y[at] = weight[9 * tx + yz].astype(jnp.float32).T.astype(jnp.bfloat16)
            table_g[at] = weight[26 - 9 * tx - yz]


def convolve(table, inner, outer, present, out):
    bricks, channels = out.shape[1], out.shape[2]
    lower = lane_of((channels, TILE)) < 64
    for b in range(bricks):
        main = jnp.dot(table[...], inner[b], preferred_element_type=jnp.float32)
        ends = jnp.dot(table[...], outer[b], preferred_element_type=jnp.float32)

        def term(t, q):
            rows = slice(t * channels, (t + 1) * channels)
            return main[rows, q * TILE : (q + 1) * TILE] if 0 <= q < TILES else ends[rows]

        for q in range(TILES):
            sides = jnp.where(lower, term(0, q), term(0, q - 1)) + jnp.where(lower, term(2, q + 1), term(2, q))
            at = slice(q * TILE, (q + 1) * TILE)
            out[0, b, :, at] = ((term(1, q) + swap_halves(sides)) * present[b : b + 1, at]).astype(jnp.bfloat16)


def backward_kernel(
    near, own, present, first, second, from_first, from_second, table, out,
    parts, middle, low, high, end_parts, end_middle, select_y, select_z, inner, outer,
):
    set_selection(select_y, select_z)
    inner_parts(near, own, parts)
    outer_parts(near, 1, first, second, from_first, from_second, low, high, end_parts)
    shift_all(parts, select_y, select_z, middle, inner, TILES)
    shift_all(end_parts, select_y, select_z, end_middle, outer, 1)
    convolve(table, inner, outer, present, out)


def unpack_kernel(groups, mine, theirs, out, whole):
    place = lax.axis_index("space") * lax.axis_size("scene") + lax.axis_index("scene")
    odd = place % 2
    where = place // 2 % groups
    size = mine.shape[0] // groups
    for k in range(groups):
        chunk = jnp.bitwise_xor(where, k)
        at = pl.multiple_of((odd * groups + chunk) * size, 8)
        whole[pl.ds(at, size), :] = mine[k * size : (k + 1) * size, :]
        at = pl.multiple_of(((1 - odd) * groups + chunk) * size, 8)
        whole[pl.ds(at, size), :] = theirs[k * size : (k + 1) * size, :]
    channels = out.shape[1]
    count, half = 9 * channels, 9 * channels // 2
    for yz in range(9):
        both = whole[yz * channels : (yz + 1) * channels, :]
        out[yz] = both[:, :channels]
        out[18 + yz] = both[:, channels:]
    for row in range(0, half, 32):
        both = whole[count + row : count + row + 32, :]
        for side in range(2):
            at = row + side * half
            out[9 + at // channels, at % channels : at % channels + 32, :] = both[
                :, side * channels : (side + 1) * channels
            ]


def exchange(x, bit):
    count = lax.axis_size("space") * lax.axis_size("scene")
    return lax.ppermute(x, AXES, [(i, i ^ bit) for i in range(count)])


def all_sum(part, groups):
    count = lax.axis_size("space") * lax.axis_size("scene")
    place = lax.axis_index("space") * lax.axis_size("scene") + lax.axis_index("scene")
    odd, where = place % 2, place // 2 % groups
    half = part.shape[0] // 2
    size = half // groups
    keep = lax.dynamic_slice_in_dim(part, odd * half, half, 0)
    send = lax.dynamic_slice_in_dim(part, (1 - odd) * half, half, 0)
    mine = keep + exchange(send, 1)
    own = lax.dynamic_slice_in_dim(mine, where * size, size, 0)
    got = []
    for k in range(1, groups):
        got.append(exchange(lax.dynamic_slice_in_dim(mine, (where ^ k) * size, size, 0), 2 * k))
    for one in got:
        own = own + one
    bit = 2 * groups
    while bit < count:
        wide = 4 if 4 * bit <= count else 2
        got = []
        for k in range(1, wide):
            got.append(exchange(own, bit * k))
        own = own + got[0]
        if wide == 4:
            own = own + (got[1] + got[2])
        bit *= wide
    chunks = [own]
    for k in range(1, groups):
        chunks.append(exchange(own, 2 * k))
    mine = jnp.concatenate(chunks)
    return mine, exchange(mine, 1)


def program(features, cotangent, weight, neighbours, occupancy):
    bricks, channels = features.shape[1], features.shape[2]
    spaces, scenes = lax.axis_size("space"), lax.axis_size("scene")
    scale = 1.0 / math.sqrt(scenes * bricks * spaces * 512)
    groups = 4
    unit = 16 * groups
    rows = -(-(27 * channels // 2) // unit) * unit

    def call(kernel, shapes, inputs, specs, scratch, limit=32 << 20):
        single = not isinstance(shapes, list)
        return pl.pallas_call(
            kernel,
            out_shape=shapes,
            in_specs=specs,
            out_specs=VMEM if single else [VMEM] * len(shapes),
            scratch_shapes=scratch,
            compiler_params=pltpu.CompilerParams(vmem_limit_bytes=limit),
            cost_estimate=pl.CostEstimate(flops=10**8, bytes_accessed=10**6, transcendentals=0),
        )(*inputs)

    def shape(*dims, dtype=jnp.bfloat16):
        return jax.ShapeDtypeStruct(dims, dtype)

    def scratch(*dims, dtype=jnp.bfloat16):
        return pltpu.VMEM(dims, dtype)

    many = bricks * TILES * channels
    parts = [scratch(2 * many, 2 * TILE), scratch(3 * many, 2 * TILE)]
    few = bricks * channels
    ends = [
        scratch(2 * bricks + 1, channels, TILE),
        scratch(2 * bricks + 1, channels, TILE),
        scratch(2 * few, 2 * TILE),
        scratch(3 * few, 2 * TILE),
    ]
    select = [scratch(2 * TILE, 3 * TILE)] * 2
    face, brick = shape(bricks, channels, TILE), shape(bricks + 1, channels, 512)
    first, second, own_x, own_g, present, near = call(
        faces_kernel,
        [face, face, brick, brick, shape(bricks, 512, dtype=jnp.float32), shape(*neighbours.shape, dtype=jnp.int32)],
        (features, cotangent, occupancy, neighbours),
        [HBM] * 4,
        [
            scratch(*occupancy.shape, dtype=jnp.int32),
            scratch(*features.shape),
            scratch(*features.shape),
            pltpu.SemaphoreType.DMA((4,)),
        ],
        limit=None,
    )
    pairs = [[(i, i + 1), (i + 1, i)] for i in range(spaces - 1)]
    from_first = lax.ppermute(first, "space", sum(pairs[0::2], []))
    from_second = lax.ppermute(second, "space", sum(pairs[1::2], []))
    halo = (first, second, from_first, from_second)
    inner, grad = call(
        functools.partial(inner_kernel, scale),
        [shape(bricks, 9 * channels, 512), shape(rows, 2 * channels, dtype=jnp.float32)],
        (near, own_x, own_g),
        [SMEM, VMEM, VMEM],
        [*parts, *select, scratch(bricks, 3 * channels, 512)],
    )
    outer, grad = call(
        functools.partial(outer_kernel, scale),
        [shape(bricks, 9 * channels, TILE), shape(rows, 2 * channels, dtype=jnp.float32)],
        (near, *halo, grad),
        [SMEM] + [VMEM] * 5,
        [*ends, *select],
    )
    table = shape(3 * channels, 9 * channels)
    table_y, table_g = call(tables_kernel, [table, table], (weight,), [VMEM], [])
    out_y = call(convolve, shape(*features.shape), (table_y, inner, outer, present), [VMEM] * 4, [])
    out_g = call(
        backward_kernel,
        shape(*cotangent.shape),
        (near, own_g, present, *halo, table_g),
        [SMEM] + [VMEM] * 7,
        [*parts, *ends, *select, scratch(bricks, 9 * channels, 512), scratch(bricks, 9 * channels, TILE)],
    )
    mine, theirs = all_sum(grad, groups)
    out_w = call(
        functools.partial(unpack_kernel, groups),
        shape(27, channels, channels, dtype=jnp.float32),
        (mine, theirs),
        [VMEM] * 2,
        [pltpu.VMEM((rows, 2 * channels), jnp.float32)],
    )
    return out_y, out_g, out_w


def solution(mesh):
    in_specs = (
        P("scene", "space", None, None),
        P("scene", "space", None, None),
        P(),
        P("scene", "space", None),
        P("scene", "space", None),
    )
    out_specs = (P("scene", "space", None, None), P("scene", "space", None, None), P())
    return jax.shard_map(program, mesh=mesh, in_specs=in_specs, out_specs=out_specs, check_vma=False)
```

time: 340 us -> 47.1 us (0.14)
  local copies, waits for them, and re-layouts: 158 us -> 4.07 us
  waiting for transfers between devices: 106 us -> 13.1 us
  other arithmetic: 42.7 us -> 0.08 us
  between operations: 16.4 us -> 0.89 us
  Pallas kernels: 0 us -> 11 us
  starting transfers between devices: 6.93 us -> 17.7 us
  matrix products: 7.51 us -> 0 us
    psum x2 -> x0, waiting for transfers between devices: 106 us -> none  [the longest x1 76.5 us: local(): summed = lax.psum(by_scene, 'space')]
    reshape x54 -> x0, local copies, waits for them, and re-layouts: 67.4 us -> none  [window(): return volume[:, :, start_x:start_x + 8, start_y:start_y + 8, start_z:sta...]
    gather x54 -> x0, local copies, waits for them, and re-layouts: 39.8 us -> none  [assemble(): jnp.take(section, places[:, 9 * off_x + 3 * off_y + off_z], axis=0)]
    unnamed x383 -> x22, local copies, waits for them, and re-layouts: 26.9 us -> 4.02 us
    gather x23 -> x0, other arithmetic: 13.7 us -> none
    slice x17 -> x0, local copies, waits for them, and re-layouts: 13.2 us -> none  [the longest x8 8.44 us: window(): volume[:, :, start_x:start_x + 8, start_y:start_y + 8, start_z:start_z + 8]]
    ppermute x2 -> x13, waiting for transfers between devices: 0.01 us -> 13.1 us  [the longest x11 13.1 us: exchange(): return lax.ppermute(x, AXES, [(i, i ^ bit) for i in range(count)])]
    select_n x55 -> x0, other arithmetic: 11.8 us -> none  [the longest x54 11.8 us: assemble(): jnp.take(section, places[:, 9 * off_x + 3 * off_y + off_z], axis=0)]
  transfers between devices with their start and end apart: 4 -> 13, of which waited for: 2 -> 8; matrix products, arithmetic and copies ran while one was open for 10% -> 0% of each run, Pallas kernels for 0% -> 14%
where the time goes in v1:
time: 47.1 us; the launch traced here: 46.8 us
  starting transfers between devices  17.7 us (38%)
  waiting for transfers between devices  13.1 us (28%)
  Pallas kernels  11 us (23%)
  local copies, waits for them, and re-layouts  4.07 us (9%)
  between operations  0.89 us (2%)
    ppermute x11, starting transfers between devices, exchange(): return lax.ppermute(x, AXES, [(i, i ^ bit) for i in range(count)])  14 us
    ppermute x11, waiting for transfers between devices, exchange(): return lax.ppermute(x, AXES, [(i, i ^ bit) for i in range(count)])  13.1 us
    pallas_call x7, Pallas kernels, call(): pl.pallas_call(kernel, out_shape=shapes, in_specs=specs, out_specs=VMEM i...  11 us
    unnamed x22, local copies, waits for them, and re-layouts  4.02 us
    ppermute x1, starting transfers between devices, program(): from_first = lax.ppermute(first, 'space', sum(pairs[0::2], []))  3.06 us
  transfers between devices with their start and end apart: 13, of which 8 were waited for; matrix products, arithmetic and copies ran while one was open for 0% of the time, Pallas kernels for 14%

profile of v1, /device:TPU:0, one launch (start us, length us, event | category | flops | bytes accessed | tf_op | source)
XLA Modules:
  0.0 46.8 jit_solution(16982623262617100956)
XLA Ops:
  0.6 1.9 %shard_map.77 = (bf16[2,64,128]{2,1,0:T(8,128)(2,1)}, bf16[2,64,128]{2,1,0:T(8,128)(2,1)}, bf16[3,64,512]{2,1,0:T(8,128)(2,1)}, bf16[3,64,512]{2,1,0:T(8,128)(2,...) custom-call(bf16[1,2,64,512]{3,2,1,0:T(8,128)(2,1)} %features.1, bf16[1,2,64,512]{3,2,1,0:T(8,128)(2,1)} %cotangent.1, ...), custom_call_target="tpu_custom_call" | custom-call | flops 100000000 | bytes 1000000 | tf_op jit(solution)/shard_map/pallas_call | solution.py:317
  2.5 3.1 %collective-permute-start = (bf16[2,64,128]{2,1,0:T(8,128)(2,1)}, bf16[2,64,128]{2,1,0:T(8,128)(2,1)S(1)}, u32[]{:S(2)}, u32[]{:S(2)}) collective-permute-start(bf16[2,64,128]{2,1,0:T(8,128)(2,1)} %get-tuple-element.20.first), channel_id=1, source_target_pairs={{0,4},{4,0},{8,12},{12,8},{16,20},{20,16},{24,28},{28,24},{1,5},{5... | collective-permute-start | bytes 98312 | tf_op jit(solution)/shard_map/ppermute | solution.py:358
  6.3 0.9 %copy-done = bf16[3,64,512]{2,1,0:T(8,128)(2,1)S(1)} copy-done((bf16[3,64,512]{2,1,0:T(8,128)(2,1)S(1)}, bf16[3,64,512]{2,1,0:T(8,128)(2,1)}, u32[]{:S(2)}) %copy-start) | copy-done | bytes 196632
  7.2 0.9 %copy-done.3 = bf16[3,64,512]{2,1,0:T(8,128)(2,1)S(1)} copy-done((bf16[3,64,512]{2,1,0:T(8,128)(2,1)S(1)}, bf16[3,64,512]{2,1,0:T(8,128)(2,1)}, u32[]{:S(2)}) %copy-start.3) | copy-done | bytes 196632
  8.8 1.9 %shard_map.78 = (bf16[2,576,512]{2,1,0:T(8,128)(2,1)S(1)}, f32[896,128]{1,0:T(8,128)S(1)}) custom-call(s32[1,2,27]{2,1,0:T(2,128)S(1)} %copy-done.9, bf16[3,64,512]{2,1,0:T(8,128)(2,1)S(1)} %copy-done.3, bf16[3,64,512]{2,1,0:T(8,128)(2,1)S(1)} %copy-done), custom_call_target="tpu_custom_call" | custom-call | flops 100000000 | bytes 1000000 | tf_op jit(solution)/shard_map/pallas_call | solution.py:317
  11.4 0.8 %copy-done.6 = bf16[2,64,128]{2,1,0:T(8,128)(2,1)S(1)} copy-done((bf16[2,64,128]{2,1,0:T(8,128)(2,1)S(1)}, bf16[2,64,128]{2,1,0:T(8,128)(2,1)}, u32[]{:S(2)}) %copy-start.6) | copy-done | bytes 32792
  12.2 1.3 %shard_map.79 = (bf16[2,576,128]{2,1,0:T(8,128)(2,1)S(1)}, f32[896,128]{1,0:T(8,128)S(1)}) custom-call(s32[1,2,27]{2,1,0:T(2,128)S(1)} %copy-done.9, bf16[2,64,128]{2,1,0:T(8,128)(2,1)S(1)} %copy-done.4, bf16[2,64,128]{2,1,0:T(8,128)(2,1)S(1)} %copy-done.6, bf16[2,64,128]{2,1,0:T(8,128)(2,1)S(1)} %collective-permute-done.from_first, ...), custom_call_target="tpu_custom_call" | custom-call | flops 100000000 | bytes 1000000 | tf_op jit(solution)/shard_map/pallas_call | solution.py:317
  13.6 1.4 %collective-permute-done.2 = f32[448,128]{1,0:T(8,128)S(1)} collective-permute-done((f32[448,128]{1,0:T(8,128)S(1)}, f32[448,128]{1,0:T(8,128)S(1)}, u32[]{:S(2)}, u32[]{:S(2)}) %collective-permute-start.2) | collective-permute-done | bytes 229408 | tf_op jit(solution)/shard_map/ppermute | solution.py:272
  15.1 1.6 %collective-permute-start.3 = (f32[112,128]{1,0:T(8,128)S(1)}, f32[112,128]{1,0:T(8,128)S(1)}, u32[]{:S(2)}, u32[]{:S(2)}) collective-permute-start(f32[112,128]{1,0:T(8,128)S(1)} %get-tuple-element.27), channel_id=1, source_target_pairs={{0,2},{1,3},{2,0},{3,1},{4,6},{5,7},{6,4},{7,5},{8,10},{9,11},{10,... | collective-permute-start | bytes 172040 | tf_op jit(solution)/shard_map/ppermute | solution.py:272
  16.7 4.3 %collective-permute-start.5 = (f32[112,128]{1,0:T(8,128)S(1)}, f32[112,128]{1,0:T(8,128)S(1)}, u32[]{:S(2)}, u32[]{:S(2)}) collective-permute-start(f32[112,128]{1,0:T(8,128)S(1)} %get-tuple-element.28), channel_id=1, source_target_pairs={{0,6},{1,7},{2,4},{3,5},{4,2},{5,3},{6,0},{7,1},{8,14},{9,15},{10,... | collective-permute-start | bytes 172040 | tf_op jit(solution)/shard_map/ppermute | solution.py:272
  21.0 3.2 %collective-permute-done.5 = f32[112,128]{1,0:T(8,128)S(1)} collective-permute-done((f32[112,128]{1,0:T(8,128)S(1)}, f32[112,128]{1,0:T(8,128)S(1)}, u32[]{:S(2)}, u32[]{:S(2)}) %collective-permute-start.5) | collective-permute-done | bytes 57376 | tf_op jit(solution)/shard_map/ppermute | solution.py:272
  24.2 0.9 %collective-permute-done.4 = f32[112,128]{1,0:T(8,128)S(1)} collective-permute-done((f32[112,128]{1,0:T(8,128)S(1)}, f32[112,128]{1,0:T(8,128)S(1)}, u32[]{:S(2)}, u32[]{:S(2)}) %collective-permute-start.4) | collective-permute-done | bytes 57376 | tf_op jit(solution)/shard_map/ppermute | solution.py:272
  25.1 2.3 %collective-permute-start.8 = (f32[112,128]{1,0:T(8,128)S(1)}, f32[112,128]{1,0:T(8,128)S(1)}, u32[]{:S(2)}, u32[]{:S(2)}) collective-permute-start(f32[112,128]{1,0:T(8,128)S(1)} %add_add_fusion.1), channel_id=1, source_target_pairs={{0,24},{1,25},{2,26},{3,27},{4,28},{5,29},{6,30},{7,31},{8,16},{9,... | collective-permute-start | bytes 172040 | tf_op jit(solution)/shard_map/ppermute | solution.py:272
  27.4 0.8 %collective-permute-start.7 = (f32[112,128]{1,0:T(8,128)S(1)}, f32[112,128]{1,0:T(8,128)S(1)}, u32[]{:S(2)}, u32[]{:S(2)}) collective-permute-start(f32[112,128]{1,0:T(8,128)S(1)} %add_add_fusion.1), channel_id=1, source_target_pairs={{0,16},{1,17},{2,18},{3,19},{4,20},{5,21},{6,22},{7,23},{8,24},{9,... | collective-permute-start | bytes 172040 | tf_op jit(solution)/shard_map/ppermute | solution.py:272
  28.2 1.3 %collective-permute-start.6 = (f32[112,128]{1,0:T(8,128)S(1)}, f32[112,128]{1,0:T(8,128)S(1)}, u32[]{:S(2)}, u32[]{:S(2)}) collective-permute-start(f32[112,128]{1,0:T(8,128)S(1)} %add_add_fusion.1), channel_id=1, source_target_pairs={{0,8},{1,9},{2,10},{3,11},{4,12},{5,13},{6,14},{7,15},{8,0},{9,1},... | collective-permute-start | bytes 172040 | tf_op jit(solution)/shard_map/ppermute | solution.py:272
  29.6 2.2 %collective-permute-done.8 = f32[112,128]{1,0:T(8,128)S(1)} collective-permute-done((f32[112,128]{1,0:T(8,128)S(1)}, f32[112,128]{1,0:T(8,128)S(1)}, u32[]{:S(2)}, u32[]{:S(2)}) %collective-permute-start.8) | collective-permute-done | bytes 57376 | tf_op jit(solution)/shard_map/ppermute | solution.py:272
  31.8 1.3 %collective-permute-done.7 = f32[112,128]{1,0:T(8,128)S(1)} collective-permute-done((f32[112,128]{1,0:T(8,128)S(1)}, f32[112,128]{1,0:T(8,128)S(1)}, u32[]{:S(2)}, u32[]{:S(2)}) %collective-permute-start.7) | collective-permute-done | bytes 57376 | tf_op jit(solution)/shard_map/ppermute | solution.py:272
  33.1 2.1 %collective-permute-start.11 = (f32[112,128]{1,0:T(8,128)S(1)}, f32[112,128]{1,0:T(8,128)S(1)}, u32[]{:S(2)}, u32[]{:S(2)}) collective-permute-start(f32[112,128]{1,0:T(8,128)S(1)} %add_add_fusion), channel_id=1, source_target_pairs={{0,6},{1,7},{2,4},{3,5},{4,2},{5,3},{6,0},{7,1},{8,14},{9,15},{10,... | collective-permute-start | bytes 172040 | tf_op jit(solution)/shard_map/ppermute | solution.py:272
  35.2 1.3 %collective-permute-start.10 = (f32[112,128]{1,0:T(8,128)S(1)}, f32[112,128]{1,0:T(8,128)S(1)}, u32[]{:S(2)}, u32[]{:S(2)}) collective-permute-start(f32[112,128]{1,0:T(8,128)S(1)} %add_add_fusion), channel_id=1, source_target_pairs={{0,4},{1,5},{2,6},{3,7},{4,0},{5,1},{6,2},{7,3},{8,12},{9,13},{10,... | collective-permute-start | bytes 172040 | tf_op jit(solution)/shard_map/ppermute | solution.py:272
  36.7 2.0 %collective-permute-done.11 = f32[112,128]{1,0:T(8,128)S(1)} collective-permute-done((f32[112,128]{1,0:T(8,128)S(1)}, f32[112,128]{1,0:T(8,128)S(1)}, u32[]{:S(2)}, u32[]{:S(2)}) %collective-permute-start.11) | collective-permute-done | bytes 57376 | tf_op jit(solution)/shard_map/ppermute | solution.py:272
  39.4 1.3 %collective-permute-done.9 = f32[112,128]{1,0:T(8,128)S(1)} collective-permute-done((f32[112,128]{1,0:T(8,128)S(1)}, f32[112,128]{1,0:T(8,128)S(1)}, u32[]{:S(2)}, u32[]{:S(2)}) %collective-permute-start.9) | collective-permute-done | bytes 57376 | tf_op jit(solution)/shard_map/ppermute | solution.py:272
  41.3 1.3 %shard_map.80 = bf16[1,2,64,512]{3,2,1,0:T(8,128)(2,1)} custom-call(bf16[192,576]{1,0:T(8,128)(2,1)S(1)} %get-tuple-element.15.table, bf16[2,576,512]{2,1,0:T(8,128)(2,1)S(1)} %get-tuple-element.19.inner, bf16[2,576,128]{2,1,0:T(8,128)(2,1)S(1)} %get-tuple-element.23.outer, f32[2,512]{1,0:T(2,128)S(1)} %copy-done.8), custom_call_target="tpu_custom_call" | custom-call | flops 100000000 | bytes 1000000 | tf_op jit(solution)/shard_map/pallas_call | solution.py:317
  42.6 3.0 %shard_map.81 = bf16[1,2,64,512]{3,2,1,0:T(8,128)(2,1)} custom-call(s32[1,2,27]{2,1,0:T(2,128)S(1)} %copy-done.10, bf16[3,64,512]{2,1,0:T(8,128)(2,1)S(1)} %copy-done.1, f32[2,512]{1,0:T(2,128)S(1)} %copy-done.8, bf16[2,64,128]{2,1,0:T(8,128)(2,1)S(1)} %copy-done.5, bf16[2,64,128]{2,1,0:T(8,128)(2,1)S(1)} %copy-done.7, ...), custom_call_target="tpu_custom_call" | custom-call | flops 100000000 | bytes 1000000 | tf_op jit(solution)/shard_map/pallas_call | solution.py:317
  45.6 1.1 %shard_map.82 = f32[27,64,64]{2,1,0:T(8,128)} custom-call(f32[448,128]{1,0:T(8,128)S(1)} %pad_maximum_fusion.mine, f32[448,128]{1,0:T(8,128)S(1)} %collective-permute-done.12.theirs), custom_call_target="tpu_custom_call" | custom-call | flops 100000000 | bytes 1000000 | tf_op jit(solution)/shard_map/pallas_call | solution.py:317
  (37 shorter events, 3.7 us)
Async XLA Ops:
  2.5 8.1 %collective-permute-start = (bf16[2,64,128]{2,1,0:T(8,128)(2,1)}, bf16[2,64,128]{2,1,0:T(8,128)(2,1)S(1)}, u32[]{:S(2)}, u32[]{:S(2)}) collective-permute-start(bf16[2,64,128]{2,1,0:T(8,128)(2,1)} %get-tuple-element.20.first), channel_id=1, source_target_pairs={{0,4},{4,0},{8,12},{12,8},{16,20},{20,16},{24,28},{28,24},{1,5},{5... | collective-permute-start | bytes 98312 | tf_op jit(solution)/shard_map/ppermute | solution.py:358
  5.6 5.1 %collective-permute-start.1 = (bf16[2,64,128]{2,1,0:T(8,128)(2,1)}, bf16[2,64,128]{2,1,0:T(8,128)(2,1)S(1)}, u32[]{:S(2)}, u32[]{:S(2)}) collective-permute-start(bf16[2,64,128]{2,1,0:T(8,128)(2,1)} %get-tuple-element.21.second), channel_id=1, source_target_pairs={{4,8},{8,4},{12,16},{16,12},{20,24},{24,20},{5,9},{9,5},{13,17},{1... | collective-permute-start | bytes 98312 | tf_op jit(solution)/shard_map/ppermute | solution.py:359
  6.3 0.9 %copy-start = (bf16[3,64,512]{2,1,0:T(8,128)(2,1)S(1)}, bf16[3,64,512]{2,1,0:T(8,128)(2,1)}, u32[]{:S(2)}) copy-start(bf16[3,64,512]{2,1,0:T(8,128)(2,1)} %get-tuple-element.18.gradient.own) | copy-start | bytes 589828
  7.2 0.9 %copy-start.3 = (bf16[3,64,512]{2,1,0:T(8,128)(2,1)S(1)}, bf16[3,64,512]{2,1,0:T(8,128)(2,1)}, u32[]{:S(2)}) copy-start(bf16[3,64,512]{2,1,0:T(8,128)(2,1)} %get-tuple-element.17.own) | copy-start | bytes 589828
  8.1 0.6 %copy-start.9 = (s32[1,2,27]{2,1,0:T(2,128)S(1)}, s32[1,2,27]{2,1,0:T(2,128)}, u32[]{:S(2)}) copy-start(s32[1,2,27]{2,1,0:T(2,128)} %get-tuple-element.16.near) | copy-start | bytes 652
  10.7 0.8 %copy-start.4 = (bf16[2,64,128]{2,1,0:T(8,128)(2,1)S(1)}, bf16[2,64,128]{2,1,0:T(8,128)(2,1)}, u32[]{:S(2)}) copy-start(bf16[2,64,128]{2,1,0:T(8,128)(2,1)} %get-tuple-element.20.first) | copy-start | bytes 98308
  11.4 0.8 %copy-start.6 = (bf16[2,64,128]{2,1,0:T(8,128)(2,1)S(1)}, bf16[2,64,128]{2,1,0:T(8,128)(2,1)}, u32[]{:S(2)}) copy-start(bf16[2,64,128]{2,1,0:T(8,128)(2,1)} %get-tuple-element.21.second) | copy-start | bytes 98308
  13.5 27.3 %copy-start.2 = (bf16[27,64,64]{2,1,0:T(8,128)(2,1)S(1)}, bf16[27,64,64]{2,1,0:T(8,128)(2,1)}, u32[]{:S(2)}) copy-start(bf16[27,64,64]{2,1,0:T(8,128)(2,1)} %weight.1) | copy-start | bytes 663556
  13.5 1.6 %collective-permute-start.2 = (f32[448,128]{1,0:T(8,128)S(1)}, f32[448,128]{1,0:T(8,128)S(1)}, u32[]{:S(2)}, u32[]{:S(2)}) collective-permute-start(f32[448,128]{1,0:T(8,128)S(1)} %constant_dynamic-slice_fusion.3), channel_id=1, source_target_pairs={{0,1},{1,0},{2,3},{3,2},{4,5},{5,4},{6,7},{7,6},{8,9},{9,8},{10,11... | collective-permute-start | bytes 688136 | tf_op jit(solution)/shard_map/ppermute | solution.py:272
  13.6 27.6 %copy-start.8 = (f32[2,512]{1,0:T(2,128)S(1)}, f32[2,512]{1,0:T(2,128)}, u32[]{:S(2)}) copy-start(f32[2,512]{1,0:T(2,128)} %get-tuple-element.24.present) | copy-start | bytes 12292
  15.1 5.8 %collective-permute-start.3 = (f32[112,128]{1,0:T(8,128)S(1)}, f32[112,128]{1,0:T(8,128)S(1)}, u32[]{:S(2)}, u32[]{:S(2)}) collective-permute-start(f32[112,128]{1,0:T(8,128)S(1)} %get-tuple-element.27), channel_id=1, source_target_pairs={{0,2},{1,3},{2,0},{3,1},{4,6},{5,7},{6,4},{7,5},{8,10},{9,11},{10,... | collective-permute-start | bytes 172040 | tf_op jit(solution)/shard_map/ppermute | solution.py:272
  16.7 7.5 %collective-permute-start.5 = (f32[112,128]{1,0:T(8,128)S(1)}, f32[112,128]{1,0:T(8,128)S(1)}, u32[]{:S(2)}, u32[]{:S(2)}) collective-permute-start(f32[112,128]{1,0:T(8,128)S(1)} %get-tuple-element.28), channel_id=1, source_target_pairs={{0,6},{1,7},{2,4},{3,5},{4,2},{5,3},{6,0},{7,1},{8,14},{9,15},{10,... | collective-permute-start | bytes 172040 | tf_op jit(solution)/shard_map/ppermute | solution.py:272
  20.9 4.2 %collective-permute-start.4 = (f32[112,128]{1,0:T(8,128)S(1)}, f32[112,128]{1,0:T(8,128)S(1)}, u32[]{:S(2)}, u32[]{:S(2)}) collective-permute-start(f32[112,128]{1,0:T(8,128)S(1)} %get-tuple-element.29), channel_id=1, source_target_pairs={{0,4},{1,5},{2,6},{3,7},{4,0},{5,1},{6,2},{7,3},{8,12},{9,13},{10,... | collective-permute-start | bytes 172040 | tf_op jit(solution)/shard_map/ppermute | solution.py:272
  25.1 6.7 %collective-permute-start.8 = (f32[112,128]{1,0:T(8,128)S(1)}, f32[112,128]{1,0:T(8,128)S(1)}, u32[]{:S(2)}, u32[]{:S(2)}) collective-permute-start(f32[112,128]{1,0:T(8,128)S(1)} %add_add_fusion.1), channel_id=1, source_target_pairs={{0,24},{1,25},{2,26},{3,27},{4,28},{5,29},{6,30},{7,31},{8,16},{9,... | collective-permute-start | bytes 172040 | tf_op jit(solution)/shard_map/ppermute | solution.py:272
  27.4 5.7 %collective-permute-start.7 = (f32[112,128]{1,0:T(8,128)S(1)}, f32[112,128]{1,0:T(8,128)S(1)}, u32[]{:S(2)}, u32[]{:S(2)}) collective-permute-start(f32[112,128]{1,0:T(8,128)S(1)} %add_add_fusion.1), channel_id=1, source_target_pairs={{0,16},{1,17},{2,18},{3,19},{4,20},{5,21},{6,22},{7,23},{8,24},{9,... | collective-permute-start | bytes 172040 | tf_op jit(solution)/shard_map/ppermute | solution.py:272
  28.2 4.9 %collective-permute-start.6 = (f32[112,128]{1,0:T(8,128)S(1)}, f32[112,128]{1,0:T(8,128)S(1)}, u32[]{:S(2)}, u32[]{:S(2)}) collective-permute-start(f32[112,128]{1,0:T(8,128)S(1)} %add_add_fusion.1), channel_id=1, source_target_pairs={{0,8},{1,9},{2,10},{3,11},{4,12},{5,13},{6,14},{7,15},{8,0},{9,1},... | collective-permute-start | bytes 172040 | tf_op jit(solution)/shard_map/ppermute | solution.py:272
  33.1 5.5 %collective-permute-start.11 = (f32[112,128]{1,0:T(8,128)S(1)}, f32[112,128]{1,0:T(8,128)S(1)}, u32[]{:S(2)}, u32[]{:S(2)}) collective-permute-start(f32[112,128]{1,0:T(8,128)S(1)} %add_add_fusion), channel_id=1, source_target_pairs={{0,6},{1,7},{2,4},{3,5},{4,2},{5,3},{6,0},{7,1},{8,14},{9,15},{10,... | collective-permute-start | bytes 172040 | tf_op jit(solution)/shard_map/ppermute | solution.py:272
  35.2 4.2 %collective-permute-start.10 = (f32[112,128]{1,0:T(8,128)S(1)}, f32[112,128]{1,0:T(8,128)S(1)}, u32[]{:S(2)}, u32[]{:S(2)}) collective-permute-start(f32[112,128]{1,0:T(8,128)S(1)} %add_add_fusion), channel_id=1, source_target_pairs={{0,4},{1,5},{2,6},{3,7},{4,0},{5,1},{6,2},{7,3},{8,12},{9,13},{10,... | collective-permute-start | bytes 172040 | tf_op jit(solution)/shard_map/ppermute | solution.py:272
  36.5 4.2 %collective-permute-start.9 = (f32[112,128]{1,0:T(8,128)S(1)}, f32[112,128]{1,0:T(8,128)S(1)}, u32[]{:S(2)}, u32[]{:S(2)}) collective-permute-start(f32[112,128]{1,0:T(8,128)S(1)} %add_add_fusion), channel_id=1, source_target_pairs={{0,2},{1,3},{2,0},{3,1},{4,6},{5,7},{6,4},{7,5},{8,10},{9,11},{10,... | collective-permute-start | bytes 172040 | tf_op jit(solution)/shard_map/ppermute | solution.py:272
  40.7 1.9 %copy-start.1 = (bf16[3,64,512]{2,1,0:T(8,128)(2,1)S(1)}, bf16[3,64,512]{2,1,0:T(8,128)(2,1)}, u32[]{:S(2)}) copy-start(bf16[3,64,512]{2,1,0:T(8,128)(2,1)} %get-tuple-element.18.gradient.own) | copy-start | bytes 589828
  40.7 1.9 %copy-start.5 = (bf16[2,64,128]{2,1,0:T(8,128)(2,1)S(1)}, bf16[2,64,128]{2,1,0:T(8,128)(2,1)}, u32[]{:S(2)}) copy-start(bf16[2,64,128]{2,1,0:T(8,128)(2,1)} %get-tuple-element.20.first) | copy-start | bytes 98308
  40.7 1.9 %copy-start.7 = (bf16[2,64,128]{2,1,0:T(8,128)(2,1)S(1)}, bf16[2,64,128]{2,1,0:T(8,128)(2,1)}, u32[]{:S(2)}) copy-start(bf16[2,64,128]{2,1,0:T(8,128)(2,1)} %get-tuple-element.21.second) | copy-start | bytes 98308
  40.7 1.9 %copy-start.10 = (s32[1,2,27]{2,1,0:T(2,128)S(1)}, s32[1,2,27]{2,1,0:T(2,128)}, u32[]{:S(2)}) copy-start(s32[1,2,27]{2,1,0:T(2,128)} %get-tuple-element.16.near) | copy-start | bytes 652
  40.7 4.9 %collective-permute-start.12 = (f32[448,128]{1,0:T(8,128)S(1)}, f32[448,128]{1,0:T(8,128)S(1)}, u32[]{:S(2)}, u32[]{:S(2)}) collective-permute-start(f32[448,128]{1,0:T(8,128)S(1)} %pad_maximum_fusion.mine), channel_id=1, source_target_pairs={{0,1},{1,0},{2,3},{3,2},{4,5},{5,4},{6,7},{7,6},{8,9},{9,8},{10,11... | collective-permute-start | bytes 688136 | tf_op jit(solution)/shard_map/ppermute | solution.py:272

commit v2 on v1

--- a/solution.py
+++ b/solution.py
@@ -40,10 +40,6 @@
 
 def swap_halves(x):
     return pltpu.roll(x, 64, x.ndim - 1)
-
-
-def on_even():
-    return lax.axis_index("space") % 2 == 0
 
 
 def set_groups(parts, row, pick):
@@ -99,36 +95,24 @@
             )
 
 
-def outer_parts(near, side, first, second, from_first, from_second, low, high, parts):
-    bricks, channels = first.shape[0], first.shape[1]
-    even = on_even()
-    zero = jnp.zeros((channels, TILE), jnp.bfloat16)
-
-    def placed(x):
-        return swap_halves(x.astype(jnp.float32)).astype(jnp.bfloat16) if side else x
-
-    for b in range(bricks):
-        high[b] = placed(jnp.where(even, from_second[b], from_first[b]))
-        high[bricks + b] = placed(jnp.where(even, first[b], second[b]))
-        low[b] = placed(jnp.where(even, second[b], first[b]))
-        low[bricks + b] = placed(jnp.where(even, from_first[b], from_second[b]))
-    high[2 * bricks] = zero
-    low[2 * bricks] = zero
-    base = lax.axis_index("space") * bricks
-    lower = lane_of((channels, TILE)) < 64
-    for b in range(bricks):
-        up = {s: index_of(near, b, 1, *s, base, 2 * bricks) for s in SIDES}
-        down = {s: index_of(near, b, -1, *s, base - bricks, 2 * bricks) for s in SIDES}
-        set_groups(parts, b * channels, lambda c, e: jnp.where(lower, low[up[c, e]], high[down[c, e]]))
-
-
-def faces_kernel(features, cotangent, mask, near, first, second, own_x, own_g, present, near_out, *rest):
+def set_ends(near, a, mine, other, table, parts):
+    bricks, channels = mine.shape[0], mine.shape[1]
+    for b in range(bricks):
+        table[b] = (other if a < 0 else mine)[b]
+        table[bricks + b] = (mine if a < 0 else other)[b]
+    table[2 * bricks] = jnp.zeros((channels, TILE), jnp.bfloat16)
+    start = (lax.axis_index("space") + min(a, 0)) * bricks
+    for b in range(bricks):
+        at = {s: index_of(near, b, a, *s, start, 2 * bricks) for s in SIDES}
+        set_groups(parts, b * channels, lambda c, e: table[at[c, e]])
+
+
+def faces_kernel(features, cotangent, mask, near, head, tail, own_x, own_g, present, near_out, *rest):
     buffers, sems = rest[:3], rest[3]
     copies = [pltpu.make_async_copy(a, b, sems.at[n]) for n, (a, b) in enumerate(zip((mask, features, cotangent), buffers))]
     copies.append(pltpu.make_async_copy(near, near_out, sems.at[3]))
     for copy in copies:
         copy.start()
-    even = on_even()
     bricks, channels = own_x.shape[0] - 1, own_x.shape[1]
     lower = lane_of((channels, TILE)) < 64
     copies[0].wait()
@@ -142,10 +126,8 @@
         own[bricks] = jnp.zeros((channels, 512), jnp.bfloat16)
     for b in range(bricks):
         x, g = own_x[b].astype(jnp.float32), own_g[b].astype(jnp.float32)
-        head = jnp.where(lower, x[:, :TILE], swap_halves(g[:, :TILE])).astype(jnp.bfloat16)
-        tail = jnp.where(lower, swap_halves(g[:, 3 * TILE :]), x[:, 3 * TILE :]).astype(jnp.bfloat16)
-        first[b] = jnp.where(even, tail, head)
-        second[b] = jnp.where(even, head, tail)
+        head[b] = jnp.where(lower, x[:, :TILE], swap_halves(g[:, :TILE])).astype(jnp.bfloat16)
+        tail[b] = jnp.where(lower, swap_halves(g[:, 3 * TILE :]), x[:, 3 * TILE :]).astype(jnp.bfloat16)
     copies[3].wait()
 
 
@@ -182,25 +164,31 @@
 
 
 def outer_kernel(
-    scale, near, first, second, from_first, from_second, inner, shifted, grad,
-    low, high, parts, middle, select_y, select_z,
+    scale, near, head, tail, below, inner, shifted, grad, table, parts, middle, select_y, select_z
 ):
-    bricks, channels = first.shape[0], first.shape[1]
+    bricks, channels = head.shape[0], head.shape[1]
     set_selection(select_y, select_z)
-    outer_parts(near, 0, first, second, from_first, from_second, low, high, parts)
+    set_ends(near, -1, tail, below, table, parts)
     shift_all(parts, select_y, select_z, middle, shifted, 1)
-    even = on_even()
     lower = lane_of((channels, TILE)) < 64
-    total = None
-    for b in range(bricks):
-        head = jnp.where(even, second[b], first[b])
-        tail = jnp.where(even, first[b], second[b])
-        ends = jnp.concatenate([jnp.where(lower, 0, head), jnp.where(lower, tail, 0)], axis=0)
-        term = lax.dot_general(shifted[b], ends, (((1,), (1,)), ((), ())), preferred_element_type=jnp.float32)
-        total = term if total is None else total + term
-    count = 9 * channels
-    grad[:count, :] = inner[:count, :] + total * scale
-    grad[count:, :] = inner[count:, :]
+    contract = (((1,), (1,)), ((), ()))
+    first = last = None
+    for b in range(bricks):
+        g, x = jnp.where(lower, 0, head[b]), jnp.where(lower, head[b], 0)
+        one = lax.dot_general(shifted[b], g, contract, preferred_element_type=jnp.float32)
+        two = lax.dot_general(x, shifted[b], contract, preferred_element_type=jnp.float32)
+        first, last = (one, two) if b == 0 else (first + one, last + two)
+    for yz in range(9):
+        at = slice(yz * channels, (yz + 1) * channels)
+        back = slice((8 - yz) * channels, (9 - yz) * channels)
+        grad[at, :] = inner[at, :] + jnp.concatenate([first[at], last[:, back]], axis=1) * scale
+    grad[9 * channels :, :] = inner[9 * channels :, :]
+
+
+def shift_kernel(near, own, shifted, parts, middle, select_y, select_z):
+    set_selection(select_y, select_z)
+    inner_parts(near, own, parts)
+    shift_all(parts, select_y, select_z, middle, shifted, TILES)
 
 
 def tables_kernel(weight, table_y, table_g):
@@ -212,16 +200,18 @@
             table_g[at] = weight[26 - 9 * tx - yz]
 
 
-def convolve(table, inner, outer, present, out):
+def convolve(table, inner, ends, present, out, swapped):
     bricks, channels = out.shape[1], out.shape[2]
     lower = lane_of((channels, TILE)) < 64
     for b in range(bricks):
         main = jnp.dot(table[...], inner[b], preferred_element_type=jnp.float32)
-        ends = jnp.dot(table[...], outer[b], preferred_element_type=jnp.float32)
+        side = jnp.dot(table[...], ends(b), preferred_element_type=jnp.float32)
+        if swapped:
+            side = swap_halves(side)
 
         def term(t, q):
             rows = slice(t * channels, (t + 1) * channels)
-            return main[rows, q * TILE : (q + 1) * TILE] if 0 <= q < TILES else ends[rows]
+            return main[rows, q * TILE : (q + 1) * TILE] if 0 <= q < TILES else side[rows]
 
         for q in range(TILES):
             sides = jnp.where(lower, term(0, q), term(0, q - 1)) + jnp.where(lower, term(2, q + 1), term(2, q))
@@ -229,16 +219,19 @@
             out[0, b, :, at] = ((term(1, q) + swap_halves(sides)) * present[b : b + 1, at]).astype(jnp.bfloat16)
 
 
-def backward_kernel(
-    near, own, present, first, second, from_first, from_second, table, out,
-    parts, middle, low, high, end_parts, end_middle, select_y, select_z, inner, outer,
+def forward_kernel(
+    near, head, above, table, inner, tails, present, out, heads, ends, parts, middle, select_y, select_z
 ):
     set_selection(select_y, select_z)
-    inner_parts(near, own, parts)
-    outer_parts(near, 1, first, second, from_first, from_second, low, high, end_parts)
-    shift_all(parts, select_y, select_z, middle, inner, TILES)
-    shift_all(end_parts, select_y, select_z, end_middle, outer, 1)
-    convolve(table, inner, outer, present, out)
+    set_ends(near, 1, head, above, ends, parts)
+    shift_all(parts, select_y, select_z, middle, heads, 1)
+    lower = lane_of(heads.shape[1:]) < 64
+    convolve(table, inner, lambda b: jnp.where(lower, heads[b], tails[b]), present, out, False)
+
+
+def backward_kernel(table, inner, heads, tails, present, out):
+    lower = lane_of(heads.shape[1:]) < 64
+    convolve(table, inner, lambda b: jnp.where(lower, tails[b], heads[b]), present, out, True)
 
 
 def unpack_kernel(groups, mine, theirs, out, whole):
@@ -333,18 +326,15 @@
     many = bricks * TILES * channels
     parts = [scratch(2 * many, 2 * TILE), scratch(3 * many, 2 * TILE)]
     few = bricks * channels
-    ends = [
-        scratch(2 * bricks + 1, channels, TILE),
-        scratch(2 * bricks + 1, channels, TILE),
-        scratch(2 * few, 2 * TILE),
-        scratch(3 * few, 2 * TILE),
-    ]
+    ends = [scratch(2 * bricks + 1, channels, TILE), scratch(2 * few, 2 * TILE), scratch(3 * few, 2 * TILE)]
     select = [scratch(2 * TILE, 3 * TILE)] * 2
     face, brick = shape(bricks, channels, TILE), shape(bricks + 1, channels, 512)
-    first, second, own_x, own_g, present, near = call(
+    head, tail, own_x, own_g, present, near = call(
         faces_kernel,
         [face, face, brick, brick, shape(bricks, 512, dtype=jnp.float32), shape(*neighbours.shape, dtype=jnp.int32)],
-        (features, cotangent, occupancy, neighbours),
+        tuple(
+            pltpu.with_memory_space_constraint(a, pltpu.HBM) for a in (features, cotangent, occupancy, neighbours)
+        ),
         [HBM] * 4,
         [
             scratch(*occupancy.shape, dtype=jnp.int32),
@@ -352,36 +342,37 @@
             scratch(*features.shape),
             pltpu.SemaphoreType.DMA((4,)),
         ],
-        limit=None,
-    )
-    pairs = [[(i, i + 1), (i + 1, i)] for i in range(spaces - 1)]
-    from_first = lax.ppermute(first, "space", sum(pairs[0::2], []))
-    from_second = lax.ppermute(second, "space", sum(pairs[1::2], []))
-    halo = (first, second, from_first, from_second)
-    inner, grad = call(
+        limit=16 << 20,
+    )
+    below = lax.ppermute(tail, "space", [(i, i + 1) for i in range(spaces - 1)])
+    above = lax.ppermute(head, "space", [(i + 1, i) for i in range(spaces - 1)])
+    volume, grads = shape(bricks, 9 * channels, 512), shape(rows, 2 * channels, dtype=jnp.float32)
+    shifted = shape(bricks, 9 * channels, TILE)
+    inner_x, grad = call(
         functools.partial(inner_kernel, scale),
-        [shape(bricks, 9 * channels, 512), shape(rows, 2 * channels, dtype=jnp.float32)],
+        [volume, grads],
         (near, own_x, own_g),
         [SMEM, VMEM, VMEM],
         [*parts, *select, scratch(bricks, 3 * channels, 512)],
     )
-    outer, grad = call(
+    tails, grad = call(
         functools.partial(outer_kernel, scale),
-        [shape(bricks, 9 * channels, TILE), shape(rows, 2 * channels, dtype=jnp.float32)],
-        (near, *halo, grad),
-        [SMEM] + [VMEM] * 5,
+        [shifted, grads],
+        (near, head, tail, below, grad),
+        [SMEM] + [VMEM] * 4,
         [*ends, *select],
     )
     table = shape(3 * channels, 9 * channels)
     table_y, table_g = call(tables_kernel, [table, table], (weight,), [VMEM], [])
-    out_y = call(convolve, shape(*features.shape), (table_y, inner, outer, present), [VMEM] * 4, [])
-    out_g = call(
-        backward_kernel,
-        shape(*cotangent.shape),
-        (near, own_g, present, *halo, table_g),
-        [SMEM] + [VMEM] * 7,
-        [*parts, *ends, *select, scratch(bricks, 9 * channels, 512), scratch(bricks, 9 * channels, TILE)],
-    )
+    inner_g = call(shift_kernel, volume, (near, own_g), [SMEM, VMEM], [*parts, *select])
+    out_y, heads = call(
+        forward_kernel,
+        [shape(*features.shape), shifted],
+        (near, head, above, table_y, inner_x, tails, present),
+        [SMEM] + [VMEM] * 6,
+        [*ends, *select],
+    )
+    out_g = call(backward_kernel, shape(*cotangent.shape), (table_g, inner_g, heads, tails, present), [VMEM] * 5, [])
     mine, theirs = all_sum(grad, groups)
     out_w = call(
         functools.partial(unpack_kernel, groups),

time: 47.1 us -> 46.1 us (0.979)
  local copies, waits for them, and re-layouts: 4.07 us -> 0.05 us
  waiting for transfers between devices: 13.1 us -> 14.8 us
  starting transfers between devices: 17.7 us -> 19.1 us
    unnamed x22 -> x2, local copies, waits for them, and re-layouts: 4.02 us -> 0.01 us
    ppermute x2, waiting for transfers between devices: 0.01 us -> 2.54 us  [the longest x1 2.54 us: program(): above = lax.ppermute(head, 'space', [(i + 1, i) for i in range(spaces - 1)])]
    ppermute x2, starting transfers between devices: 3.71 us -> 6.19 us  [the longest x1 4.9 us: program(): below = lax.ppermute(tail, 'space', [(i, i + 1) for i in range(spaces - 1)])]
    ppermute x11, starting transfers between devices: 14 us -> 12.9 us  [exchange(): return lax.ppermute(x, AXES, [(i, i ^ bit) for i in range(count)])]
    ppermute x11, waiting for transfers between devices: 13.1 us -> 12.2 us  [exchange(): return lax.ppermute(x, AXES, [(i, i ^ bit) for i in range(count)])]
    pallas_call x7 -> x8, Pallas kernels: 11 us -> 11.1 us  [call(): pl.pallas_call(kernel, out_shape=shapes, in_specs=specs, out_specs=VMEM i...]
  transfers between devices with their start and end apart: 13 -> 13, of which waited for: 8 -> 10; matrix products, arithmetic and copies ran while one was open for 0% -> 0% of each run, Pallas kernels for 14% -> 16%
where the time goes in v2:
time: 46.1 us; the launch traced here: 45.9 us
  starting transfers between devices  19.1 us (41%)
  waiting for transfers between devices  14.8 us (32%)
  Pallas kernels  11.1 us (24%)
  between operations  0.82 us (2%)
    ppermute x11, starting transfers between devices, exchange(): return lax.ppermute(x, AXES, [(i, i ^ bit) for i in range(count)])  12.9 us
    ppermute x11, waiting for transfers between devices, exchange(): return lax.ppermute(x, AXES, [(i, i ^ bit) for i in range(count)])  12.2 us
    pallas_call x8, Pallas kernels, call(): pl.pallas_call(kernel, out_shape=shapes, in_specs=specs, out_specs=VMEM i...  11.1 us
    ppermute x1, starting transfers between devices, program(): below = lax.ppermute(tail, 'space', [(i, i + 1) for i in range(spaces - 1)])  4.9 us
    ppermute x1, waiting for transfers between devices, program(): above = lax.ppermute(head, 'space', [(i + 1, i) for i in range(spaces - 1)])  2.54 us
    ppermute x1, starting transfers between devices, program(): above = lax.ppermute(head, 'space', [(i + 1, i) for i in range(spaces - 1)])  1.29 us
  transfers between devices with their start and end apart: 13, of which 10 were waited for; matrix products, arithmetic and copies ran while one was open for 0% of the time, Pallas kernels for 16%

profile of v2, /device:TPU:0, one launch (start us, length us, event | category | flops | bytes accessed | tf_op | source)
XLA Modules:
  0.0 45.9 jit_solution(17909261204977125471)
XLA Ops:
  0.6 1.1 %shard_map.76 = (bf16[2,64,128]{2,1,0:T(8,128)(2,1)S(1)}, bf16[2,64,128]{2,1,0:T(8,128)(2,1)S(1)}, bf16[3,64,512]{2,1,0:T(8,128)(2,1)S(1)}, bf16[3,64,512]{2,1,0...) custom-call(bf16[1,2,64,512]{3,2,1,0:T(8,128)(2,1)} %features.1, bf16[1,2,64,512]{3,2,1,0:T(8,128)(2,1)} %cotangent.1, ...), custom_call_target="tpu_custom_call" | custom-call | flops 100000000 | bytes 1000000 | tf_op jit(solution)/shard_map/pallas_call | solution.py:310
  1.8 4.9 %collective-permute-start.1 = (bf16[2,64,128]{2,1,0:T(8,128)(2,1)S(1)}, bf16[2,64,128]{2,1,0:T(8,128)(2,1)S(1)}, u32[]{:S(2)}, u32[]{:S(2)}) collective-permute-start(bf16[2,64,128]{2,1,0:T(8,128)(2,1)S(1)} %get-tuple-element.23.tail), channel_id=1, source_target_pairs={{0,4},{4,8},{8,12},{12,16},{16,20},{20,24},{24,28},{1,5},{5,9},{9,... | collective-permute-start | bytes 98312 | tf_op jit(solution)/shard_map/ppermute | solution.py:347
  6.7 1.9 %shard_map.78 = (bf16[2,576,512]{2,1,0:T(8,128)(2,1)S(1)}, f32[896,128]{1,0:T(8,128)S(1)}) custom-call(s32[1,2,27]{2,1,0:T(2,128)S(1)} %get-tuple-element.17.near, bf16[3,64,512]{2,1,0:T(8,128)(2,1)S(1)} %get-tuple-element.20.own, bf16[3,64,512]{2,1,0:T(8,128)(2,1)S(1)} %get-tuple-element.21.gradient.own), custom_call_target="tpu_custom_call" | custom-call | flops 100000000 | bytes 1000000 | tf_op jit(solution)/shard_map/pallas_call | solution.py:310
  8.6 1.4 %shard_map.79 = (bf16[2,576,128]{2,1,0:T(8,128)(2,1)S(1)}, f32[896,128]{1,0:T(8,128)S(1)}) custom-call(s32[1,2,27]{2,1,0:T(2,128)S(1)} %get-tuple-element.17.near, bf16[2,64,128]{2,1,0:T(8,128)(2,1)S(1)} %get-tuple-element.18.head, bf16[2,64,128]{2,1,0:T(8,128)(2,1)S(1)} %get-tuple-element.23.tail, bf16[2,64,128]{2,1,0:T(8,128)(2,1)S(1)} %collective-permute-done.1.below, ...), custom_call_target="tpu_custom_call" | custom-call | flops 100000000 | bytes 1000000 | tf_op jit(solution)/shard_map/pallas_call | solution.py:310
  10.1 1.4 %collective-permute-done.2 = f32[448,128]{1,0:T(8,128)S(1)} collective-permute-done((f32[448,128]{1,0:T(8,128)S(1)}, f32[448,128]{1,0:T(8,128)S(1)}, u32[]{:S(2)}, u32[]{:S(2)}) %collective-permute-start.2) | collective-permute-done | bytes 229408 | tf_op jit(solution)/shard_map/ppermute | solution.py:265
  11.6 3.0 %collective-permute-start.5 = (f32[112,128]{1,0:T(8,128)S(1)}, f32[112,128]{1,0:T(8,128)S(1)}, u32[]{:S(2)}, u32[]{:S(2)}) collective-permute-start(f32[112,128]{1,0:T(8,128)S(1)} %get-tuple-element.32), channel_id=1, source_target_pairs={{0,6},{1,7},{2,4},{3,5},{4,2},{5,3},{6,0},{7,1},{8,14},{9,15},{10,... | collective-permute-start | bytes 172040 | tf_op jit(solution)/shard_map/ppermute | solution.py:265
  14.6 0.6 %collective-permute-start.3 = (f32[112,128]{1,0:T(8,128)S(1)}, f32[112,128]{1,0:T(8,128)S(1)}, u32[]{:S(2)}, u32[]{:S(2)}) collective-permute-start(f32[112,128]{1,0:T(8,128)S(1)} %get-tuple-element.31), channel_id=1, source_target_pairs={{0,2},{1,3},{2,0},{3,1},{4,6},{5,7},{6,4},{7,5},{8,10},{9,11},{10,... | collective-permute-start | bytes 172040 | tf_op jit(solution)/shard_map/ppermute | solution.py:265
  15.2 1.6 %collective-permute-done.5 = f32[112,128]{1,0:T(8,128)S(1)} collective-permute-done((f32[112,128]{1,0:T(8,128)S(1)}, f32[112,128]{1,0:T(8,128)S(1)}, u32[]{:S(2)}, u32[]{:S(2)}) %collective-permute-start.5) | collective-permute-done | bytes 57376 | tf_op jit(solution)/shard_map/ppermute | solution.py:265
  16.8 2.0 %collective-permute-done.4 = f32[112,128]{1,0:T(8,128)S(1)} collective-permute-done((f32[112,128]{1,0:T(8,128)S(1)}, f32[112,128]{1,0:T(8,128)S(1)}, u32[]{:S(2)}, u32[]{:S(2)}) %collective-permute-start.4) | collective-permute-done | bytes 57376 | tf_op jit(solution)/shard_map/ppermute | solution.py:265
  18.8 4.0 %collective-permute-start.7 = (f32[112,128]{1,0:T(8,128)S(1)}, f32[112,128]{1,0:T(8,128)S(1)}, u32[]{:S(2)}, u32[]{:S(2)}) collective-permute-start(f32[112,128]{1,0:T(8,128)S(1)} %add_add_fusion.1), channel_id=1, source_target_pairs={{0,16},{1,17},{2,18},{3,19},{4,20},{5,21},{6,22},{7,23},{8,24},{9,... | collective-permute-start | bytes 172040 | tf_op jit(solution)/shard_map/ppermute | solution.py:265
  22.8 1.3 %collective-permute-start.8 = (f32[112,128]{1,0:T(8,128)S(1)}, f32[112,128]{1,0:T(8,128)S(1)}, u32[]{:S(2)}, u32[]{:S(2)}) collective-permute-start(f32[112,128]{1,0:T(8,128)S(1)} %add_add_fusion.1), channel_id=1, source_target_pairs={{0,24},{1,25},{2,26},{3,27},{4,28},{5,29},{6,30},{7,31},{8,16},{9,... | collective-permute-start | bytes 172040 | tf_op jit(solution)/shard_map/ppermute | solution.py:265
  24.4 0.6 %collective-permute-done.7 = f32[112,128]{1,0:T(8,128)S(1)} collective-permute-done((f32[112,128]{1,0:T(8,128)S(1)}, f32[112,128]{1,0:T(8,128)S(1)}, u32[]{:S(2)}, u32[]{:S(2)}) %collective-permute-start.7) | collective-permute-done | bytes 57376 | tf_op jit(solution)/shard_map/ppermute | solution.py:265
  25.0 3.9 %collective-permute-done.8 = f32[112,128]{1,0:T(8,128)S(1)} collective-permute-done((f32[112,128]{1,0:T(8,128)S(1)}, f32[112,128]{1,0:T(8,128)S(1)}, u32[]{:S(2)}, u32[]{:S(2)}) %collective-permute-start.8) | collective-permute-done | bytes 57376 | tf_op jit(solution)/shard_map/ppermute | solution.py:265
  29.0 0.7 %collective-permute-start.11 = (f32[112,128]{1,0:T(8,128)S(1)}, f32[112,128]{1,0:T(8,128)S(1)}, u32[]{:S(2)}, u32[]{:S(2)}) collective-permute-start(f32[112,128]{1,0:T(8,128)S(1)} %add_add_fusion), channel_id=1, source_target_pairs={{0,6},{1,7},{2,4},{3,5},{4,2},{5,3},{6,0},{7,1},{8,14},{9,15},{10,... | collective-permute-start | bytes 172040 | tf_op jit(solution)/shard_map/ppermute | solution.py:265
  29.6 1.4 %collective-permute-start.10 = (f32[112,128]{1,0:T(8,128)S(1)}, f32[112,128]{1,0:T(8,128)S(1)}, u32[]{:S(2)}, u32[]{:S(2)}) collective-permute-start(f32[112,128]{1,0:T(8,128)S(1)} %add_add_fusion), channel_id=1, source_target_pairs={{0,4},{1,5},{2,6},{3,7},{4,0},{5,1},{6,2},{7,3},{8,12},{9,13},{10,... | collective-permute-start | bytes 172040 | tf_op jit(solution)/shard_map/ppermute | solution.py:265
  31.1 1.5 %collective-permute-start.9 = (f32[112,128]{1,0:T(8,128)S(1)}, f32[112,128]{1,0:T(8,128)S(1)}, u32[]{:S(2)}, u32[]{:S(2)}) collective-permute-start(f32[112,128]{1,0:T(8,128)S(1)} %add_add_fusion), channel_id=1, source_target_pairs={{0,2},{1,3},{2,0},{3,1},{4,6},{5,7},{6,4},{7,5},{8,10},{9,11},{10,... | collective-permute-start | bytes 172040 | tf_op jit(solution)/shard_map/ppermute | solution.py:265
  32.5 1.7 %collective-permute-done.11 = f32[112,128]{1,0:T(8,128)S(1)} collective-permute-done((f32[112,128]{1,0:T(8,128)S(1)}, f32[112,128]{1,0:T(8,128)S(1)}, u32[]{:S(2)}, u32[]{:S(2)}) %collective-permute-start.11) | collective-permute-done | bytes 57376 | tf_op jit(solution)/shard_map/ppermute | solution.py:265
  34.4 0.8 %collective-permute-done.9 = f32[112,128]{1,0:T(8,128)S(1)} collective-permute-done((f32[112,128]{1,0:T(8,128)S(1)}, f32[112,128]{1,0:T(8,128)S(1)}, u32[]{:S(2)}, u32[]{:S(2)}) %collective-permute-start.9) | collective-permute-done | bytes 57376 | tf_op jit(solution)/shard_map/ppermute | solution.py:265
  35.3 1.3 %collective-permute-start = (bf16[2,64,128]{2,1,0:T(8,128)(2,1)S(1)}, bf16[2,64,128]{2,1,0:T(8,128)(2,1)S(1)}, u32[]{:S(2)}, u32[]{:S(2)}) collective-permute-start(bf16[2,64,128]{2,1,0:T(8,128)(2,1)S(1)} %get-tuple-element.18.head), channel_id=1, source_target_pairs={{4,0},{8,4},{12,8},{16,12},{20,16},{24,20},{28,24},{5,1},{9,5},{13... | collective-permute-start | bytes 98312 | tf_op jit(solution)/shard_map/ppermute | solution.py:348
  36.6 1.5 %shard_map.81.inner = bf16[2,576,512]{2,1,0:T(8,128)(2,1)S(1)} custom-call(s32[1,2,27]{2,1,0:T(2,128)S(1)} %get-tuple-element.17.near, bf16[3,64,512]{2,1,0:T(8,128)(2,1)S(1)} %get-tuple-element.21.gradient.own), custom_call_target="tpu_custom_call" | custom-call | flops 100000000 | bytes 1000000 | tf_op jit(solution)/shard_map/pallas_call | solution.py:310
  38.6 2.5 %collective-permute-done.above = bf16[2,64,128]{2,1,0:T(8,128)(2,1)S(1)} collective-permute-done((bf16[2,64,128]{2,1,0:T(8,128)(2,1)S(1)}, bf16[2,64,128]{2,1,0:T(8,128)(2,1)S(1)}, u32[]{:S(2)}, u32[]{:S(2)}) %collective-permute-start) | collective-permute-done | bytes 32800 | tf_op jit(solution)/shard_map/ppermute | solution.py:348
  41.1 2.2 %shard_map.80 = (bf16[1,2,64,512]{3,2,1,0:T(8,128)(2,1)}, bf16[2,576,128]{2,1,0:T(8,128)(2,1)S(1)}) custom-call(s32[1,2,27]{2,1,0:T(2,128)S(1)} %get-tuple-element.17.near, bf16[2,64,128]{2,1,0:T(8,128)(2,1)S(1)} %get-tuple-element.18.head, bf16[2,64,128]{2,1,0:T(8,128)(2,1)S(1)} %collective-permute-done.above, ...), custom_call_target="tpu_custom_call" | custom-call | flops 100000000 | bytes 1000000 | tf_op jit(solution)/shard_map/pallas_call | solution.py:310
  43.4 1.4 %shard_map.82 = bf16[1,2,64,512]{3,2,1,0:T(8,128)(2,1)} custom-call(bf16[192,576]{1,0:T(8,128)(2,1)S(1)} %get-tuple-element.28.table, bf16[2,576,512]{2,1,0:T(8,128)(2,1)S(1)} %shard_map.81.inner, bf16[2,576,128]{2,1,0:T(8,128)(2,1)S(1)} %get-tuple-element.29.heads, bf16[2,576,128]{2,1,0:T(8,128)(2,1)S(1)} %get-tuple-element.25.tails, ...), custom_call_target="tpu_custom_call" | custom-call | flops 100000000 | bytes 1000000 | tf_op jit(solution)/shard_map/pallas_call | solution.py:310
  44.8 1.1 %shard_map.83 = f32[27,64,64]{2,1,0:T(8,128)} custom-call(f32[448,128]{1,0:T(8,128)S(1)} %pad_maximum_fusion.mine, f32[448,128]{1,0:T(8,128)S(1)} %collective-permute-done.12.theirs), custom_call_target="tpu_custom_call" | custom-call | flops 100000000 | bytes 1000000 | tf_op jit(solution)/shard_map/pallas_call | solution.py:310
  (18 shorter events, 1.3 us)
Async XLA Ops:
  1.8 6.8 %collective-permute-start.1 = (bf16[2,64,128]{2,1,0:T(8,128)(2,1)S(1)}, bf16[2,64,128]{2,1,0:T(8,128)(2,1)S(1)}, u32[]{:S(2)}, u32[]{:S(2)}) collective-permute-start(bf16[2,64,128]{2,1,0:T(8,128)(2,1)S(1)} %get-tuple-element.23.tail), channel_id=1, source_target_pairs={{0,4},{4,8},{8,12},{12,16},{16,20},{20,24},{24,28},{1,5},{5,9},{9,... | collective-permute-start | bytes 98312 | tf_op jit(solution)/shard_map/ppermute | solution.py:347
  10.0 1.6 %collective-permute-start.2 = (f32[448,128]{1,0:T(8,128)S(1)}, f32[448,128]{1,0:T(8,128)S(1)}, u32[]{:S(2)}, u32[]{:S(2)}) collective-permute-start(f32[448,128]{1,0:T(8,128)S(1)} %constant_dynamic-slice_fusion.3), channel_id=1, source_target_pairs={{0,1},{1,0},{2,3},{3,2},{4,5},{5,4},{6,7},{7,6},{8,9},{9,8},{10,11... | collective-permute-start | bytes 688136 | tf_op jit(solution)/shard_map/ppermute | solution.py:265
  11.6 5.2 %collective-permute-start.5 = (f32[112,128]{1,0:T(8,128)S(1)}, f32[112,128]{1,0:T(8,128)S(1)}, u32[]{:S(2)}, u32[]{:S(2)}) collective-permute-start(f32[112,128]{1,0:T(8,128)S(1)} %get-tuple-element.32), channel_id=1, source_target_pairs={{0,6},{1,7},{2,4},{3,5},{4,2},{5,3},{6,0},{7,1},{8,14},{9,15},{10,... | collective-permute-start | bytes 172040 | tf_op jit(solution)/shard_map/ppermute | solution.py:265
  14.6 4.2 %collective-permute-start.4 = (f32[112,128]{1,0:T(8,128)S(1)}, f32[112,128]{1,0:T(8,128)S(1)}, u32[]{:S(2)}, u32[]{:S(2)}) collective-permute-start(f32[112,128]{1,0:T(8,128)S(1)} %get-tuple-element.33), channel_id=1, source_target_pairs={{0,4},{1,5},{2,6},{3,7},{4,0},{5,1},{6,2},{7,3},{8,12},{9,13},{10,... | collective-permute-start | bytes 172040 | tf_op jit(solution)/shard_map/ppermute | solution.py:265
  14.6 4.2 %collective-permute-start.3 = (f32[112,128]{1,0:T(8,128)S(1)}, f32[112,128]{1,0:T(8,128)S(1)}, u32[]{:S(2)}, u32[]{:S(2)}) collective-permute-start(f32[112,128]{1,0:T(8,128)S(1)} %get-tuple-element.31), channel_id=1, source_target_pairs={{0,2},{1,3},{2,0},{3,1},{4,6},{5,7},{6,4},{7,5},{8,10},{9,11},{10,... | collective-permute-start | bytes 172040 | tf_op jit(solution)/shard_map/ppermute | solution.py:265
  15.2 22.9 %copy-start = (bf16[27,64,64]{2,1,0:T(8,128)(2,1)S(1)}, bf16[27,64,64]{2,1,0:T(8,128)(2,1)}, u32[]{:S(2)}) copy-start(bf16[27,64,64]{2,1,0:T(8,128)(2,1)} %weight.1) | copy-start | bytes 663556
  18.8 6.2 %collective-permute-start.7 = (f32[112,128]{1,0:T(8,128)S(1)}, f32[112,128]{1,0:T(8,128)S(1)}, u32[]{:S(2)}, u32[]{:S(2)}) collective-permute-start(f32[112,128]{1,0:T(8,128)S(1)} %add_add_fusion.1), channel_id=1, source_target_pairs={{0,16},{1,17},{2,18},{3,19},{4,20},{5,21},{6,22},{7,23},{8,24},{9,... | collective-permute-start | bytes 172040 | tf_op jit(solution)/shard_map/ppermute | solution.py:265
  22.8 6.1 %collective-permute-start.8 = (f32[112,128]{1,0:T(8,128)S(1)}, f32[112,128]{1,0:T(8,128)S(1)}, u32[]{:S(2)}, u32[]{:S(2)}) collective-permute-start(f32[112,128]{1,0:T(8,128)S(1)} %add_add_fusion.1), channel_id=1, source_target_pairs={{0,24},{1,25},{2,26},{3,27},{4,28},{5,29},{6,30},{7,31},{8,16},{9,... | collective-permute-start | bytes 172040 | tf_op jit(solution)/shard_map/ppermute | solution.py:265
  24.2 4.8 %collective-permute-start.6 = (f32[112,128]{1,0:T(8,128)S(1)}, f32[112,128]{1,0:T(8,128)S(1)}, u32[]{:S(2)}, u32[]{:S(2)}) collective-permute-start(f32[112,128]{1,0:T(8,128)S(1)} %add_add_fusion.1), channel_id=1, source_target_pairs={{0,8},{1,9},{2,10},{3,11},{4,12},{5,13},{6,14},{7,15},{8,0},{9,1},... | collective-permute-start | bytes 172040 | tf_op jit(solution)/shard_map/ppermute | solution.py:265
  29.0 5.2 %collective-permute-start.11 = (f32[112,128]{1,0:T(8,128)S(1)}, f32[112,128]{1,0:T(8,128)S(1)}, u32[]{:S(2)}, u32[]{:S(2)}) collective-permute-start(f32[112,128]{1,0:T(8,128)S(1)} %add_add_fusion), channel_id=1, source_target_pairs={{0,6},{1,7},{2,4},{3,5},{4,2},{5,3},{6,0},{7,1},{8,14},{9,15},{10,... | collective-permute-start | bytes 172040 | tf_op jit(solution)/shard_map/ppermute | solution.py:265
  29.6 4.8 %collective-permute-start.10 = (f32[112,128]{1,0:T(8,128)S(1)}, f32[112,128]{1,0:T(8,128)S(1)}, u32[]{:S(2)}, u32[]{:S(2)}) collective-permute-start(f32[112,128]{1,0:T(8,128)S(1)} %add_add_fusion), channel_id=1, source_target_pairs={{0,4},{1,5},{2,6},{3,7},{4,0},{5,1},{6,2},{7,3},{8,12},{9,13},{10,... | collective-permute-start | bytes 172040 | tf_op jit(solution)/shard_map/ppermute | solution.py:265
  31.1 4.2 %collective-permute-start.9 = (f32[112,128]{1,0:T(8,128)S(1)}, f32[112,128]{1,0:T(8,128)S(1)}, u32[]{:S(2)}, u32[]{:S(2)}) collective-permute-start(f32[112,128]{1,0:T(8,128)S(1)} %add_add_fusion), channel_id=1, source_target_pairs={{0,2},{1,3},{2,0},{3,1},{4,6},{5,7},{6,4},{7,5},{8,10},{9,11},{10,... | collective-permute-start | bytes 172040 | tf_op jit(solution)/shard_map/ppermute | solution.py:265
  35.3 9.5 %collective-permute-start.12 = (f32[448,128]{1,0:T(8,128)S(1)}, f32[448,128]{1,0:T(8,128)S(1)}, u32[]{:S(2)}, u32[]{:S(2)}) collective-permute-start(f32[448,128]{1,0:T(8,128)S(1)} %pad_maximum_fusion.mine), channel_id=1, source_target_pairs={{0,1},{1,0},{2,3},{3,2},{4,5},{5,4},{6,7},{7,6},{8,9},{9,8},{10,11... | collective-permute-start | bytes 688136 | tf_op jit(solution)/shard_map/ppermute | solution.py:265
  35.3 5.8 %collective-permute-start = (bf16[2,64,128]{2,1,0:T(8,128)(2,1)S(1)}, bf16[2,64,128]{2,1,0:T(8,128)(2,1)S(1)}, u32[]{:S(2)}, u32[]{:S(2)}) collective-permute-start(bf16[2,64,128]{2,1,0:T(8,128)(2,1)S(1)} %get-tuple-element.18.head), channel_id=1, source_target_pairs={{4,0},{8,4},{12,8},{16,12},{20,16},{24,20},{28,24},{5,1},{9,5},{13... | collective-permute-start | bytes 98312 | tf_op jit(solution)/shard_map/ppermute | solution.py:348

commit v3 on v2

--- a/solution.py
+++ b/solution.py
@@ -95,19 +95,30 @@
             )
 
 
-def set_ends(near, a, mine, other, table, parts):
+def on_odd():
+    return lax.axis_index("scene") % 2
+
+
+def set_ends(near, up, mine, other, table, parts):
     bricks, channels = mine.shape[0], mine.shape[1]
     for b in range(bricks):
-        table[b] = (other if a < 0 else mine)[b]
-        table[bricks + b] = (mine if a < 0 else other)[b]
+        table[b] = other[b]
+        table[bricks + b] = mine[b]
     table[2 * bricks] = jnp.zeros((channels, TILE), jnp.bfloat16)
-    start = (lax.axis_index("space") + min(a, 0)) * bricks
-    for b in range(bricks):
-        at = {s: index_of(near, b, a, *s, start, 2 * bricks) for s in SIDES}
+    start = (lax.axis_index("space") - 1 + up) * bricks
+
+    def place(b, c, e):
+        number = near[0, b, 18 * up + 3 * (c + 1) + e + 1]
+        at = number - start
+        turned = jnp.where(at < bricks, at + bricks, at - bricks)
+        return jnp.where(number < 0, 2 * bricks, jnp.where(up == 1, turned, at))
+
+    for b in range(bricks):
+        at = {s: place(b, *s) for s in SIDES}
         set_groups(parts, b * channels, lambda c, e: table[at[c, e]])
 
 
-def faces_kernel(features, cotangent, mask, near, head, tail, own_x, own_g, present, near_out, *rest):
+def faces_kernel(features, cotangent, mask, near, one, two, own_x, own_g, present, near_out, *rest):
     buffers, sems = rest[:3], rest[3]
     copies = [pltpu.make_async_copy(a, b, sems.at[n]) for n, (a, b) in enumerate(zip((mask, features, cotangent), buffers))]
     copies.append(pltpu.make_async_copy(near, near_out, sems.at[3]))
@@ -115,6 +126,7 @@
         copy.start()
     bricks, channels = own_x.shape[0] - 1, own_x.shape[1]
     lower = lane_of((channels, TILE)) < 64
+    odd = on_odd() == 1
     copies[0].wait()
     present[...] = buffers[0][0].astype(jnp.float32)
     for side, own in enumerate((own_x, own_g)):
@@ -126,8 +138,10 @@
         own[bricks] = jnp.zeros((channels, 512), jnp.bfloat16)
     for b in range(bricks):
         x, g = own_x[b].astype(jnp.float32), own_g[b].astype(jnp.float32)
-        head[b] = jnp.where(lower, x[:, :TILE], swap_halves(g[:, :TILE])).astype(jnp.bfloat16)
-        tail[b] = jnp.where(lower, swap_halves(g[:, 3 * TILE :]), x[:, 3 * TILE :]).astype(jnp.bfloat16)
+        head = jnp.where(lower, x[:, :TILE], swap_halves(g[:, :TILE])).astype(jnp.bfloat16)
+        tail = jnp.where(lower, swap_halves(g[:, 3 * TILE :]), x[:, 3 * TILE :]).astype(jnp.bfloat16)
+        one[b] = jnp.where(odd, head, tail)
+        two[b] = jnp.where(odd, tail, head)
     copies[3].wait()
 
 
@@ -164,24 +178,26 @@
 
 
 def outer_kernel(
-    scale, near, head, tail, below, inner, shifted, grad, table, parts, middle, select_y, select_z
+    scale, near, mine, facing, other, inner, shifted, grad, table, parts, middle, select_y, select_z
 ):
-    bricks, channels = head.shape[0], head.shape[1]
+    bricks, channels = mine.shape[0], mine.shape[1]
+    odd = on_odd()
     set_selection(select_y, select_z)
-    set_ends(near, -1, tail, below, table, parts)
+    set_ends(near, odd, mine, other, table, parts)
     shift_all(parts, select_y, select_z, middle, shifted, 1)
-    lower = lane_of((channels, TILE)) < 64
+    x_half = lane_of((channels, TILE)) // 64 == odd
     contract = (((1,), (1,)), ((), ()))
     first = last = None
     for b in range(bricks):
-        g, x = jnp.where(lower, 0, head[b]), jnp.where(lower, head[b], 0)
+        g, x = jnp.where(x_half, 0, facing[b]), jnp.where(x_half, facing[b], 0)
         one = lax.dot_general(shifted[b], g, contract, preferred_element_type=jnp.float32)
         two = lax.dot_general(x, shifted[b], contract, preferred_element_type=jnp.float32)
         first, last = (one, two) if b == 0 else (first + one, last + two)
     for yz in range(9):
         at = slice(yz * channels, (yz + 1) * channels)
-        back = slice((8 - yz) * channels, (9 - yz) * channels)
-        grad[at, :] = inner[at, :] + jnp.concatenate([first[at], last[:, back]], axis=1) * scale
+        one, two = first[at], last[:, (8 - yz) * channels : (9 - yz) * channels]
+        term = jnp.concatenate([jnp.where(odd == 1, two, one), jnp.where(odd == 1, one, two)], axis=1)
+        grad[at, :] = inner[at, :] + term * scale
     grad[9 * channels :, :] = inner[9 * channels :, :]
 
 
@@ -220,18 +236,19 @@
 
 
 def forward_kernel(
-    near, head, above, table, inner, tails, present, out, heads, ends, parts, middle, select_y, select_z
+    near, mine, other, table, inner, ends, present, out, more_ends, tiles, parts, middle, select_y, select_z
 ):
+    odd = on_odd()
     set_selection(select_y, select_z)
-    set_ends(near, 1, head, above, ends, parts)
-    shift_all(parts, select_y, select_z, middle, heads, 1)
-    lower = lane_of(heads.shape[1:]) < 64
-    convolve(table, inner, lambda b: jnp.where(lower, heads[b], tails[b]), present, out, False)
-
-
-def backward_kernel(table, inner, heads, tails, present, out):
-    lower = lane_of(heads.shape[1:]) < 64
-    convolve(table, inner, lambda b: jnp.where(lower, tails[b], heads[b]), present, out, True)
+    set_ends(near, 1 - odd, mine, other, tiles, parts)
+    shift_all(parts, select_y, select_z, middle, more_ends, 1)
+    half = lane_of(ends.shape[1:]) // 64 == odd
+    convolve(table, inner, lambda b: jnp.where(half, more_ends[b], ends[b]), present, out, False)
+
+
+def backward_kernel(table, inner, ends, more_ends, present, out):
+    half = lane_of(ends.shape[1:]) // 64 == on_odd()
+    convolve(table, inner, lambda b: jnp.where(half, ends[b], more_ends[b]), present, out, True)
 
 
 def unpack_kernel(groups, mine, theirs, out, whole):
@@ -258,6 +275,17 @@
             out[9 + at // channels, at % channels : at % channels + 32, :] = both[
                 :, side * channels : (side + 1) * channels
             ]
+
+
+def halo_pairs(spaces, scenes):
+    pairs = []
+    for scene in range(scenes):
+        line = [space * scenes + scene for space in range(spaces)]
+        line = line[::-1] if scene % 2 else line
+        pairs += list(zip(line, line[1:]))
+        if scene ^ 1 < scenes:
+            pairs.append((line[-1], line[-1] + (scene ^ 1) - scene))
+    return pairs
 
 
 def exchange(x, bit):
@@ -329,7 +357,7 @@
     ends = [scratch(2 * bricks + 1, channels, TILE), scratch(2 * few, 2 * TILE), scratch(3 * few, 2 * TILE)]
     select = [scratch(2 * TILE, 3 * TILE)] * 2
     face, brick = shape(bricks, channels, TILE), shape(bricks + 1, channels, 512)
-    head, tail, own_x, own_g, present, near = call(
+    one, two, own_x, own_g, present, near = call(
         faces_kernel,
         [face, face, brick, brick, shape(bricks, 512, dtype=jnp.float32), shape(*neighbours.shape, dtype=jnp.int32)],
         tuple(
@@ -344,8 +372,9 @@
         ],
         limit=16 << 20,
     )
-    below = lax.ppermute(tail, "space", [(i, i + 1) for i in range(spaces - 1)])
-    above = lax.ppermute(head, "space", [(i + 1, i) for i in range(spaces - 1)])
+    forth = halo_pairs(spaces, scenes)
+    got_one = lax.ppermute(one, AXES, forth)
+    got_two = lax.ppermute(two, AXES, [(b, a) for a, b in forth])
     volume, grads = shape(bricks, 9 * channels, 512), shape(rows, 2 * channels, dtype=jnp.float32)
     shifted = shape(bricks, 9 * channels, TILE)
     inner_x, grad = call(
@@ -355,24 +384,26 @@
         [SMEM, VMEM, VMEM],
         [*parts, *select, scratch(bricks, 3 * channels, 512)],
     )
-    tails, grad = call(
+    ends_one, grad = call(
         functools.partial(outer_kernel, scale),
         [shifted, grads],
-        (near, head, tail, below, grad),
+        (near, one, two, got_one, grad),
         [SMEM] + [VMEM] * 4,
         [*ends, *select],
     )
     table = shape(3 * channels, 9 * channels)
     table_y, table_g = call(tables_kernel, [table, table], (weight,), [VMEM], [])
     inner_g = call(shift_kernel, volume, (near, own_g), [SMEM, VMEM], [*parts, *select])
-    out_y, heads = call(
+    out_y, ends_two = call(
         forward_kernel,
         [shape(*features.shape), shifted],
-        (near, head, above, table_y, inner_x, tails, present),
+        (near, two, got_two, table_y, inner_x, ends_one, present),
         [SMEM] + [VMEM] * 6,
         [*ends, *select],
     )
-    out_g = call(backward_kernel, shape(*cotangent.shape), (table_g, inner_g, heads, tails, present), [VMEM] * 5, [])
+    out_g = call(
+        backward_kernel, shape(*cotangent.shape), (table_g, inner_g, ends_one, ends_two, present), [VMEM] * 5, []
+    )
     mine, theirs = all_sum(grad, groups)
     out_w = call(
         functools.partial(unpack_kernel, groups),

time: 46.1 us -> 42.6 us (0.924)
  starting transfers between devices: 19.1 us -> 16.5 us
  waiting for transfers between devices: 14.8 us -> 13.7 us
    ppermute x2, starting transfers between devices: 6.19 us -> 3.55 us  [the longest x1 3.05 us: program(): got_one = lax.ppermute(one, AXES, forth)]
    ppermute x2, waiting for transfers between devices: 2.54 us -> 1.51 us  [the longest x1 1.51 us: program(): got_two = lax.ppermute(two, AXES, [(b, a) for a, b in forth])]
  transfers between devices with their start and end apart: 13 -> 13, of which waited for: 10 -> 10; matrix products, arithmetic and copies ran while one was open for 0% -> 0% of each run, Pallas kernels for 16% -> 18%
where the time goes in v3:
time: 42.6 us; the launch traced here: 42.4 us
  starting transfers between devices  16.5 us (39%)
  waiting for transfers between devices  13.7 us (32%)
  Pallas kernels  11.2 us (26%)
  between operations  0.78 us (2%)
    ppermute x11, starting transfers between devices, exchange(): return lax.ppermute(x, AXES, [(i, i ^ bit) for i in range(count)])  13 us
    ppermute x11, waiting for transfers between devices, exchange(): return lax.ppermute(x, AXES, [(i, i ^ bit) for i in range(count)])  12.2 us
    pallas_call x8, Pallas kernels, call(): pl.pallas_call(kernel, out_shape=shapes, in_specs=specs, out_specs=VMEM i...  11.2 us
    ppermute x1, starting transfers between devices, program(): got_one = lax.ppermute(one, AXES, forth)  3.05 us
    ppermute x1, waiting for transfers between devices, program(): got_two = lax.ppermute(two, AXES, [(b, a) for a, b in forth])  1.51 us
  transfers between devices with their start and end apart: 13, of which 10 were waited for; matrix products, arithmetic and copies ran while one was open for 0% of the time, Pallas kernels for 18%

profile of v3, /device:TPU:0, one launch (start us, length us, event | category | flops | bytes accessed | tf_op | source)
XLA Modules:
  0.0 42.4 jit_solution(8130400525761572228)
XLA Ops:
  0.6 1.1 %shard_map.76 = (bf16[2,64,128]{2,1,0:T(8,128)(2,1)S(1)}, bf16[2,64,128]{2,1,0:T(8,128)(2,1)S(1)}, bf16[3,64,512]{2,1,0:T(8,128)(2,1)S(1)}, bf16[3,64,512]{2,1,0...) custom-call(bf16[1,2,64,512]{3,2,1,0:T(8,128)(2,1)} %features.1, bf16[1,2,64,512]{3,2,1,0:T(8,128)(2,1)} %cotangent.1, ...), custom_call_target="tpu_custom_call" | custom-call | flops 100000000 | bytes 1000000 | tf_op jit(solution)/shard_map/pallas_call | solution.py:338
  1.8 3.1 %collective-permute-start.1 = (bf16[2,64,128]{2,1,0:T(8,128)(2,1)S(1)}, bf16[2,64,128]{2,1,0:T(8,128)(2,1)S(1)}, u32[]{:S(2)}, u32[]{:S(2)}) collective-permute-start(bf16[2,64,128]{2,1,0:T(8,128)(2,1)S(1)} %get-tuple-element.23.mine), channel_id=1, source_target_pairs={{0,4},{4,8},{8,12},{12,16},{16,20},{20,24},{24,28},{28,29},{29,25}... | collective-permute-start | bytes 98312 | tf_op jit(solution)/shard_map/ppermute | solution.py:376
  4.8 1.9 %shard_map.78 = (bf16[2,576,512]{2,1,0:T(8,128)(2,1)S(1)}, f32[896,128]{1,0:T(8,128)S(1)}) custom-call(s32[1,2,27]{2,1,0:T(2,128)S(1)} %get-tuple-element.17.near, bf16[3,64,512]{2,1,0:T(8,128)(2,1)S(1)} %get-tuple-element.20.own, bf16[3,64,512]{2,1,0:T(8,128)(2,1)S(1)} %get-tuple-element.21.gradient.own), custom_call_target="tpu_custom_call" | custom-call | flops 100000000 | bytes 1000000 | tf_op jit(solution)/shard_map/pallas_call | solution.py:338
  6.7 1.5 %shard_map.79 = (bf16[2,576,128]{2,1,0:T(8,128)(2,1)S(1)}, f32[896,128]{1,0:T(8,128)S(1)}) custom-call(s32[1,2,27]{2,1,0:T(2,128)S(1)} %get-tuple-element.17.near, bf16[2,64,128]{2,1,0:T(8,128)(2,1)S(1)} %get-tuple-element.23.mine, bf16[2,64,128]{2,1,0:T(8,128)(2,1)S(1)} %get-tuple-element.18.facing.mine, ...), custom_call_target="tpu_custom_call" | custom-call | flops 100000000 | bytes 1000000 | tf_op jit(solution)/shard_map/pallas_call | solution.py:338
  8.4 1.4 %collective-permute-done.2 = f32[448,128]{1,0:T(8,128)S(1)} collective-permute-done((f32[448,128]{1,0:T(8,128)S(1)}, f32[448,128]{1,0:T(8,128)S(1)}, u32[]{:S(2)}, u32[]{:S(2)}) %collective-permute-start.2) | collective-permute-done | bytes 229408 | tf_op jit(solution)/shard_map/ppermute | solution.py:293
  9.9 3.1 %collective-permute-start.5 = (f32[112,128]{1,0:T(8,128)S(1)}, f32[112,128]{1,0:T(8,128)S(1)}, u32[]{:S(2)}, u32[]{:S(2)}) collective-permute-start(f32[112,128]{1,0:T(8,128)S(1)} %get-tuple-element.32), channel_id=1, source_target_pairs={{0,6},{1,7},{2,4},{3,5},{4,2},{5,3},{6,0},{7,1},{8,14},{9,15},{10,... | collective-permute-start | bytes 172040 | tf_op jit(solution)/shard_map/ppermute | solution.py:293
  13.0 0.6 %collective-permute-start.3 = (f32[112,128]{1,0:T(8,128)S(1)}, f32[112,128]{1,0:T(8,128)S(1)}, u32[]{:S(2)}, u32[]{:S(2)}) collective-permute-start(f32[112,128]{1,0:T(8,128)S(1)} %get-tuple-element.31), channel_id=1, source_target_pairs={{0,2},{1,3},{2,0},{3,1},{4,6},{5,7},{6,4},{7,5},{8,10},{9,11},{10,... | collective-permute-start | bytes 172040 | tf_op jit(solution)/shard_map/ppermute | solution.py:293
  13.6 1.6 %collective-permute-done.5 = f32[112,128]{1,0:T(8,128)S(1)} collective-permute-done((f32[112,128]{1,0:T(8,128)S(1)}, f32[112,128]{1,0:T(8,128)S(1)}, u32[]{:S(2)}, u32[]{:S(2)}) %collective-permute-start.5) | collective-permute-done | bytes 57376 | tf_op jit(solution)/shard_map/ppermute | solution.py:293
  15.2 2.0 %collective-permute-done.4 = f32[112,128]{1,0:T(8,128)S(1)} collective-permute-done((f32[112,128]{1,0:T(8,128)S(1)}, f32[112,128]{1,0:T(8,128)S(1)}, u32[]{:S(2)}, u32[]{:S(2)}) %collective-permute-start.4) | collective-permute-done | bytes 57376 | tf_op jit(solution)/shard_map/ppermute | solution.py:293
  17.2 3.9 %collective-permute-start.7 = (f32[112,128]{1,0:T(8,128)S(1)}, f32[112,128]{1,0:T(8,128)S(1)}, u32[]{:S(2)}, u32[]{:S(2)}) collective-permute-start(f32[112,128]{1,0:T(8,128)S(1)} %add_add_fusion.1), channel_id=1, source_target_pairs={{0,16},{1,17},{2,18},{3,19},{4,20},{5,21},{6,22},{7,23},{8,24},{9,... | collective-permute-start | bytes 172040 | tf_op jit(solution)/shard_map/ppermute | solution.py:293
  21.1 1.3 %collective-permute-start.8 = (f32[112,128]{1,0:T(8,128)S(1)}, f32[112,128]{1,0:T(8,128)S(1)}, u32[]{:S(2)}, u32[]{:S(2)}) collective-permute-start(f32[112,128]{1,0:T(8,128)S(1)} %add_add_fusion.1), channel_id=1, source_target_pairs={{0,24},{1,25},{2,26},{3,27},{4,28},{5,29},{6,30},{7,31},{8,16},{9,... | collective-permute-start | bytes 172040 | tf_op jit(solution)/shard_map/ppermute | solution.py:293
  22.7 0.6 %collective-permute-done.7 = f32[112,128]{1,0:T(8,128)S(1)} collective-permute-done((f32[112,128]{1,0:T(8,128)S(1)}, f32[112,128]{1,0:T(8,128)S(1)}, u32[]{:S(2)}, u32[]{:S(2)}) %collective-permute-start.7) | collective-permute-done | bytes 57376 | tf_op jit(solution)/shard_map/ppermute | solution.py:293
  23.3 3.9 %collective-permute-done.8 = f32[112,128]{1,0:T(8,128)S(1)} collective-permute-done((f32[112,128]{1,0:T(8,128)S(1)}, f32[112,128]{1,0:T(8,128)S(1)}, u32[]{:S(2)}, u32[]{:S(2)}) %collective-permute-start.8) | collective-permute-done | bytes 57376 | tf_op jit(solution)/shard_map/ppermute | solution.py:293
  27.3 0.8 %collective-permute-start.11 = (f32[112,128]{1,0:T(8,128)S(1)}, f32[112,128]{1,0:T(8,128)S(1)}, u32[]{:S(2)}, u32[]{:S(2)}) collective-permute-start(f32[112,128]{1,0:T(8,128)S(1)} %add_add_fusion), channel_id=1, source_target_pairs={{0,6},{1,7},{2,4},{3,5},{4,2},{5,3},{6,0},{7,1},{8,14},{9,15},{10,... | collective-permute-start | bytes 172040 | tf_op jit(solution)/shard_map/ppermute | solution.py:293
  28.1 1.3 %collective-permute-start.10 = (f32[112,128]{1,0:T(8,128)S(1)}, f32[112,128]{1,0:T(8,128)S(1)}, u32[]{:S(2)}, u32[]{:S(2)}) collective-permute-start(f32[112,128]{1,0:T(8,128)S(1)} %add_add_fusion), channel_id=1, source_target_pairs={{0,4},{1,5},{2,6},{3,7},{4,0},{5,1},{6,2},{7,3},{8,12},{9,13},{10,... | collective-permute-start | bytes 172040 | tf_op jit(solution)/shard_map/ppermute | solution.py:293
  29.4 1.5 %collective-permute-start.9 = (f32[112,128]{1,0:T(8,128)S(1)}, f32[112,128]{1,0:T(8,128)S(1)}, u32[]{:S(2)}, u32[]{:S(2)}) collective-permute-start(f32[112,128]{1,0:T(8,128)S(1)} %add_add_fusion), channel_id=1, source_target_pairs={{0,2},{1,3},{2,0},{3,1},{4,6},{5,7},{6,4},{7,5},{8,10},{9,11},{10,... | collective-permute-start | bytes 172040 | tf_op jit(solution)/shard_map/ppermute | solution.py:293
  30.9 1.7 %collective-permute-done.11 = f32[112,128]{1,0:T(8,128)S(1)} collective-permute-done((f32[112,128]{1,0:T(8,128)S(1)}, f32[112,128]{1,0:T(8,128)S(1)}, u32[]{:S(2)}, u32[]{:S(2)}) %collective-permute-start.11) | collective-permute-done | bytes 57376 | tf_op jit(solution)/shard_map/ppermute | solution.py:293
  32.9 0.7 %collective-permute-done.9 = f32[112,128]{1,0:T(8,128)S(1)} collective-permute-done((f32[112,128]{1,0:T(8,128)S(1)}, f32[112,128]{1,0:T(8,128)S(1)}, u32[]{:S(2)}, u32[]{:S(2)}) %collective-permute-start.9) | collective-permute-done | bytes 57376 | tf_op jit(solution)/shard_map/ppermute | solution.py:293
  33.6 0.5 %collective-permute-start = (bf16[2,64,128]{2,1,0:T(8,128)(2,1)S(1)}, bf16[2,64,128]{2,1,0:T(8,128)(2,1)S(1)}, u32[]{:S(2)}, u32[]{:S(2)}) collective-permute-start(bf16[2,64,128]{2,1,0:T(8,128)(2,1)S(1)} %get-tuple-element.18.facing.mine), channel_id=1, source_target_pairs={{4,0},{8,4},{12,8},{16,12},{20,16},{24,20},{28,24},{29,28},{25,29}... | collective-permute-start | bytes 98312 | tf_op jit(solution)/shard_map/ppermute | solution.py:377
  34.1 1.5 %shard_map.81.inner = bf16[2,576,512]{2,1,0:T(8,128)(2,1)S(1)} custom-call(s32[1,2,27]{2,1,0:T(2,128)S(1)} %get-tuple-element.17.near, bf16[3,64,512]{2,1,0:T(8,128)(2,1)S(1)} %get-tuple-element.21.gradient.own), custom_call_target="tpu_custom_call" | custom-call | flops 100000000 | bytes 1000000 | tf_op jit(solution)/shard_map/pallas_call | solution.py:338
  36.1 1.5 %collective-permute-done.other = bf16[2,64,128]{2,1,0:T(8,128)(2,1)S(1)} collective-permute-done((bf16[2,64,128]{2,1,0:T(8,128)(2,1)S(1)}, bf16[2,64,128]{2,1,0:T(8,128)(2,1)S(1)}, u32[]{:S(2)}, u32[]{:S(2)}) %collective-permute-start) | collective-permute-done | bytes 32800 | tf_op jit(solution)/shard_map/ppermute | solution.py:377
  37.6 2.2 %shard_map.80 = (bf16[1,2,64,512]{3,2,1,0:T(8,128)(2,1)}, bf16[2,576,128]{2,1,0:T(8,128)(2,1)S(1)}) custom-call(s32[1,2,27]{2,1,0:T(2,128)S(1)} %get-tuple-element.17.near, bf16[2,64,128]{2,1,0:T(8,128)(2,1)S(1)} %get-tuple-element.18.facing.mine, bf16[2,64,128]{2,1,0:T(8,128)(2,1)S(1)} %collective-permute-done.other, ...), custom_call_target="tpu_custom_call" | custom-call | flops 100000000 | bytes 1000000 | tf_op jit(solution)/shard_map/pallas_call | solution.py:338
  39.9 1.4 %shard_map.82 = bf16[1,2,64,512]{3,2,1,0:T(8,128)(2,1)} custom-call(bf16[192,576]{1,0:T(8,128)(2,1)S(1)} %get-tuple-element.28.table, bf16[2,576,512]{2,1,0:T(8,128)(2,1)S(1)} %shard_map.81.inner, bf16[2,576,128]{2,1,0:T(8,128)(2,1)S(1)} %get-tuple-element.25.ends, bf16[2,576,128]{2,1,0:T(8,128)(2,1)S(1)} %get-tuple-element.29.more_ends, ...), custom_call_target="tpu_custom_call" | custom-call | flops 100000000 | bytes 1000000 | tf_op jit(solution)/shard_map/pallas_call | solution.py:338
  41.3 1.1 %shard_map.83 = f32[27,64,64]{2,1,0:T(8,128)} custom-call(f32[448,128]{1,0:T(8,128)S(1)} %pad_maximum_fusion.mine, f32[448,128]{1,0:T(8,128)S(1)} %collective-permute-done.12.theirs), custom_call_target="tpu_custom_call" | custom-call | flops 100000000 | bytes 1000000 | tf_op jit(solution)/shard_map/pallas_call | solution.py:338
  (18 shorter events, 1.3 us)
Async XLA Ops:
  1.8 4.9 %collective-permute-start.1 = (bf16[2,64,128]{2,1,0:T(8,128)(2,1)S(1)}, bf16[2,64,128]{2,1,0:T(8,128)(2,1)S(1)}, u32[]{:S(2)}, u32[]{:S(2)}) collective-permute-start(bf16[2,64,128]{2,1,0:T(8,128)(2,1)S(1)} %get-tuple-element.23.mine), channel_id=1, source_target_pairs={{0,4},{4,8},{8,12},{12,16},{16,20},{20,24},{24,28},{28,29},{29,25}... | collective-permute-start | bytes 98312 | tf_op jit(solution)/shard_map/ppermute | solution.py:376
  8.2 1.6 %collective-permute-start.2 = (f32[448,128]{1,0:T(8,128)S(1)}, f32[448,128]{1,0:T(8,128)S(1)}, u32[]{:S(2)}, u32[]{:S(2)}) collective-permute-start(f32[448,128]{1,0:T(8,128)S(1)} %constant_dynamic-slice_fusion.3), channel_id=1, source_target_pairs={{0,1},{1,0},{2,3},{3,2},{4,5},{5,4},{6,7},{7,6},{8,9},{9,8},{10,11... | collective-permute-start | bytes 688136 | tf_op jit(solution)/shard_map/ppermute | solution.py:293
  9.9 5.4 %collective-permute-start.5 = (f32[112,128]{1,0:T(8,128)S(1)}, f32[112,128]{1,0:T(8,128)S(1)}, u32[]{:S(2)}, u32[]{:S(2)}) collective-permute-start(f32[112,128]{1,0:T(8,128)S(1)} %get-tuple-element.32), channel_id=1, source_target_pairs={{0,6},{1,7},{2,4},{3,5},{4,2},{5,3},{6,0},{7,1},{8,14},{9,15},{10,... | collective-permute-start | bytes 172040 | tf_op jit(solution)/shard_map/ppermute | solution.py:293
  13.0 4.2 %collective-permute-start.4 = (f32[112,128]{1,0:T(8,128)S(1)}, f32[112,128]{1,0:T(8,128)S(1)}, u32[]{:S(2)}, u32[]{:S(2)}) collective-permute-start(f32[112,128]{1,0:T(8,128)S(1)} %get-tuple-element.33), channel_id=1, source_target_pairs={{0,4},{1,5},{2,6},{3,7},{4,0},{5,1},{6,2},{7,3},{8,12},{9,13},{10,... | collective-permute-start | bytes 172040 | tf_op jit(solution)/shard_map/ppermute | solution.py:293
  13.0 4.2 %collective-permute-start.3 = (f32[112,128]{1,0:T(8,128)S(1)}, f32[112,128]{1,0:T(8,128)S(1)}, u32[]{:S(2)}, u32[]{:S(2)}) collective-permute-start(f32[112,128]{1,0:T(8,128)S(1)} %get-tuple-element.31), channel_id=1, source_target_pairs={{0,2},{1,3},{2,0},{3,1},{4,6},{5,7},{6,4},{7,5},{8,10},{9,11},{10,... | collective-permute-start | bytes 172040 | tf_op jit(solution)/shard_map/ppermute | solution.py:293
  13.6 22.0 %copy-start = (bf16[27,64,64]{2,1,0:T(8,128)(2,1)S(1)}, bf16[27,64,64]{2,1,0:T(8,128)(2,1)}, u32[]{:S(2)}) copy-start(bf16[27,64,64]{2,1,0:T(8,128)(2,1)} %weight.1) | copy-start | bytes 663556
  17.2 6.1 %collective-permute-start.7 = (f32[112,128]{1,0:T(8,128)S(1)}, f32[112,128]{1,0:T(8,128)S(1)}, u32[]{:S(2)}, u32[]{:S(2)}) collective-permute-start(f32[112,128]{1,0:T(8,128)S(1)} %add_add_fusion.1), channel_id=1, source_target_pairs={{0,16},{1,17},{2,18},{3,19},{4,20},{5,21},{6,22},{7,23},{8,24},{9,... | collective-permute-start | bytes 172040 | tf_op jit(solution)/shard_map/ppermute | solution.py:293
  21.1 6.1 %collective-permute-start.8 = (f32[112,128]{1,0:T(8,128)S(1)}, f32[112,128]{1,0:T(8,128)S(1)}, u32[]{:S(2)}, u32[]{:S(2)}) collective-permute-start(f32[112,128]{1,0:T(8,128)S(1)} %add_add_fusion.1), channel_id=1, source_target_pairs={{0,24},{1,25},{2,26},{3,27},{4,28},{5,29},{6,30},{7,31},{8,16},{9,... | collective-permute-start | bytes 172040 | tf_op jit(solution)/shard_map/ppermute | solution.py:293
  22.5 4.8 %collective-permute-start.6 = (f32[112,128]{1,0:T(8,128)S(1)}, f32[112,128]{1,0:T(8,128)S(1)}, u32[]{:S(2)}, u32[]{:S(2)}) collective-permute-start(f32[112,128]{1,0:T(8,128)S(1)} %add_add_fusion.1), channel_id=1, source_target_pairs={{0,8},{1,9},{2,10},{3,11},{4,12},{5,13},{6,14},{7,15},{8,0},{9,1},... | collective-permute-start | bytes 172040 | tf_op jit(solution)/shard_map/ppermute | solution.py:293
  27.3 5.2 %collective-permute-start.11 = (f32[112,128]{1,0:T(8,128)S(1)}, f32[112,128]{1,0:T(8,128)S(1)}, u32[]{:S(2)}, u32[]{:S(2)}) collective-permute-start(f32[112,128]{1,0:T(8,128)S(1)} %add_add_fusion), channel_id=1, source_target_pairs={{0,6},{1,7},{2,4},{3,5},{4,2},{5,3},{6,0},{7,1},{8,14},{9,15},{10,... | collective-permute-start | bytes 172040 | tf_op jit(solution)/shard_map/ppermute | solution.py:293
  28.1 4.8 %collective-permute-start.10 = (f32[112,128]{1,0:T(8,128)S(1)}, f32[112,128]{1,0:T(8,128)S(1)}, u32[]{:S(2)}, u32[]{:S(2)}) collective-permute-start(f32[112,128]{1,0:T(8,128)S(1)} %add_add_fusion), channel_id=1, source_target_pairs={{0,4},{1,5},{2,6},{3,7},{4,0},{5,1},{6,2},{7,3},{8,12},{9,13},{10,... | collective-permute-start | bytes 172040 | tf_op jit(solution)/shard_map/ppermute | solution.py:293
  29.4 4.2 %collective-permute-start.9 = (f32[112,128]{1,0:T(8,128)S(1)}, f32[112,128]{1,0:T(8,128)S(1)}, u32[]{:S(2)}, u32[]{:S(2)}) collective-permute-start(f32[112,128]{1,0:T(8,128)S(1)} %add_add_fusion), channel_id=1, source_target_pairs={{0,2},{1,3},{2,0},{3,1},{4,6},{5,7},{6,4},{7,5},{8,10},{9,11},{10,... | collective-permute-start | bytes 172040 | tf_op jit(solution)/shard_map/ppermute | solution.py:293
  33.6 7.7 %collective-permute-start.12 = (f32[448,128]{1,0:T(8,128)S(1)}, f32[448,128]{1,0:T(8,128)S(1)}, u32[]{:S(2)}, u32[]{:S(2)}) collective-permute-start(f32[448,128]{1,0:T(8,128)S(1)} %pad_maximum_fusion.mine), channel_id=1, source_target_pairs={{0,1},{1,0},{2,3},{3,2},{4,5},{5,4},{6,7},{7,6},{8,9},{9,8},{10,11... | collective-permute-start | bytes 688136 | tf_op jit(solution)/shard_map/ppermute | solution.py:293
  33.6 4.0 %collective-permute-start = (bf16[2,64,128]{2,1,0:T(8,128)(2,1)S(1)}, bf16[2,64,128]{2,1,0:T(8,128)(2,1)S(1)}, u32[]{:S(2)}, u32[]{:S(2)}) collective-permute-start(bf16[2,64,128]{2,1,0:T(8,128)(2,1)S(1)} %get-tuple-element.18.facing.mine), channel_id=1, source_target_pairs={{4,0},{8,4},{12,8},{16,12},{20,16},{24,20},{28,24},{29,28},{25,29}... | collective-permute-start | bytes 98312 | tf_op jit(solution)/shard_map/ppermute | solution.py:377

commit v4 on v3

--- a/solution.py
+++ b/solution.py
@@ -145,7 +145,7 @@
     copies[3].wait()
 
 
-def inner_kernel(scale, near, own, gradient, shifted, grad, parts, middle, select_y, select_z, placed):
+def inner_kernel(scale, near, own, gradient, shifted, grad, select_y, select_z, parts, middle, placed):
     rows, bricks, channels = grad.shape[0], own.shape[0] - 1, own.shape[1]
     set_selection(select_y, select_z)
     inner_parts(near, own, parts)
@@ -178,11 +178,10 @@
 
 
 def outer_kernel(
-    scale, near, mine, facing, other, inner, shifted, grad, table, parts, middle, select_y, select_z
+    scale, near, mine, facing, other, inner, select_y, select_z, shifted, grad, table, parts, middle
 ):
     bricks, channels = mine.shape[0], mine.shape[1]
     odd = on_odd()
-    set_selection(select_y, select_z)
     set_ends(near, odd, mine, other, table, parts)
     shift_all(parts, select_y, select_z, middle, shifted, 1)
     x_half = lane_of((channels, TILE)) // 64 == odd
@@ -201,8 +200,7 @@
     grad[9 * channels :, :] = inner[9 * channels :, :]
 
 
-def shift_kernel(near, own, shifted, parts, middle, select_y, select_z):
-    set_selection(select_y, select_z)
+def shift_kernel(near, own, select_y, select_z, shifted, parts, middle):
     inner_parts(near, own, parts)
     shift_all(parts, select_y, select_z, middle, shifted, TILES)
 
@@ -236,10 +234,9 @@
 
 
 def forward_kernel(
-    near, mine, other, table, inner, ends, present, out, more_ends, tiles, parts, middle, select_y, select_z
+    near, mine, other, table, inner, ends, present, select_y, select_z, out, more_ends, tiles, parts, middle
 ):
     odd = on_odd()
-    set_selection(select_y, select_z)
     set_ends(near, 1 - odd, mine, other, tiles, parts)
     shift_all(parts, select_y, select_z, middle, more_ends, 1)
     half = lane_of(ends.shape[1:]) // 64 == odd
@@ -251,30 +248,53 @@
     convolve(table, inner, lambda b: jnp.where(half, ends[b], more_ends[b]), present, out, True)
 
 
-def unpack_kernel(groups, mine, theirs, out, whole):
+def unpack_kernel(groups, own, *refs):
+    part, out, whole, blocks, sem = refs[0], *refs[-4:]
     place = lax.axis_index("space") * lax.axis_size("scene") + lax.axis_index("scene")
-    odd = place % 2
     where = place // 2 % groups
-    size = mine.shape[0] // groups
+    size, channels = part.shape[0] // groups, blocks.shape[1]
     for k in range(groups):
-        chunk = jnp.bitwise_xor(where, k)
-        at = pl.multiple_of((odd * groups + chunk) * size, 8)
-        whole[pl.ds(at, size), :] = mine[k * size : (k + 1) * size, :]
-        at = pl.multiple_of(((1 - odd) * groups + chunk) * size, 8)
-        whole[pl.ds(at, size), :] = theirs[k * size : (k + 1) * size, :]
-    channels = out.shape[1]
-    count, half = 9 * channels, 9 * channels // 2
-    for yz in range(9):
-        both = whole[yz * channels : (yz + 1) * channels, :]
-        out[yz] = both[:, :channels]
-        out[18 + yz] = both[:, channels:]
-    for row in range(0, half, 32):
-        both = whole[count + row : count + row + 32, :]
-        for side in range(2):
-            at = row + side * half
-            out[9 + at // channels, at % channels : at % channels + 32, :] = both[
-                :, side * channels : (side + 1) * channels
-            ]
+        at = pl.multiple_of(jnp.bitwise_xor(where, k) * size, 8)
+        whole[pl.ds(at, size), :] = part[k * size : (k + 1) * size, :]
+    half, count = part.shape[0], 9 * channels
+
+    def write(low, high):
+        runs = []
+
+        def put(tap, lane, row, rows, first):
+            if not runs or runs[-1][0] + runs[-1][2] not in (tap, tap + 1) or (first == 0) != (
+                runs[-1][0] + runs[-1][2] == tap
+            ):
+                runs.append([tap, sum(run[2] for run in runs), 0])
+            if first == 0:
+                runs[-1][2] += 1
+            at = runs[-1][1] + runs[-1][2] - 1
+            blocks[at, first : first + rows, :] = whole[row : row + rows, lane * channels : (lane + 1) * channels]
+
+        taps = range(low // channels, min(high, count) // channels)
+        for lane, base in ((0, 0), (1, 18)):
+            for yz in taps:
+                put(base + yz, lane, yz * channels - low, channels, 0)
+        if high > count:
+            for lane in range(2):
+                done = 0
+                while done < count // 2:
+                    at = lane * (count // 2) + done
+                    rows = min(channels - at % channels, count // 2 - done)
+                    put(9 + at // channels, lane, count - low + done, rows, at % channels)
+                    done += rows
+        copies = [
+            pltpu.make_async_copy(blocks.at[start : start + n], out.at[tap : tap + n], sem.at[i])
+            for i, (tap, start, n) in enumerate(runs)
+        ]
+        for copy in copies:
+            copy.start()
+        for copy in copies:
+            copy.wait()
+
+    lower = (place % 2 == 0) == own
+    pl.when(lower)(lambda: write(0, half))
+    pl.when(jnp.logical_not(lower))(lambda: write(half, 2 * half))
 
 
 def halo_pairs(spaces, scenes):
@@ -355,7 +375,7 @@
     parts = [scratch(2 * many, 2 * TILE), scratch(3 * many, 2 * TILE)]
     few = bricks * channels
     ends = [scratch(2 * bricks + 1, channels, TILE), scratch(2 * few, 2 * TILE), scratch(3 * few, 2 * TILE)]
-    select = [scratch(2 * TILE, 3 * TILE)] * 2
+    chosen = shape(2 * TILE, 3 * TILE)
     face, brick = shape(bricks, channels, TILE), shape(bricks + 1, channels, 512)
     one, two, own_x, own_g, present, near = call(
         faces_kernel,
@@ -377,41 +397,55 @@
     got_two = lax.ppermute(two, AXES, [(b, a) for a, b in forth])
     volume, grads = shape(bricks, 9 * channels, 512), shape(rows, 2 * channels, dtype=jnp.float32)
     shifted = shape(bricks, 9 * channels, TILE)
-    inner_x, grad = call(
+    inner_x, grad, *select = call(
         functools.partial(inner_kernel, scale),
-        [volume, grads],
+        [volume, grads, chosen, chosen],
         (near, own_x, own_g),
         [SMEM, VMEM, VMEM],
-        [*parts, *select, scratch(bricks, 3 * channels, 512)],
+        [*parts, scratch(bricks, 3 * channels, 512)],
     )
     ends_one, grad = call(
         functools.partial(outer_kernel, scale),
         [shifted, grads],
-        (near, one, two, got_one, grad),
-        [SMEM] + [VMEM] * 4,
-        [*ends, *select],
+        (near, one, two, got_one, grad, *select),
+        [SMEM] + [VMEM] * 6,
+        ends,
     )
     table = shape(3 * channels, 9 * channels)
     table_y, table_g = call(tables_kernel, [table, table], (weight,), [VMEM], [])
-    inner_g = call(shift_kernel, volume, (near, own_g), [SMEM, VMEM], [*parts, *select])
+    inner_g = call(shift_kernel, volume, (near, own_g, *select), [SMEM] + [VMEM] * 3, parts)
     out_y, ends_two = call(
         forward_kernel,
         [shape(*features.shape), shifted],
-        (near, two, got_two, table_y, inner_x, ends_one, present),
-        [SMEM] + [VMEM] * 6,
-        [*ends, *select],
+        (near, two, got_two, table_y, inner_x, ends_one, present, *select),
+        [SMEM] + [VMEM] * 8,
+        ends,
     )
     out_g = call(
         backward_kernel, shape(*cotangent.shape), (table_g, inner_g, ends_one, ends_two, present), [VMEM] * 5, []
     )
     mine, theirs = all_sum(grad, groups)
-    out_w = call(
-        functools.partial(unpack_kernel, groups),
-        shape(27, channels, channels, dtype=jnp.float32),
-        (mine, theirs),
-        [VMEM] * 2,
-        [pltpu.VMEM((rows, 2 * channels), jnp.float32)],
-    )
+    taps = shape(27, channels, channels, dtype=jnp.float32)
+
+    def unpack(own, part, *before):
+        return pl.pallas_call(
+            functools.partial(unpack_kernel, groups, own),
+            out_shape=taps,
+            in_specs=[VMEM] + [HBM] * len(before),
+            out_specs=HBM,
+            scratch_shapes=[
+                scratch(rows // 2, 2 * channels, dtype=jnp.float32),
+                scratch(14, channels, channels, dtype=jnp.float32),
+                pltpu.SemaphoreType.DMA((3,)),
+            ],
+            input_output_aliases={1: 0} if before else {},
+            compiler_params=pltpu.CompilerParams(vmem_limit_bytes=16 << 20),
+            cost_estimate=pl.CostEstimate(flops=10**6, bytes_accessed=10**6, transcendentals=0),
+            name="unpack",
+        )(part, *before)
+
+    out_w = unpack(True, mine)
+    out_w = unpack(False, theirs, out_w)
     return out_y, out_g, out_w
 
 

time: 42.6 us -> 43.3 us (1.016)
  Pallas kernels: 11.2 us -> 11.9 us
    pallas_call x0 -> x2, Pallas kernels: none -> 1.89 us  [unpack(): pl.pallas_call(functools.partial(unpack_kernel, groups, own), out_shape=t...]
    pallas_call x8 -> x7, Pallas kernels: 11.2 us -> 10 us  [call(): pl.pallas_call(kernel, out_shape=shapes, in_specs=specs, out_specs=VMEM i...]
  transfers between devices with their start and end apart: 13 -> 13, of which waited for: 10 -> 10; matrix products, arithmetic and copies ran while one was open for 0% -> 0% of each run, Pallas kernels for 18% -> 19%
where the time goes in v4:
time: 43.3 us; the launch traced here: 43.2 us
  starting transfers between devices  16.5 us (38%)
  waiting for transfers between devices  13.8 us (32%)
  Pallas kernels  11.9 us (27%)
  between operations  0.81 us (2%)
    ppermute x11, starting transfers between devices, exchange(): return lax.ppermute(x, AXES, [(i, i ^ bit) for i in range(count)])  13 us
    ppermute x11, waiting for transfers between devices, exchange(): return lax.ppermute(x, AXES, [(i, i ^ bit) for i in range(count)])  12.2 us
    pallas_call x7, Pallas kernels, call(): pl.pallas_call(kernel, out_shape=shapes, in_specs=specs, out_specs=VMEM i...  10 us
    ppermute x1, starting transfers between devices, program(): got_one = lax.ppermute(one, AXES, forth)  3.05 us
    pallas_call x2, Pallas kernels, unpack(): pl.pallas_call(functools.partial(unpack_kernel, groups, own), out_shape=t...  1.89 us
    ppermute x1, waiting for transfers between devices, program(): got_two = lax.ppermute(two, AXES, [(b, a) for a, b in forth])  1.55 us
  transfers between devices with their start and end apart: 13, of which 10 were waited for; matrix products, arithmetic and copies ran while one was open for 0% of the time, Pallas kernels for 19%

profile of v4, /device:TPU:0, one launch (start us, length us, event | category | flops | bytes accessed | tf_op | source)
XLA Modules:
  0.0 43.2 jit_solution(4449718638473442)
XLA Ops:
  0.6 1.1 %shard_map.76 = (bf16[2,64,128]{2,1,0:T(8,128)(2,1)S(1)}, bf16[2,64,128]{2,1,0:T(8,128)(2,1)S(1)}, bf16[3,64,512]{2,1,0:T(8,128)(2,1)S(1)}, bf16[3,64,512]{2,1,0...) custom-call(bf16[1,2,64,512]{3,2,1,0:T(8,128)(2,1)} %features.1, bf16[1,2,64,512]{3,2,1,0:T(8,128)(2,1)} %cotangent.1, ...), custom_call_target="tpu_custom_call" | custom-call | flops 100000000 | bytes 1000000 | tf_op jit(solution)/shard_map/pallas_call | solution.py:358
  1.8 3.1 %collective-permute-start.1 = (bf16[2,64,128]{2,1,0:T(8,128)(2,1)S(1)}, bf16[2,64,128]{2,1,0:T(8,128)(2,1)S(1)}, u32[]{:S(2)}, u32[]{:S(2)}) collective-permute-start(bf16[2,64,128]{2,1,0:T(8,128)(2,1)S(1)} %get-tuple-element.25.mine), channel_id=1, source_target_pairs={{0,4},{4,8},{8,12},{12,16},{16,20},{20,24},{24,28},{28,29},{29,25}... | collective-permute-start | bytes 98312 | tf_op jit(solution)/shard_map/ppermute | solution.py:396
  4.8 1.9 %shard_map.78 = (bf16[2,576,512]{2,1,0:T(8,128)(2,1)S(1)}, f32[896,128]{1,0:T(8,128)S(1)}, bf16[256,384]{1,0:T(8,128)(2,1)S(1)}, bf16[256,384]{1,0:T(8,128)(2,1)S(1)}) custom-call(s32[1,2,27]{2,1,0:T(2,128)S(1)} %get-tuple-element.19.near, bf16[3,64,512]{2,1,0:T(8,128)(2,1)S(1)} %get-tuple-element.22.own, bf16[3,64,512]{2,1,0:T(8,128)(2,1)S(1)} %get-tuple-element.23.gradient.own), custom_call_target="tpu_custom_call" | custom-call | flops 100000000 | bytes 1000000 | tf_op jit(solution)/shard_map/pallas_call | solution.py:358
  6.7 1.5 %shard_map.79 = (bf16[2,576,128]{2,1,0:T(8,128)(2,1)S(1)}, f32[896,128]{1,0:T(8,128)S(1)}) custom-call(s32[1,2,27]{2,1,0:T(2,128)S(1)} %get-tuple-element.19.near, bf16[2,64,128]{2,1,0:T(8,128)(2,1)S(1)} %get-tuple-element.25.mine, bf16[2,64,128]{2,1,0:T(8,128)(2,1)S(1)} %get-tuple-element.20.facing.mine, ...), custom_call_target="tpu_custom_call" | custom-call | flops 100000000 | bytes 1000000 | tf_op jit(solution)/shard_map/pallas_call | solution.py:358
  8.4 1.4 %collective-permute-done.2 = f32[448,128]{1,0:T(8,128)S(1)} collective-permute-done((f32[448,128]{1,0:T(8,128)S(1)}, f32[448,128]{1,0:T(8,128)S(1)}, u32[]{:S(2)}, u32[]{:S(2)}) %collective-permute-start.2) | collective-permute-done | bytes 229408 | tf_op jit(solution)/shard_map/ppermute | solution.py:313
  9.8 3.1 %collective-permute-start.5 = (f32[112,128]{1,0:T(8,128)S(1)}, f32[112,128]{1,0:T(8,128)S(1)}, u32[]{:S(2)}, u32[]{:S(2)}) collective-permute-start(f32[112,128]{1,0:T(8,128)S(1)} %get-tuple-element.36), channel_id=1, source_target_pairs={{0,6},{1,7},{2,4},{3,5},{4,2},{5,3},{6,0},{7,1},{8,14},{9,15},{10,... | collective-permute-start | bytes 172040 | tf_op jit(solution)/shard_map/ppermute | solution.py:313
  13.0 0.6 %collective-permute-start.3 = (f32[112,128]{1,0:T(8,128)S(1)}, f32[112,128]{1,0:T(8,128)S(1)}, u32[]{:S(2)}, u32[]{:S(2)}) collective-permute-start(f32[112,128]{1,0:T(8,128)S(1)} %get-tuple-element.35), channel_id=1, source_target_pairs={{0,2},{1,3},{2,0},{3,1},{4,6},{5,7},{6,4},{7,5},{8,10},{9,11},{10,... | collective-permute-start | bytes 172040 | tf_op jit(solution)/shard_map/ppermute | solution.py:313
  13.6 1.6 %collective-permute-done.5 = f32[112,128]{1,0:T(8,128)S(1)} collective-permute-done((f32[112,128]{1,0:T(8,128)S(1)}, f32[112,128]{1,0:T(8,128)S(1)}, u32[]{:S(2)}, u32[]{:S(2)}) %collective-permute-start.5) | collective-permute-done | bytes 57376 | tf_op jit(solution)/shard_map/ppermute | solution.py:313
  15.2 2.0 %collective-permute-done.4 = f32[112,128]{1,0:T(8,128)S(1)} collective-permute-done((f32[112,128]{1,0:T(8,128)S(1)}, f32[112,128]{1,0:T(8,128)S(1)}, u32[]{:S(2)}, u32[]{:S(2)}) %collective-permute-start.4) | collective-permute-done | bytes 57376 | tf_op jit(solution)/shard_map/ppermute | solution.py:313
  17.2 4.0 %collective-permute-start.7 = (f32[112,128]{1,0:T(8,128)S(1)}, f32[112,128]{1,0:T(8,128)S(1)}, u32[]{:S(2)}, u32[]{:S(2)}) collective-permute-start(f32[112,128]{1,0:T(8,128)S(1)} %add_add_fusion.1), channel_id=1, source_target_pairs={{0,16},{1,17},{2,18},{3,19},{4,20},{5,21},{6,22},{7,23},{8,24},{9,... | collective-permute-start | bytes 172040 | tf_op jit(solution)/shard_map/ppermute | solution.py:313
  21.1 1.3 %collective-permute-start.8 = (f32[112,128]{1,0:T(8,128)S(1)}, f32[112,128]{1,0:T(8,128)S(1)}, u32[]{:S(2)}, u32[]{:S(2)}) collective-permute-start(f32[112,128]{1,0:T(8,128)S(1)} %add_add_fusion.1), channel_id=1, source_target_pairs={{0,24},{1,25},{2,26},{3,27},{4,28},{5,29},{6,30},{7,31},{8,16},{9,... | collective-permute-start | bytes 172040 | tf_op jit(solution)/shard_map/ppermute | solution.py:313
  22.7 0.6 %collective-permute-done.7 = f32[112,128]{1,0:T(8,128)S(1)} collective-permute-done((f32[112,128]{1,0:T(8,128)S(1)}, f32[112,128]{1,0:T(8,128)S(1)}, u32[]{:S(2)}, u32[]{:S(2)}) %collective-permute-start.7) | collective-permute-done | bytes 57376 | tf_op jit(solution)/shard_map/ppermute | solution.py:313
  23.3 3.9 %collective-permute-done.8 = f32[112,128]{1,0:T(8,128)S(1)} collective-permute-done((f32[112,128]{1,0:T(8,128)S(1)}, f32[112,128]{1,0:T(8,128)S(1)}, u32[]{:S(2)}, u32[]{:S(2)}) %collective-permute-start.8) | collective-permute-done | bytes 57376 | tf_op jit(solution)/shard_map/ppermute | solution.py:313
  27.3 0.8 %collective-permute-start.11 = (f32[112,128]{1,0:T(8,128)S(1)}, f32[112,128]{1,0:T(8,128)S(1)}, u32[]{:S(2)}, u32[]{:S(2)}) collective-permute-start(f32[112,128]{1,0:T(8,128)S(1)} %add_add_fusion), channel_id=1, source_target_pairs={{0,6},{1,7},{2,4},{3,5},{4,2},{5,3},{6,0},{7,1},{8,14},{9,15},{10,... | collective-permute-start | bytes 172040 | tf_op jit(solution)/shard_map/ppermute | solution.py:313
  28.0 1.3 %collective-permute-start.10 = (f32[112,128]{1,0:T(8,128)S(1)}, f32[112,128]{1,0:T(8,128)S(1)}, u32[]{:S(2)}, u32[]{:S(2)}) collective-permute-start(f32[112,128]{1,0:T(8,128)S(1)} %add_add_fusion), channel_id=1, source_target_pairs={{0,4},{1,5},{2,6},{3,7},{4,0},{5,1},{6,2},{7,3},{8,12},{9,13},{10,... | collective-permute-start | bytes 172040 | tf_op jit(solution)/shard_map/ppermute | solution.py:313
  29.3 1.5 %collective-permute-start.9 = (f32[112,128]{1,0:T(8,128)S(1)}, f32[112,128]{1,0:T(8,128)S(1)}, u32[]{:S(2)}, u32[]{:S(2)}) collective-permute-start(f32[112,128]{1,0:T(8,128)S(1)} %add_add_fusion), channel_id=1, source_target_pairs={{0,2},{1,3},{2,0},{3,1},{4,6},{5,7},{6,4},{7,5},{8,10},{9,11},{10,... | collective-permute-start | bytes 172040 | tf_op jit(solution)/shard_map/ppermute | solution.py:313
  30.8 1.7 %collective-permute-done.11 = f32[112,128]{1,0:T(8,128)S(1)} collective-permute-done((f32[112,128]{1,0:T(8,128)S(1)}, f32[112,128]{1,0:T(8,128)S(1)}, u32[]{:S(2)}, u32[]{:S(2)}) %collective-permute-start.11) | collective-permute-done | bytes 57376 | tf_op jit(solution)/shard_map/ppermute | solution.py:313
  32.8 0.7 %collective-permute-done.9 = f32[112,128]{1,0:T(8,128)S(1)} collective-permute-done((f32[112,128]{1,0:T(8,128)S(1)}, f32[112,128]{1,0:T(8,128)S(1)}, u32[]{:S(2)}, u32[]{:S(2)}) %collective-permute-start.9) | collective-permute-done | bytes 57376 | tf_op jit(solution)/shard_map/ppermute | solution.py:313
  34.1 1.5 %shard_map.81.inner = bf16[2,576,512]{2,1,0:T(8,128)(2,1)S(1)} custom-call(s32[1,2,27]{2,1,0:T(2,128)S(1)} %get-tuple-element.19.near, bf16[3,64,512]{2,1,0:T(8,128)(2,1)S(1)} %get-tuple-element.23.gradient.own, bf16[256,384]{1,0:T(8,128)(2,1)S(1)} %get-tuple-element.27.select_y, bf16[256,384]{1,0:T(8,128)(2,1)S(1)} %get-tuple-element.28.select_z), custom_call_target="tpu_custom_call" | custom-call | flops 100000000 | bytes 1000000 | tf_op jit(solution)/shard_map/pallas_call | solution.py:358
  36.0 1.5 %collective-permute-done.other = bf16[2,64,128]{2,1,0:T(8,128)(2,1)S(1)} collective-permute-done((bf16[2,64,128]{2,1,0:T(8,128)(2,1)S(1)}, bf16[2,64,128]{2,1,0:T(8,128)(2,1)S(1)}, u32[]{:S(2)}, u32[]{:S(2)}) %collective-permute-start) | collective-permute-done | bytes 32800 | tf_op jit(solution)/shard_map/ppermute | solution.py:397
  37.6 2.2 %shard_map.80 = (bf16[1,2,64,512]{3,2,1,0:T(8,128)(2,1)}, bf16[2,576,128]{2,1,0:T(8,128)(2,1)S(1)}) custom-call(s32[1,2,27]{2,1,0:T(2,128)S(1)} %get-tuple-element.19.near, bf16[2,64,128]{2,1,0:T(8,128)(2,1)S(1)} %get-tuple-element.20.facing.mine, bf16[2,64,128]{2,1,0:T(8,128)(2,1)S(1)} %collective-permute-done.other, ...), custom_call_target="tpu_custom_call" | custom-call | flops 100000000 | bytes 1000000 | tf_op jit(solution)/shard_map/pallas_call | solution.py:358
  39.8 1.4 %shard_map.82 = bf16[1,2,64,512]{3,2,1,0:T(8,128)(2,1)} custom-call(bf16[192,576]{1,0:T(8,128)(2,1)S(1)} %get-tuple-element.32.table, bf16[2,576,512]{2,1,0:T(8,128)(2,1)S(1)} %shard_map.81.inner, bf16[2,576,128]{2,1,0:T(8,128)(2,1)S(1)} %get-tuple-element.29.ends, bf16[2,576,128]{2,1,0:T(8,128)(2,1)S(1)} %get-tuple-element.33.more_ends, ...), custom_call_target="tpu_custom_call" | custom-call | flops 100000000 | bytes 1000000 | tf_op jit(solution)/shard_map/pallas_call | solution.py:358
  41.2 0.9 %unpack.2.refs_1_ = f32[27,64,64]{2,1,0:T(8,128)} custom-call(f32[448,128]{1,0:T(8,128)S(1)} %pad_maximum_fusion.refs_0_), custom_call_target="tpu_custom_call" | custom-call | flops 1000000 | bytes 1000000 | tf_op jit(solution)/shard_map/unpack/pallas_call | solution.py:431
  42.2 0.9 %unpack.3 = f32[27,64,64]{2,1,0:T(8,128)} custom-call(f32[448,128]{1,0:T(8,128)S(1)} %collective-permute-done.12.refs_0_, f32[27,64,64]{2,1,0:T(8,128)} %unpack.2.refs_1_), custom_call_target="tpu_custom_call", output_to_operand_aliasing={{}: (1, {})} | custom-call | flops 1000000 | bytes 1000000 | tf_op jit(solution)/shard_map/unpack/pallas_call | solution.py:431
  (19 shorter events, 1.8 us)
Async XLA Ops:
  1.8 4.9 %collective-permute-start.1 = (bf16[2,64,128]{2,1,0:T(8,128)(2,1)S(1)}, bf16[2,64,128]{2,1,0:T(8,128)(2,1)S(1)}, u32[]{:S(2)}, u32[]{:S(2)}) collective-permute-start(bf16[2,64,128]{2,1,0:T(8,128)(2,1)S(1)} %get-tuple-element.25.mine), channel_id=1, source_target_pairs={{0,4},{4,8},{8,12},{12,16},{16,20},{20,24},{24,28},{28,29},{29,25}... | collective-permute-start | bytes 98312 | tf_op jit(solution)/shard_map/ppermute | solution.py:396
  8.2 1.6 %collective-permute-start.2 = (f32[448,128]{1,0:T(8,128)S(1)}, f32[448,128]{1,0:T(8,128)S(1)}, u32[]{:S(2)}, u32[]{:S(2)}) collective-permute-start(f32[448,128]{1,0:T(8,128)S(1)} %constant_dynamic-slice_fusion.3), channel_id=1, source_target_pairs={{0,1},{1,0},{2,3},{3,2},{4,5},{5,4},{6,7},{7,6},{8,9},{9,8},{10,11... | collective-permute-start | bytes 688136 | tf_op jit(solution)/shard_map/ppermute | solution.py:313
  9.8 5.3 %collective-permute-start.5 = (f32[112,128]{1,0:T(8,128)S(1)}, f32[112,128]{1,0:T(8,128)S(1)}, u32[]{:S(2)}, u32[]{:S(2)}) collective-permute-start(f32[112,128]{1,0:T(8,128)S(1)} %get-tuple-element.36), channel_id=1, source_target_pairs={{0,6},{1,7},{2,4},{3,5},{4,2},{5,3},{6,0},{7,1},{8,14},{9,15},{10,... | collective-permute-start | bytes 172040 | tf_op jit(solution)/shard_map/ppermute | solution.py:313
  13.0 4.2 %collective-permute-start.4 = (f32[112,128]{1,0:T(8,128)S(1)}, f32[112,128]{1,0:T(8,128)S(1)}, u32[]{:S(2)}, u32[]{:S(2)}) collective-permute-start(f32[112,128]{1,0:T(8,128)S(1)} %get-tuple-element.37), channel_id=1, source_target_pairs={{0,4},{1,5},{2,6},{3,7},{4,0},{5,1},{6,2},{7,3},{8,12},{9,13},{10,... | collective-permute-start | bytes 172040 | tf_op jit(solution)/shard_map/ppermute | solution.py:313
  13.0 4.2 %collective-permute-start.3 = (f32[112,128]{1,0:T(8,128)S(1)}, f32[112,128]{1,0:T(8,128)S(1)}, u32[]{:S(2)}, u32[]{:S(2)}) collective-permute-start(f32[112,128]{1,0:T(8,128)S(1)} %get-tuple-element.35), channel_id=1, source_target_pairs={{0,2},{1,3},{2,0},{3,1},{4,6},{5,7},{6,4},{7,5},{8,10},{9,11},{10,... | collective-permute-start | bytes 172040 | tf_op jit(solution)/shard_map/ppermute | solution.py:313
  17.2 6.1 %collective-permute-start.7 = (f32[112,128]{1,0:T(8,128)S(1)}, f32[112,128]{1,0:T(8,128)S(1)}, u32[]{:S(2)}, u32[]{:S(2)}) collective-permute-start(f32[112,128]{1,0:T(8,128)S(1)} %add_add_fusion.1), channel_id=1, source_target_pairs={{0,16},{1,17},{2,18},{3,19},{4,20},{5,21},{6,22},{7,23},{8,24},{9,... | collective-permute-start | bytes 172040 | tf_op jit(solution)/shard_map/ppermute | solution.py:313
  21.1 6.1 %collective-permute-start.8 = (f32[112,128]{1,0:T(8,128)S(1)}, f32[112,128]{1,0:T(8,128)S(1)}, u32[]{:S(2)}, u32[]{:S(2)}) collective-permute-start(f32[112,128]{1,0:T(8,128)S(1)} %add_add_fusion.1), channel_id=1, source_target_pairs={{0,24},{1,25},{2,26},{3,27},{4,28},{5,29},{6,30},{7,31},{8,16},{9,... | collective-permute-start | bytes 172040 | tf_op jit(solution)/shard_map/ppermute | solution.py:313
  22.4 4.8 %collective-permute-start.6 = (f32[112,128]{1,0:T(8,128)S(1)}, f32[112,128]{1,0:T(8,128)S(1)}, u32[]{:S(2)}, u32[]{:S(2)}) collective-permute-start(f32[112,128]{1,0:T(8,128)S(1)} %add_add_fusion.1), channel_id=1, source_target_pairs={{0,8},{1,9},{2,10},{3,11},{4,12},{5,13},{6,14},{7,15},{8,0},{9,1},... | collective-permute-start | bytes 172040 | tf_op jit(solution)/shard_map/ppermute | solution.py:313
  27.3 8.3 %copy-start = (bf16[27,64,64]{2,1,0:T(8,128)(2,1)S(1)}, bf16[27,64,64]{2,1,0:T(8,128)(2,1)}, u32[]{:S(2)}) copy-start(bf16[27,64,64]{2,1,0:T(8,128)(2,1)} %weight.1) | copy-start | bytes 663556
  27.3 5.2 %collective-permute-start.11 = (f32[112,128]{1,0:T(8,128)S(1)}, f32[112,128]{1,0:T(8,128)S(1)}, u32[]{:S(2)}, u32[]{:S(2)}) collective-permute-start(f32[112,128]{1,0:T(8,128)S(1)} %add_add_fusion), channel_id=1, source_target_pairs={{0,6},{1,7},{2,4},{3,5},{4,2},{5,3},{6,0},{7,1},{8,14},{9,15},{10,... | collective-permute-start | bytes 172040 | tf_op jit(solution)/shard_map/ppermute | solution.py:313
  28.0 4.8 %collective-permute-start.10 = (f32[112,128]{1,0:T(8,128)S(1)}, f32[112,128]{1,0:T(8,128)S(1)}, u32[]{:S(2)}, u32[]{:S(2)}) collective-permute-start(f32[112,128]{1,0:T(8,128)S(1)} %add_add_fusion), channel_id=1, source_target_pairs={{0,4},{1,5},{2,6},{3,7},{4,0},{5,1},{6,2},{7,3},{8,12},{9,13},{10,... | collective-permute-start | bytes 172040 | tf_op jit(solution)/shard_map/ppermute | solution.py:313
  29.3 4.2 %collective-permute-start.9 = (f32[112,128]{1,0:T(8,128)S(1)}, f32[112,128]{1,0:T(8,128)S(1)}, u32[]{:S(2)}, u32[]{:S(2)}) collective-permute-start(f32[112,128]{1,0:T(8,128)S(1)} %add_add_fusion), channel_id=1, source_target_pairs={{0,2},{1,3},{2,0},{3,1},{4,6},{5,7},{6,4},{7,5},{8,10},{9,11},{10,... | collective-permute-start | bytes 172040 | tf_op jit(solution)/shard_map/ppermute | solution.py:313
  33.5 8.7 %collective-permute-start.12 = (f32[448,128]{1,0:T(8,128)S(1)}, f32[448,128]{1,0:T(8,128)S(1)}, u32[]{:S(2)}, u32[]{:S(2)}) collective-permute-start(f32[448,128]{1,0:T(8,128)S(1)} %pad_maximum_fusion.refs_0_), channel_id=1, source_target_pairs={{0,1},{1,0},{2,3},{3,2},{4,5},{5,4},{6,7},{7,6},{8,9},{9,8},{10,11... | collective-permute-start | bytes 688136 | tf_op jit(solution)/shard_map/ppermute | solution.py:313
  33.6 4.0 %collective-permute-start = (bf16[2,64,128]{2,1,0:T(8,128)(2,1)S(1)}, bf16[2,64,128]{2,1,0:T(8,128)(2,1)S(1)}, u32[]{:S(2)}, u32[]{:S(2)}) collective-permute-start(bf16[2,64,128]{2,1,0:T(8,128)(2,1)S(1)} %get-tuple-element.20.facing.mine), channel_id=1, source_target_pairs={{4,0},{8,4},{12,8},{16,12},{20,16},{24,20},{28,24},{29,28},{25,29}... | collective-permute-start | bytes 98312 | tf_op jit(solution)/shard_map/ppermute | solution.py:397

commit v5 on v4

--- a/solution.py
+++ b/solution.py
@@ -249,14 +249,14 @@
 
 
 def unpack_kernel(groups, own, *refs):
-    part, out, whole, blocks, sem = refs[0], *refs[-4:]
+    parts, (out, whole, blocks, sem) = refs[:groups], refs[-4:]
     place = lax.axis_index("space") * lax.axis_size("scene") + lax.axis_index("scene")
     where = place // 2 % groups
-    size, channels = part.shape[0] // groups, blocks.shape[1]
+    size, channels = parts[0].shape[0], blocks.shape[1]
     for k in range(groups):
         at = pl.multiple_of(jnp.bitwise_xor(where, k) * size, 8)
-        whole[pl.ds(at, size), :] = part[k * size : (k + 1) * size, :]
-    half, count = part.shape[0], 9 * channels
+        whole[pl.ds(at, size), :] = parts[k][...]
+    half, count = groups * size, 9 * channels
 
     def write(low, high):
         runs = []
@@ -341,8 +341,10 @@
     chunks = [own]
     for k in range(1, groups):
         chunks.append(exchange(own, 2 * k))
-    mine = jnp.concatenate(chunks)
-    return mine, exchange(mine, 1)
+    theirs = []
+    for k in range(groups):
+        theirs.append(exchange(chunks[k], 1))
+    return chunks, theirs
 
 
 def program(features, cotangent, weight, neighbours, occupancy):
@@ -427,22 +429,22 @@
     mine, theirs = all_sum(grad, groups)
     taps = shape(27, channels, channels, dtype=jnp.float32)
 
-    def unpack(own, part, *before):
+    def unpack(own, parts, *before):
         return pl.pallas_call(
             functools.partial(unpack_kernel, groups, own),
             out_shape=taps,
-            in_specs=[VMEM] + [HBM] * len(before),
+            in_specs=[VMEM] * groups + [HBM] * len(before),
             out_specs=HBM,
             scratch_shapes=[
                 scratch(rows // 2, 2 * channels, dtype=jnp.float32),
                 scratch(14, channels, channels, dtype=jnp.float32),
                 pltpu.SemaphoreType.DMA((3,)),
             ],
-            input_output_aliases={1: 0} if before else {},
+            input_output_aliases={groups: 0} if before else {},
             compiler_params=pltpu.CompilerParams(vmem_limit_bytes=16 << 20),
             cost_estimate=pl.CostEstimate(flops=10**6, bytes_accessed=10**6, transcendentals=0),
             name="unpack",
-        )(part, *before)
+        )(*parts, *before)
 
     out_w = unpack(True, mine)
     out_w = unpack(False, theirs, out_w)

time: 43.3 us -> 43.4 us (level)
    ppermute x11 -> x14, waiting for transfers between devices: 12.2 us -> 12.4 us  [exchange(): return lax.ppermute(x, AXES, [(i, i ^ bit) for i in range(count)])]
    ppermute x11 -> x14, starting transfers between devices: 13 us -> 12.9 us  [exchange(): return lax.ppermute(x, AXES, [(i, i ^ bit) for i in range(count)])]
  transfers between devices with their start and end apart: 13 -> 16, of which waited for: 10 -> 10; matrix products, arithmetic and copies ran while one was open for 0% -> 0% of each run, Pallas kernels for 19% -> 19%
where the time goes in v5:
time: 43.4 us; the launch traced here: 43.2 us
  starting transfers between devices  16.5 us (38%)
  waiting for transfers between devices  13.9 us (32%)
  Pallas kernels  11.9 us (27%)
  between operations  0.82 us (2%)
    ppermute x14, starting transfers between devices, exchange(): return lax.ppermute(x, AXES, [(i, i ^ bit) for i in range(count)])  12.9 us
    ppermute x14, waiting for transfers between devices, exchange(): return lax.ppermute(x, AXES, [(i, i ^ bit) for i in range(count)])  12.4 us
    pallas_call x7, Pallas kernels, call(): pl.pallas_call(kernel, out_shape=shapes, in_specs=specs, out_specs=VMEM i...  10 us
    ppermute x1, starting transfers between devices, program(): got_one = lax.ppermute(one, AXES, forth)  3.05 us
    pallas_call x2, Pallas kernels, unpack(): pl.pallas_call(functools.partial(unpack_kernel, groups, own), out_shape=t...  1.9 us
    ppermute x1, waiting for transfers between devices, program(): got_two = lax.ppermute(two, AXES, [(b, a) for a, b in forth])  1.48 us
  transfers between devices with their start and end apart: 16, of which 10 were waited for; matrix products, arithmetic and copies ran while one was open for 0% of the time, Pallas kernels for 19%

profile of v5, /device:TPU:0, one launch (start us, length us, event | category | flops | bytes accessed | tf_op | source)
XLA Modules:
  0.0 43.2 jit_solution(6496469469287064304)
XLA Ops:
  0.6 1.1 %shard_map.76 = (bf16[2,64,128]{2,1,0:T(8,128)(2,1)S(1)}, bf16[2,64,128]{2,1,0:T(8,128)(2,1)S(1)}, bf16[3,64,512]{2,1,0:T(8,128)(2,1)S(1)}, bf16[3,64,512]{2,1,0...) custom-call(bf16[1,2,64,512]{3,2,1,0:T(8,128)(2,1)} %features.1, bf16[1,2,64,512]{3,2,1,0:T(8,128)(2,1)} %cotangent.1, ...), custom_call_target="tpu_custom_call" | custom-call | flops 100000000 | bytes 1000000 | tf_op jit(solution)/shard_map/pallas_call | solution.py:360
  1.8 3.1 %collective-permute-start.1 = (bf16[2,64,128]{2,1,0:T(8,128)(2,1)S(1)}, bf16[2,64,128]{2,1,0:T(8,128)(2,1)S(1)}, u32[]{:S(2)}, u32[]{:S(2)}) collective-permute-start(bf16[2,64,128]{2,1,0:T(8,128)(2,1)S(1)} %get-tuple-element.25.mine), channel_id=1, source_target_pairs={{0,4},{4,8},{8,12},{12,16},{16,20},{20,24},{24,28},{28,29},{29,25}... | collective-permute-start | bytes 98312 | tf_op jit(solution)/shard_map/ppermute | solution.py:398
  4.8 1.9 %shard_map.78 = (bf16[2,576,512]{2,1,0:T(8,128)(2,1)S(1)}, f32[896,128]{1,0:T(8,128)S(1)}, bf16[256,384]{1,0:T(8,128)(2,1)S(1)}, bf16[256,384]{1,0:T(8,128)(2,1)S(1)}) custom-call(s32[1,2,27]{2,1,0:T(2,128)S(1)} %get-tuple-element.19.near, bf16[3,64,512]{2,1,0:T(8,128)(2,1)S(1)} %get-tuple-element.22.own, bf16[3,64,512]{2,1,0:T(8,128)(2,1)S(1)} %get-tuple-element.23.gradient.own), custom_call_target="tpu_custom_call" | custom-call | flops 100000000 | bytes 1000000 | tf_op jit(solution)/shard_map/pallas_call | solution.py:360
  6.7 1.5 %shard_map.79 = (bf16[2,576,128]{2,1,0:T(8,128)(2,1)S(1)}, f32[896,128]{1,0:T(8,128)S(1)}) custom-call(s32[1,2,27]{2,1,0:T(2,128)S(1)} %get-tuple-element.19.near, bf16[2,64,128]{2,1,0:T(8,128)(2,1)S(1)} %get-tuple-element.25.mine, bf16[2,64,128]{2,1,0:T(8,128)(2,1)S(1)} %get-tuple-element.20.facing.mine, ...), custom_call_target="tpu_custom_call" | custom-call | flops 100000000 | bytes 1000000 | tf_op jit(solution)/shard_map/pallas_call | solution.py:360
  8.4 1.4 %collective-permute-done.2 = f32[448,128]{1,0:T(8,128)S(1)} collective-permute-done((f32[448,128]{1,0:T(8,128)S(1)}, f32[448,128]{1,0:T(8,128)S(1)}, u32[]{:S(2)}, u32[]{:S(2)}) %collective-permute-start.2) | collective-permute-done | bytes 229408 | tf_op jit(solution)/shard_map/ppermute | solution.py:313
  9.9 3.1 %collective-permute-start.5 = (f32[112,128]{1,0:T(8,128)S(1)}, f32[112,128]{1,0:T(8,128)S(1)}, u32[]{:S(2)}, u32[]{:S(2)}) collective-permute-start(f32[112,128]{1,0:T(8,128)S(1)} %get-tuple-element.36), channel_id=1, source_target_pairs={{0,6},{1,7},{2,4},{3,5},{4,2},{5,3},{6,0},{7,1},{8,14},{9,15},{10,... | collective-permute-start | bytes 172040 | tf_op jit(solution)/shard_map/ppermute | solution.py:313
  13.0 0.6 %collective-permute-start.3 = (f32[112,128]{1,0:T(8,128)S(1)}, f32[112,128]{1,0:T(8,128)S(1)}, u32[]{:S(2)}, u32[]{:S(2)}) collective-permute-start(f32[112,128]{1,0:T(8,128)S(1)} %get-tuple-element.35), channel_id=1, source_target_pairs={{0,2},{1,3},{2,0},{3,1},{4,6},{5,7},{6,4},{7,5},{8,10},{9,11},{10,... | collective-permute-start | bytes 172040 | tf_op jit(solution)/shard_map/ppermute | solution.py:313
  13.6 1.6 %collective-permute-done.5 = f32[112,128]{1,0:T(8,128)S(1)} collective-permute-done((f32[112,128]{1,0:T(8,128)S(1)}, f32[112,128]{1,0:T(8,128)S(1)}, u32[]{:S(2)}, u32[]{:S(2)}) %collective-permute-start.5) | collective-permute-done | bytes 57376 | tf_op jit(solution)/shard_map/ppermute | solution.py:313
  15.2 2.0 %collective-permute-done.4 = f32[112,128]{1,0:T(8,128)S(1)} collective-permute-done((f32[112,128]{1,0:T(8,128)S(1)}, f32[112,128]{1,0:T(8,128)S(1)}, u32[]{:S(2)}, u32[]{:S(2)}) %collective-permute-start.4) | collective-permute-done | bytes 57376 | tf_op jit(solution)/shard_map/ppermute | solution.py:313
  17.2 4.0 %collective-permute-start.7 = (f32[112,128]{1,0:T(8,128)S(1)}, f32[112,128]{1,0:T(8,128)S(1)}, u32[]{:S(2)}, u32[]{:S(2)}) collective-permute-start(f32[112,128]{1,0:T(8,128)S(1)} %add_add_fusion.1), channel_id=1, source_target_pairs={{0,16},{1,17},{2,18},{3,19},{4,20},{5,21},{6,22},{7,23},{8,24},{9,... | collective-permute-start | bytes 172040 | tf_op jit(solution)/shard_map/ppermute | solution.py:313
  21.1 1.3 %collective-permute-start.8 = (f32[112,128]{1,0:T(8,128)S(1)}, f32[112,128]{1,0:T(8,128)S(1)}, u32[]{:S(2)}, u32[]{:S(2)}) collective-permute-start(f32[112,128]{1,0:T(8,128)S(1)} %add_add_fusion.1), channel_id=1, source_target_pairs={{0,24},{1,25},{2,26},{3,27},{4,28},{5,29},{6,30},{7,31},{8,16},{9,... | collective-permute-start | bytes 172040 | tf_op jit(solution)/shard_map/ppermute | solution.py:313
  22.7 0.6 %collective-permute-done.7 = f32[112,128]{1,0:T(8,128)S(1)} collective-permute-done((f32[112,128]{1,0:T(8,128)S(1)}, f32[112,128]{1,0:T(8,128)S(1)}, u32[]{:S(2)}, u32[]{:S(2)}) %collective-permute-start.7) | collective-permute-done | bytes 57376 | tf_op jit(solution)/shard_map/ppermute | solution.py:313
  23.3 3.9 %collective-permute-done.8 = f32[112,128]{1,0:T(8,128)S(1)} collective-permute-done((f32[112,128]{1,0:T(8,128)S(1)}, f32[112,128]{1,0:T(8,128)S(1)}, u32[]{:S(2)}, u32[]{:S(2)}) %collective-permute-start.8) | collective-permute-done | bytes 57376 | tf_op jit(solution)/shard_map/ppermute | solution.py:313
  27.3 0.6 %collective-permute-start.10 = (f32[112,128]{1,0:T(8,128)S(1)}, f32[112,128]{1,0:T(8,128)S(1)}, u32[]{:S(2)}, u32[]{:S(2)}) collective-permute-start(f32[112,128]{1,0:T(8,128)S(1)} %add_add_fusion.refs_0_), channel_id=1, source_target_pairs={{0,2},{1,3},{2,0},{3,1},{4,6},{5,7},{6,4},{7,5},{8,10},{9,11},{10,... | collective-permute-start | bytes 172040 | tf_op jit(solution)/shard_map/ppermute | solution.py:313
  27.9 0.7 %collective-permute-start.12 = (f32[112,128]{1,0:T(8,128)S(1)}, f32[112,128]{1,0:T(8,128)S(1)}, u32[]{:S(2)}, u32[]{:S(2)}) collective-permute-start(f32[112,128]{1,0:T(8,128)S(1)} %add_add_fusion.refs_0_), channel_id=1, source_target_pairs={{0,4},{1,5},{2,6},{3,7},{4,0},{5,1},{6,2},{7,3},{8,12},{9,13},{10,... | collective-permute-start | bytes 172040 | tf_op jit(solution)/shard_map/ppermute | solution.py:313
  28.6 2.2 %collective-permute-start.14 = (f32[112,128]{1,0:T(8,128)S(1)}, f32[112,128]{1,0:T(8,128)S(1)}, u32[]{:S(2)}, u32[]{:S(2)}) collective-permute-start(f32[112,128]{1,0:T(8,128)S(1)} %add_add_fusion.refs_0_), channel_id=1, source_target_pairs={{0,6},{1,7},{2,4},{3,5},{4,2},{5,3},{6,0},{7,1},{8,14},{9,15},{10,... | collective-permute-start | bytes 172040 | tf_op jit(solution)/shard_map/ppermute | solution.py:313
  30.8 0.7 %collective-permute-done.10.refs_1_ = f32[112,128]{1,0:T(8,128)S(1)} collective-permute-done((f32[112,128]{1,0:T(8,128)S(1)}, f32[112,128]{1,0:T(8,128)S(1)}, u32[]{:S(2)}, u32[]{:S(2)}) %collective-permute-start.10) | collective-permute-done | bytes 57376 | tf_op jit(solution)/shard_map/ppermute | solution.py:313
  32.1 1.6 %collective-permute-done.14.refs_3_ = f32[112,128]{1,0:T(8,128)S(1)} collective-permute-done((f32[112,128]{1,0:T(8,128)S(1)}, f32[112,128]{1,0:T(8,128)S(1)}, u32[]{:S(2)}, u32[]{:S(2)}) %collective-permute-start.14) | collective-permute-done | bytes 57376 | tf_op jit(solution)/shard_map/ppermute | solution.py:313
  34.2 1.5 %shard_map.81.inner = bf16[2,576,512]{2,1,0:T(8,128)(2,1)S(1)} custom-call(s32[1,2,27]{2,1,0:T(2,128)S(1)} %get-tuple-element.19.near, bf16[3,64,512]{2,1,0:T(8,128)(2,1)S(1)} %get-tuple-element.23.gradient.own, bf16[256,384]{1,0:T(8,128)(2,1)S(1)} %get-tuple-element.27.select_y, bf16[256,384]{1,0:T(8,128)(2,1)S(1)} %get-tuple-element.28.select_z), custom_call_target="tpu_custom_call" | custom-call | flops 100000000 | bytes 1000000 | tf_op jit(solution)/shard_map/pallas_call | solution.py:360
  36.1 1.5 %collective-permute-done.other = bf16[2,64,128]{2,1,0:T(8,128)(2,1)S(1)} collective-permute-done((bf16[2,64,128]{2,1,0:T(8,128)(2,1)S(1)}, bf16[2,64,128]{2,1,0:T(8,128)(2,1)S(1)}, u32[]{:S(2)}, u32[]{:S(2)}) %collective-permute-start) | collective-permute-done | bytes 32800 | tf_op jit(solution)/shard_map/ppermute | solution.py:399
  37.6 2.2 %shard_map.80 = (bf16[1,2,64,512]{3,2,1,0:T(8,128)(2,1)}, bf16[2,576,128]{2,1,0:T(8,128)(2,1)S(1)}) custom-call(s32[1,2,27]{2,1,0:T(2,128)S(1)} %get-tuple-element.19.near, bf16[2,64,128]{2,1,0:T(8,128)(2,1)S(1)} %get-tuple-element.20.facing.mine, bf16[2,64,128]{2,1,0:T(8,128)(2,1)S(1)} %collective-permute-done.other, ...), custom_call_target="tpu_custom_call" | custom-call | flops 100000000 | bytes 1000000 | tf_op jit(solution)/shard_map/pallas_call | solution.py:360
  39.8 1.4 %shard_map.82 = bf16[1,2,64,512]{3,2,1,0:T(8,128)(2,1)} custom-call(bf16[192,576]{1,0:T(8,128)(2,1)S(1)} %get-tuple-element.32.table, bf16[2,576,512]{2,1,0:T(8,128)(2,1)S(1)} %shard_map.81.inner, bf16[2,576,128]{2,1,0:T(8,128)(2,1)S(1)} %get-tuple-element.29.ends, bf16[2,576,128]{2,1,0:T(8,128)(2,1)S(1)} %get-tuple-element.33.more_ends, ...), custom_call_target="tpu_custom_call" | custom-call | flops 100000000 | bytes 1000000 | tf_op jit(solution)/shard_map/pallas_call | solution.py:360
  41.2 0.9 %unpack.2.refs_4_ = f32[27,64,64]{2,1,0:T(8,128)} custom-call(f32[112,128]{1,0:T(8,128)S(1)} %add_add_fusion.refs_0_, f32[112,128]{1,0:T(8,128)S(1)} %collective-permute-done.10.refs_1_, f32[112,128]{1,0:T(8,128)S(1)} %collective-permute-done.12.refs_2_, f32[112,128]{1,0:T(8,128)S(1)} %collective-permute-done.14.refs_3_), custom_call_target="tpu_custom_call" | custom-call | flops 1000000 | bytes 1000000 | tf_op jit(solution)/shard_map/unpack/pallas_call | solution.py:433
  42.2 0.9 %unpack.3 = f32[27,64,64]{2,1,0:T(8,128)} custom-call(f32[112,128]{1,0:T(8,128)S(1)} %collective-permute-done.9.refs_0_, f32[112,128]{1,0:T(8,128)S(1)} %collective-permute-done.11.refs_1_, f32[112,128]{1,0:T(8,128)S(1)} %collective-permute-done.13.refs_2_, f32[112,128]{1,0:T(8,128)S(1)} %collective-permute-done.15.refs_3_, ...), custom_call_target="tpu_custom_call", output_to_operand_aliasing={{}: (4, {})} | custom-call | flops 1000000 | bytes 1000000 | tf_op jit(solution)/shard_map/unpack/pallas_call | solution.py:433
  (24 shorter events, 2.0 us)
Async XLA Ops:
  1.8 4.9 %collective-permute-start.1 = (bf16[2,64,128]{2,1,0:T(8,128)(2,1)S(1)}, bf16[2,64,128]{2,1,0:T(8,128)(2,1)S(1)}, u32[]{:S(2)}, u32[]{:S(2)}) collective-permute-start(bf16[2,64,128]{2,1,0:T(8,128)(2,1)S(1)} %get-tuple-element.25.mine), channel_id=1, source_target_pairs={{0,4},{4,8},{8,12},{12,16},{16,20},{20,24},{24,28},{28,29},{29,25}... | collective-permute-start | bytes 98312 | tf_op jit(solution)/shard_map/ppermute | solution.py:398
  8.2 1.6 %collective-permute-start.2 = (f32[448,128]{1,0:T(8,128)S(1)}, f32[448,128]{1,0:T(8,128)S(1)}, u32[]{:S(2)}, u32[]{:S(2)}) collective-permute-start(f32[448,128]{1,0:T(8,128)S(1)} %constant_dynamic-slice_fusion.3), channel_id=1, source_target_pairs={{0,1},{1,0},{2,3},{3,2},{4,5},{5,4},{6,7},{7,6},{8,9},{9,8},{10,11... | collective-permute-start | bytes 688136 | tf_op jit(solution)/shard_map/ppermute | solution.py:313
  9.8 25.8 %copy-start = (bf16[27,64,64]{2,1,0:T(8,128)(2,1)S(1)}, bf16[27,64,64]{2,1,0:T(8,128)(2,1)}, u32[]{:S(2)}) copy-start(bf16[27,64,64]{2,1,0:T(8,128)(2,1)} %weight.1) | copy-start | bytes 663556
  9.9 5.3 %collective-permute-start.5 = (f32[112,128]{1,0:T(8,128)S(1)}, f32[112,128]{1,0:T(8,128)S(1)}, u32[]{:S(2)}, u32[]{:S(2)}) collective-permute-start(f32[112,128]{1,0:T(8,128)S(1)} %get-tuple-element.36), channel_id=1, source_target_pairs={{0,6},{1,7},{2,4},{3,5},{4,2},{5,3},{6,0},{7,1},{8,14},{9,15},{10,... | collective-permute-start | bytes 172040 | tf_op jit(solution)/shard_map/ppermute | solution.py:313
  13.0 4.2 %collective-permute-start.4 = (f32[112,128]{1,0:T(8,128)S(1)}, f32[112,128]{1,0:T(8,128)S(1)}, u32[]{:S(2)}, u32[]{:S(2)}) collective-permute-start(f32[112,128]{1,0:T(8,128)S(1)} %get-tuple-element.37), channel_id=1, source_target_pairs={{0,4},{1,5},{2,6},{3,7},{4,0},{5,1},{6,2},{7,3},{8,12},{9,13},{10,... | collective-permute-start | bytes 172040 | tf_op jit(solution)/shard_map/ppermute | solution.py:313
  13.0 4.2 %collective-permute-start.3 = (f32[112,128]{1,0:T(8,128)S(1)}, f32[112,128]{1,0:T(8,128)S(1)}, u32[]{:S(2)}, u32[]{:S(2)}) collective-permute-start(f32[112,128]{1,0:T(8,128)S(1)} %get-tuple-element.35), channel_id=1, source_target_pairs={{0,2},{1,3},{2,0},{3,1},{4,6},{5,7},{6,4},{7,5},{8,10},{9,11},{10,... | collective-permute-start | bytes 172040 | tf_op jit(solution)/shard_map/ppermute | solution.py:313
  17.2 6.1 %collective-permute-start.7 = (f32[112,128]{1,0:T(8,128)S(1)}, f32[112,128]{1,0:T(8,128)S(1)}, u32[]{:S(2)}, u32[]{:S(2)}) collective-permute-start(f32[112,128]{1,0:T(8,128)S(1)} %add_add_fusion.1), channel_id=1, source_target_pairs={{0,16},{1,17},{2,18},{3,19},{4,20},{5,21},{6,22},{7,23},{8,24},{9,... | collective-permute-start | bytes 172040 | tf_op jit(solution)/shard_map/ppermute | solution.py:313
  21.1 6.1 %collective-permute-start.8 = (f32[112,128]{1,0:T(8,128)S(1)}, f32[112,128]{1,0:T(8,128)S(1)}, u32[]{:S(2)}, u32[]{:S(2)}) collective-permute-start(f32[112,128]{1,0:T(8,128)S(1)} %add_add_fusion.1), channel_id=1, source_target_pairs={{0,24},{1,25},{2,26},{3,27},{4,28},{5,29},{6,30},{7,31},{8,16},{9,... | collective-permute-start | bytes 172040 | tf_op jit(solution)/shard_map/ppermute | solution.py:313
  22.5 4.8 %collective-permute-start.6 = (f32[112,128]{1,0:T(8,128)S(1)}, f32[112,128]{1,0:T(8,128)S(1)}, u32[]{:S(2)}, u32[]{:S(2)}) collective-permute-start(f32[112,128]{1,0:T(8,128)S(1)} %add_add_fusion.1), channel_id=1, source_target_pairs={{0,8},{1,9},{2,10},{3,11},{4,12},{5,13},{6,14},{7,15},{8,0},{9,1},... | collective-permute-start | bytes 172040 | tf_op jit(solution)/shard_map/ppermute | solution.py:313
  27.3 4.2 %collective-permute-start.10 = (f32[112,128]{1,0:T(8,128)S(1)}, f32[112,128]{1,0:T(8,128)S(1)}, u32[]{:S(2)}, u32[]{:S(2)}) collective-permute-start(f32[112,128]{1,0:T(8,128)S(1)} %add_add_fusion.refs_0_), channel_id=1, source_target_pairs={{0,2},{1,3},{2,0},{3,1},{4,6},{5,7},{6,4},{7,5},{8,10},{9,11},{10,... | collective-permute-start | bytes 172040 | tf_op jit(solution)/shard_map/ppermute | solution.py:313
  27.9 4.2 %collective-permute-start.12 = (f32[112,128]{1,0:T(8,128)S(1)}, f32[112,128]{1,0:T(8,128)S(1)}, u32[]{:S(2)}, u32[]{:S(2)}) collective-permute-start(f32[112,128]{1,0:T(8,128)S(1)} %add_add_fusion.refs_0_), channel_id=1, source_target_pairs={{0,4},{1,5},{2,6},{3,7},{4,0},{5,1},{6,2},{7,3},{8,12},{9,13},{10,... | collective-permute-start | bytes 172040 | tf_op jit(solution)/shard_map/ppermute | solution.py:313
  28.6 5.1 %collective-permute-start.14 = (f32[112,128]{1,0:T(8,128)S(1)}, f32[112,128]{1,0:T(8,128)S(1)}, u32[]{:S(2)}, u32[]{:S(2)}) collective-permute-start(f32[112,128]{1,0:T(8,128)S(1)} %add_add_fusion.refs_0_), channel_id=1, source_target_pairs={{0,6},{1,7},{2,4},{3,5},{4,2},{5,3},{6,0},{7,1},{8,14},{9,15},{10,... | collective-permute-start | bytes 172040 | tf_op jit(solution)/shard_map/ppermute | solution.py:313
  30.8 11.4 %collective-permute-start.9 = (f32[112,128]{1,0:T(8,128)S(1)}, f32[112,128]{1,0:T(8,128)S(1)}, u32[]{:S(2)}, u32[]{:S(2)}) collective-permute-start(f32[112,128]{1,0:T(8,128)S(1)} %add_add_fusion.refs_0_), channel_id=1, source_target_pairs={{0,1},{1,0},{2,3},{3,2},{4,5},{5,4},{6,7},{7,6},{8,9},{9,8},{10,11... | collective-permute-start | bytes 172040 | tf_op jit(solution)/shard_map/ppermute | solution.py:313
  31.5 10.7 %collective-permute-start.11 = (f32[112,128]{1,0:T(8,128)S(1)}, f32[112,128]{1,0:T(8,128)S(1)}, u32[]{:S(2)}, u32[]{:S(2)}) collective-permute-start(f32[112,128]{1,0:T(8,128)S(1)} %collective-permute-done.10.refs_1_), channel_id=1, source_target_pairs={{0,1},{1,0},{2,3},{3,2},{4,5},{5,4},{6,7},{7,6},{8,9},{9,8},{10,11... | collective-permute-start | bytes 172040 | tf_op jit(solution)/shard_map/ppermute | solution.py:313
  32.1 10.2 %collective-permute-start.13 = (f32[112,128]{1,0:T(8,128)S(1)}, f32[112,128]{1,0:T(8,128)S(1)}, u32[]{:S(2)}, u32[]{:S(2)}) collective-permute-start(f32[112,128]{1,0:T(8,128)S(1)} %collective-permute-done.12.refs_2_), channel_id=1, source_target_pairs={{0,1},{1,0},{2,3},{3,2},{4,5},{5,4},{6,7},{7,6},{8,9},{9,8},{10,11... | collective-permute-start | bytes 172040 | tf_op jit(solution)/shard_map/ppermute | solution.py:313
  33.7 8.6 %collective-permute-start.15 = (f32[112,128]{1,0:T(8,128)S(1)}, f32[112,128]{1,0:T(8,128)S(1)}, u32[]{:S(2)}, u32[]{:S(2)}) collective-permute-start(f32[112,128]{1,0:T(8,128)S(1)} %collective-permute-done.14.refs_3_), channel_id=1, source_target_pairs={{0,1},{1,0},{2,3},{3,2},{4,5},{5,4},{6,7},{7,6},{8,9},{9,8},{10,11... | collective-permute-start | bytes 172040 | tf_op jit(solution)/shard_map/ppermute | solution.py:313
  33.7 3.9 %collective-permute-start = (bf16[2,64,128]{2,1,0:T(8,128)(2,1)S(1)}, bf16[2,64,128]{2,1,0:T(8,128)(2,1)S(1)}, u32[]{:S(2)}, u32[]{:S(2)}) collective-permute-start(bf16[2,64,128]{2,1,0:T(8,128)(2,1)S(1)} %get-tuple-element.20.facing.mine), channel_id=1, source_target_pairs={{4,0},{8,4},{12,8},{16,12},{20,16},{24,20},{28,24},{29,28},{25,29}... | collective-permute-start | bytes 98312 | tf_op jit(solution)/shard_map/ppermute | solution.py:399

commit v6 on v5

--- a/solution.py
+++ b/solution.py
@@ -42,19 +42,29 @@
     return pltpu.roll(x, 64, x.ndim - 1)
 
 
-def set_groups(parts, row, pick):
-    channels, rows = pick(0, 0).shape[0], parts.shape[0] // 2
-    lane = lane_of((channels, TILE))
+def grouped(pick, shape):
+    lane = lane_of(shape)
     j_high, k_high = lane % 64 >= 32, lane % 8 >= 4
-    parts[row : row + channels, :TILE] = pick(0, 0)
-    parts[row : row + channels, TILE:] = jnp.where(j_high, pick(-1, 0), pick(1, 0))
-    row = rows + row
-    parts[row : row + channels, :TILE] = jnp.where(k_high, pick(0, -1), pick(0, 1))
-    parts[row : row + channels, TILE:] = jnp.where(
-        j_high,
-        jnp.where(k_high, pick(-1, -1), pick(-1, 1)),
-        jnp.where(k_high, pick(1, -1), pick(1, 1)),
-    )
+    return (
+        pick(0, 0),
+        jnp.where(j_high, pick(-1, 0), pick(1, 0)),
+        jnp.where(k_high, pick(0, -1), pick(0, 1)),
+        jnp.where(
+            j_high,
+            jnp.where(k_high, pick(-1, -1), pick(-1, 1)),
+            jnp.where(k_high, pick(1, -1), pick(1, 1)),
+        ),
+    )
+
+
+def group_at(parts, row, channels, g):
+    row = parts.shape[0] // 2 * (g // 2) + row
+    return slice(row, row + channels), slice(g % 2 * TILE, (g % 2 + 1) * TILE)
+
+
+def set_groups(parts, row, channels, pick):
+    for g, tile in enumerate(grouped(pick, (channels, TILE))):
+        parts[group_at(parts, row, channels, g)] = tile
 
 
 def index_of(near, b, a, c, e, start, none):
@@ -91,7 +101,7 @@
         here = {s: index_of(near, b, 0, *s, base, bricks) for s in SIDES}
         for q in range(TILES):
             set_groups(
-                parts, (b * TILES + q) * channels, lambda c, e: own[here[c, e], :, q * TILE : (q + 1) * TILE]
+                parts, (b * TILES + q) * channels, channels, lambda c, e: own[here[c, e], :, q * TILE : (q + 1) * TILE]
             )
 
 
@@ -115,7 +125,29 @@
 
     for b in range(bricks):
         at = {s: place(b, *s) for s in SIDES}
-        set_groups(parts, b * channels, lambda c, e: table[at[c, e]])
+        set_groups(parts, b * channels, channels, lambda c, e: table[at[c, e]])
+
+
+def prepare_ends(near, up, mine, table, local, weights):
+    bricks, channels = mine.shape[0], mine.shape[1]
+    for b in range(bricks):
+        table[b] = mine[b]
+    table[bricks] = jnp.zeros((channels, TILE), jnp.bfloat16)
+    start = (lax.axis_index("space") - 1 + up) * bricks
+    for b in range(bricks):
+        own, other = {}, {}
+        for c, e in SIDES:
+            number = near[0, b, 18 * up + 3 * (c + 1) + e + 1]
+            at = number - start
+            at_own, at_other = at - bricks * (1 - up), at - bricks * up
+            inside = (number >= 0) & (at_own >= 0) & (at_own < bricks)
+            own[c, e] = jnp.where(inside, at_own, bricks)
+            other[c, e] = jnp.where(number >= 0, at_other, -1)
+        set_groups(local, b * channels, channels, lambda c, e: table[own[c, e]])
+        for n in range(bricks):
+            flags = grouped(lambda c, e: jnp.where(other[c, e] == n, 1.0, 0.0), weights.shape[3:])
+            for g in range(4):
+                weights[b, g, n] = jnp.broadcast_to(flags[g], weights.shape[3:]).astype(jnp.bfloat16)
 
 
 def faces_kernel(features, cotangent, mask, near, one, two, own_x, own_g, present, near_out, *rest):
@@ -145,9 +177,12 @@
     copies[3].wait()
 
 
-def inner_kernel(scale, near, own, gradient, shifted, grad, select_y, select_z, parts, middle, placed):
+def inner_kernel(
+    scale, near, own, gradient, mine, shifted, grad, select_y, select_z, local, weights, parts, middle, placed, table
+):
     rows, bricks, channels = grad.shape[0], own.shape[0] - 1, own.shape[1]
     set_selection(select_y, select_z)
+    prepare_ends(near, on_odd(), mine, table, local, weights)
     inner_parts(near, own, parts)
     lower = lane_of((channels, TILE)) < 64
     zero = jnp.zeros((channels, TILE), jnp.float32)
@@ -178,11 +213,17 @@
 
 
 def outer_kernel(
-    scale, near, mine, facing, other, inner, select_y, select_z, shifted, grad, table, parts, middle
+    scale, facing, other, local, weights, inner, select_y, select_z, shifted, grad, parts, middle
 ):
-    bricks, channels = mine.shape[0], mine.shape[1]
+    bricks, channels = other.shape[0], other.shape[1]
     odd = on_odd()
-    set_ends(near, odd, mine, other, table, parts)
+    for b in range(bricks):
+        for g in range(4):
+            at = group_at(parts, b * channels, channels, g)
+            tile = local[at]
+            for n in range(bricks):
+                tile = tile + jnp.concatenate([weights[b, g, n]] * (channels // 16), axis=0) * other[n]
+            parts[at] = tile
     shift_all(parts, select_y, select_z, middle, shifted, 1)
     x_half = lane_of((channels, TILE)) // 64 == odd
     contract = (((1,), (1,)), ((), ()))
@@ -399,19 +440,19 @@
     got_two = lax.ppermute(two, AXES, [(b, a) for a, b in forth])
     volume, grads = shape(bricks, 9 * channels, 512), shape(rows, 2 * channels, dtype=jnp.float32)
     shifted = shape(bricks, 9 * channels, TILE)
-    inner_x, grad, *select = call(
+    inner_x, grad, *select, near_ends, weights = call(
         functools.partial(inner_kernel, scale),
-        [volume, grads, chosen, chosen],
-        (near, own_x, own_g),
-        [SMEM, VMEM, VMEM],
-        [*parts, scratch(bricks, 3 * channels, 512)],
+        [volume, grads, chosen, chosen, shape(2 * few, 2 * TILE), shape(bricks, 4, bricks, 16, TILE)],
+        (near, own_x, own_g, one),
+        [SMEM] + [VMEM] * 3,
+        [*parts, scratch(bricks, 3 * channels, 512), scratch(bricks + 1, channels, TILE)],
     )
     ends_one, grad = call(
         functools.partial(outer_kernel, scale),
         [shifted, grads],
-        (near, one, two, got_one, grad, *select),
-        [SMEM] + [VMEM] * 6,
-        ends,
+        (two, got_one, near_ends, weights, grad, *select),
+        [VMEM] * 7,
+        ends[1:],
     )
     table = shape(3 * channels, 9 * channels)
     table_y, table_g = call(tables_kernel, [table, table], (weight,), [VMEM], [])

time: 43.4 us -> 42.8 us (0.986)
  Pallas kernels: 11.9 us -> 11.4 us
    pallas_call x7, Pallas kernels: 10 us -> 9.53 us  [call(): pl.pallas_call(kernel, out_shape=shapes, in_specs=specs, out_specs=VMEM i...]
  transfers between devices with their start and end apart: 16 -> 16, of which waited for: 10 -> 10; matrix products, arithmetic and copies ran while one was open for 0% -> 0% of each run, Pallas kernels for 19% -> 20%
where the time goes in v6:
time: 42.8 us; the launch traced here: 42.6 us
  starting transfers between devices  16.4 us (38%)
  waiting for transfers between devices  13.9 us (32%)
  Pallas kernels  11.4 us (27%)
  between operations  0.82 us (2%)
    ppermute x14, starting transfers between devices, exchange(): return lax.ppermute(x, AXES, [(i, i ^ bit) for i in range(count)])  12.8 us
    ppermute x14, waiting for transfers between devices, exchange(): return lax.ppermute(x, AXES, [(i, i ^ bit) for i in range(count)])  12.4 us
    pallas_call x7, Pallas kernels, call(): pl.pallas_call(kernel, out_shape=shapes, in_specs=specs, out_specs=VMEM i...  9.53 us
    ppermute x1, starting transfers between devices, program(): got_one = lax.ppermute(one, AXES, forth)  3.05 us
    pallas_call x2, Pallas kernels, unpack(): pl.pallas_call(functools.partial(unpack_kernel, groups, own), out_shape=t...  1.9 us
    ppermute x1, waiting for transfers between devices, program(): got_two = lax.ppermute(two, AXES, [(b, a) for a, b in forth])  1.48 us
  transfers between devices with their start and end apart: 16, of which 10 were waited for; matrix products, arithmetic and copies ran while one was open for 0% of the time, Pallas kernels for 20%

profile of v6, /device:TPU:0, one launch (start us, length us, event | category | flops | bytes accessed | tf_op | source)
XLA Modules:
  0.0 42.6 jit_solution(8974037095800619781)
XLA Ops:
  0.6 1.1 %shard_map.76 = (bf16[2,64,128]{2,1,0:T(8,128)(2,1)S(1)}, bf16[2,64,128]{2,1,0:T(8,128)(2,1)S(1)}, bf16[3,64,512]{2,1,0:T(8,128)(2,1)S(1)}, bf16[3,64,512]{2,1,0...) custom-call(bf16[1,2,64,512]{3,2,1,0:T(8,128)(2,1)} %features.1, bf16[1,2,64,512]{3,2,1,0:T(8,128)(2,1)} %cotangent.1, ...), custom_call_target="tpu_custom_call" | custom-call | flops 100000000 | bytes 1000000 | tf_op jit(solution)/shard_map/pallas_call | solution.py:401
  1.8 3.1 %collective-permute-start.1 = (bf16[2,64,128]{2,1,0:T(8,128)(2,1)S(1)}, bf16[2,64,128]{2,1,0:T(8,128)(2,1)S(1)}, u32[]{:S(2)}, u32[]{:S(2)}) collective-permute-start(bf16[2,64,128]{2,1,0:T(8,128)(2,1)S(1)} %get-tuple-element.26.mine), channel_id=1, source_target_pairs={{0,4},{4,8},{8,12},{12,16},{16,20},{20,24},{24,28},{28,29},{29,25}... | collective-permute-start | bytes 98312 | tf_op jit(solution)/shard_map/ppermute | solution.py:439
  4.8 2.0 %shard_map.78 = (bf16[2,576,512]{2,1,0:T(8,128)(2,1)S(1)}, f32[896,128]{1,0:T(8,128)S(1)}, bf16[256,384]{1,0:T(8,128)(2,1)S(1)}, bf16[256,384]{1,0:T(8,128)(2,1)...) custom-call(s32[1,2,27]{2,1,0:T(2,128)S(1)} %get-tuple-element.21.near, ...), custom_call_target="tpu_custom_call" | custom-call | flops 100000000 | bytes 1000000 | tf_op jit(solution)/shard_map/pallas_call | solution.py:401
  6.8 0.9 %shard_map.79 = (bf16[2,576,128]{2,1,0:T(8,128)(2,1)S(1)}, f32[896,128]{1,0:T(8,128)S(1)}) custom-call(bf16[2,64,128]{2,1,0:T(8,128)(2,1)S(1)} %get-tuple-element.22.facing.mine, bf16[2,64,128]{2,1,0:T(8,128)(2,1)S(1)} %collective-permute-done.1.other, bf16[256,256]{1,0:T(8,128)(2,1)S(1)} %get-tuple-element.28.local, ...), custom_call_target="tpu_custom_call" | custom-call | flops 100000000 | bytes 1000000 | tf_op jit(solution)/shard_map/pallas_call | solution.py:401
  7.9 1.4 %collective-permute-done.2 = f32[448,128]{1,0:T(8,128)S(1)} collective-permute-done((f32[448,128]{1,0:T(8,128)S(1)}, f32[448,128]{1,0:T(8,128)S(1)}, u32[]{:S(2)}, u32[]{:S(2)}) %collective-permute-start.2) | collective-permute-done | bytes 229408 | tf_op jit(solution)/shard_map/ppermute | solution.py:354
  9.3 3.0 %collective-permute-start.5 = (f32[112,128]{1,0:T(8,128)S(1)}, f32[112,128]{1,0:T(8,128)S(1)}, u32[]{:S(2)}, u32[]{:S(2)}) collective-permute-start(f32[112,128]{1,0:T(8,128)S(1)} %get-tuple-element.40), channel_id=1, source_target_pairs={{0,6},{1,7},{2,4},{3,5},{4,2},{5,3},{6,0},{7,1},{8,14},{9,15},{10,... | collective-permute-start | bytes 172040 | tf_op jit(solution)/shard_map/ppermute | solution.py:354
  12.4 0.6 %collective-permute-start.3 = (f32[112,128]{1,0:T(8,128)S(1)}, f32[112,128]{1,0:T(8,128)S(1)}, u32[]{:S(2)}, u32[]{:S(2)}) collective-permute-start(f32[112,128]{1,0:T(8,128)S(1)} %get-tuple-element.39), channel_id=1, source_target_pairs={{0,2},{1,3},{2,0},{3,1},{4,6},{5,7},{6,4},{7,5},{8,10},{9,11},{10,... | collective-permute-start | bytes 172040 | tf_op jit(solution)/shard_map/ppermute | solution.py:354
  13.0 1.6 %collective-permute-done.5 = f32[112,128]{1,0:T(8,128)S(1)} collective-permute-done((f32[112,128]{1,0:T(8,128)S(1)}, f32[112,128]{1,0:T(8,128)S(1)}, u32[]{:S(2)}, u32[]{:S(2)}) %collective-permute-start.5) | collective-permute-done | bytes 57376 | tf_op jit(solution)/shard_map/ppermute | solution.py:354
  14.6 2.0 %collective-permute-done.4 = f32[112,128]{1,0:T(8,128)S(1)} collective-permute-done((f32[112,128]{1,0:T(8,128)S(1)}, f32[112,128]{1,0:T(8,128)S(1)}, u32[]{:S(2)}, u32[]{:S(2)}) %collective-permute-start.4) | collective-permute-done | bytes 57376 | tf_op jit(solution)/shard_map/ppermute | solution.py:354
  16.6 3.9 %collective-permute-start.7 = (f32[112,128]{1,0:T(8,128)S(1)}, f32[112,128]{1,0:T(8,128)S(1)}, u32[]{:S(2)}, u32[]{:S(2)}) collective-permute-start(f32[112,128]{1,0:T(8,128)S(1)} %add_add_fusion.1), channel_id=1, source_target_pairs={{0,16},{1,17},{2,18},{3,19},{4,20},{5,21},{6,22},{7,23},{8,24},{9,... | collective-permute-start | bytes 172040 | tf_op jit(solution)/shard_map/ppermute | solution.py:354
  20.5 1.3 %collective-permute-start.8 = (f32[112,128]{1,0:T(8,128)S(1)}, f32[112,128]{1,0:T(8,128)S(1)}, u32[]{:S(2)}, u32[]{:S(2)}) collective-permute-start(f32[112,128]{1,0:T(8,128)S(1)} %add_add_fusion.1), channel_id=1, source_target_pairs={{0,24},{1,25},{2,26},{3,27},{4,28},{5,29},{6,30},{7,31},{8,16},{9,... | collective-permute-start | bytes 172040 | tf_op jit(solution)/shard_map/ppermute | solution.py:354
  22.1 0.6 %collective-permute-done.7 = f32[112,128]{1,0:T(8,128)S(1)} collective-permute-done((f32[112,128]{1,0:T(8,128)S(1)}, f32[112,128]{1,0:T(8,128)S(1)}, u32[]{:S(2)}, u32[]{:S(2)}) %collective-permute-start.7) | collective-permute-done | bytes 57376 | tf_op jit(solution)/shard_map/ppermute | solution.py:354
  22.7 3.9 %collective-permute-done.8 = f32[112,128]{1,0:T(8,128)S(1)} collective-permute-done((f32[112,128]{1,0:T(8,128)S(1)}, f32[112,128]{1,0:T(8,128)S(1)}, u32[]{:S(2)}, u32[]{:S(2)}) %collective-permute-start.8) | collective-permute-done | bytes 57376 | tf_op jit(solution)/shard_map/ppermute | solution.py:354
  26.7 0.6 %collective-permute-start.10 = (f32[112,128]{1,0:T(8,128)S(1)}, f32[112,128]{1,0:T(8,128)S(1)}, u32[]{:S(2)}, u32[]{:S(2)}) collective-permute-start(f32[112,128]{1,0:T(8,128)S(1)} %add_add_fusion.refs_0_), channel_id=1, source_target_pairs={{0,2},{1,3},{2,0},{3,1},{4,6},{5,7},{6,4},{7,5},{8,10},{9,11},{10,... | collective-permute-start | bytes 172040 | tf_op jit(solution)/shard_map/ppermute | solution.py:354
  27.3 0.7 %collective-permute-start.12 = (f32[112,128]{1,0:T(8,128)S(1)}, f32[112,128]{1,0:T(8,128)S(1)}, u32[]{:S(2)}, u32[]{:S(2)}) collective-permute-start(f32[112,128]{1,0:T(8,128)S(1)} %add_add_fusion.refs_0_), channel_id=1, source_target_pairs={{0,4},{1,5},{2,6},{3,7},{4,0},{5,1},{6,2},{7,3},{8,12},{9,13},{10,... | collective-permute-start | bytes 172040 | tf_op jit(solution)/shard_map/ppermute | solution.py:354
  28.0 2.2 %collective-permute-start.14 = (f32[112,128]{1,0:T(8,128)S(1)}, f32[112,128]{1,0:T(8,128)S(1)}, u32[]{:S(2)}, u32[]{:S(2)}) collective-permute-start(f32[112,128]{1,0:T(8,128)S(1)} %add_add_fusion.refs_0_), channel_id=1, source_target_pairs={{0,6},{1,7},{2,4},{3,5},{4,2},{5,3},{6,0},{7,1},{8,14},{9,15},{10,... | collective-permute-start | bytes 172040 | tf_op jit(solution)/shard_map/ppermute | solution.py:354
  30.2 0.7 %collective-permute-done.10.refs_1_ = f32[112,128]{1,0:T(8,128)S(1)} collective-permute-done((f32[112,128]{1,0:T(8,128)S(1)}, f32[112,128]{1,0:T(8,128)S(1)}, u32[]{:S(2)}, u32[]{:S(2)}) %collective-permute-start.10) | collective-permute-done | bytes 57376 | tf_op jit(solution)/shard_map/ppermute | solution.py:354
  31.5 1.6 %collective-permute-done.14.refs_3_ = f32[112,128]{1,0:T(8,128)S(1)} collective-permute-done((f32[112,128]{1,0:T(8,128)S(1)}, f32[112,128]{1,0:T(8,128)S(1)}, u32[]{:S(2)}, u32[]{:S(2)}) %collective-permute-start.14) | collective-permute-done | bytes 57376 | tf_op jit(solution)/shard_map/ppermute | solution.py:354
  33.6 1.5 %shard_map.81.inner = bf16[2,576,512]{2,1,0:T(8,128)(2,1)S(1)} custom-call(s32[1,2,27]{2,1,0:T(2,128)S(1)} %get-tuple-element.21.near, bf16[3,64,512]{2,1,0:T(8,128)(2,1)S(1)} %get-tuple-element.25.gradient.own, bf16[256,384]{1,0:T(8,128)(2,1)S(1)} %get-tuple-element.31.select_y, bf16[256,384]{1,0:T(8,128)(2,1)S(1)} %get-tuple-element.32.select_z), custom_call_target="tpu_custom_call" | custom-call | flops 100000000 | bytes 1000000 | tf_op jit(solution)/shard_map/pallas_call | solution.py:401
  35.5 1.5 %collective-permute-done.other = bf16[2,64,128]{2,1,0:T(8,128)(2,1)S(1)} collective-permute-done((bf16[2,64,128]{2,1,0:T(8,128)(2,1)S(1)}, bf16[2,64,128]{2,1,0:T(8,128)(2,1)S(1)}, u32[]{:S(2)}, u32[]{:S(2)}) %collective-permute-start) | collective-permute-done | bytes 32800 | tf_op jit(solution)/shard_map/ppermute | solution.py:440
  37.0 2.2 %shard_map.80 = (bf16[1,2,64,512]{3,2,1,0:T(8,128)(2,1)}, bf16[2,576,128]{2,1,0:T(8,128)(2,1)S(1)}) custom-call(s32[1,2,27]{2,1,0:T(2,128)S(1)} %get-tuple-element.21.near, bf16[2,64,128]{2,1,0:T(8,128)(2,1)S(1)} %get-tuple-element.22.facing.mine, bf16[2,64,128]{2,1,0:T(8,128)(2,1)S(1)} %collective-permute-done.other, ...), custom_call_target="tpu_custom_call" | custom-call | flops 100000000 | bytes 1000000 | tf_op jit(solution)/shard_map/pallas_call | solution.py:401
  39.2 1.4 %shard_map.82 = bf16[1,2,64,512]{3,2,1,0:T(8,128)(2,1)} custom-call(bf16[192,576]{1,0:T(8,128)(2,1)S(1)} %get-tuple-element.36.table, bf16[2,576,512]{2,1,0:T(8,128)(2,1)S(1)} %shard_map.81.inner, bf16[2,576,128]{2,1,0:T(8,128)(2,1)S(1)} %get-tuple-element.33.ends, bf16[2,576,128]{2,1,0:T(8,128)(2,1)S(1)} %get-tuple-element.37.more_ends, ...), custom_call_target="tpu_custom_call" | custom-call | flops 100000000 | bytes 1000000 | tf_op jit(solution)/shard_map/pallas_call | solution.py:401
  40.7 0.9 %unpack.2.refs_4_ = f32[27,64,64]{2,1,0:T(8,128)} custom-call(f32[112,128]{1,0:T(8,128)S(1)} %add_add_fusion.refs_0_, f32[112,128]{1,0:T(8,128)S(1)} %collective-permute-done.10.refs_1_, f32[112,128]{1,0:T(8,128)S(1)} %collective-permute-done.12.refs_2_, f32[112,128]{1,0:T(8,128)S(1)} %collective-permute-done.14.refs_3_), custom_call_target="tpu_custom_call" | custom-call | flops 1000000 | bytes 1000000 | tf_op jit(solution)/shard_map/unpack/pallas_call | solution.py:474
  41.6 0.9 %unpack.3 = f32[27,64,64]{2,1,0:T(8,128)} custom-call(f32[112,128]{1,0:T(8,128)S(1)} %collective-permute-done.9.refs_0_, f32[112,128]{1,0:T(8,128)S(1)} %collective-permute-done.11.refs_1_, f32[112,128]{1,0:T(8,128)S(1)} %collective-permute-done.13.refs_2_, f32[112,128]{1,0:T(8,128)S(1)} %collective-permute-done.15.refs_3_, ...), custom_call_target="tpu_custom_call", output_to_operand_aliasing={{}: (4, {})} | custom-call | flops 1000000 | bytes 1000000 | tf_op jit(solution)/shard_map/unpack/pallas_call | solution.py:474
  (24 shorter events, 2.0 us)
Async XLA Ops:
  1.8 5.0 %collective-permute-start.1 = (bf16[2,64,128]{2,1,0:T(8,128)(2,1)S(1)}, bf16[2,64,128]{2,1,0:T(8,128)(2,1)S(1)}, u32[]{:S(2)}, u32[]{:S(2)}) collective-permute-start(bf16[2,64,128]{2,1,0:T(8,128)(2,1)S(1)} %get-tuple-element.26.mine), channel_id=1, source_target_pairs={{0,4},{4,8},{8,12},{12,16},{16,20},{20,24},{24,28},{28,29},{29,25}... | collective-permute-start | bytes 98312 | tf_op jit(solution)/shard_map/ppermute | solution.py:439
  7.7 1.6 %collective-permute-start.2 = (f32[448,128]{1,0:T(8,128)S(1)}, f32[448,128]{1,0:T(8,128)S(1)}, u32[]{:S(2)}, u32[]{:S(2)}) collective-permute-start(f32[448,128]{1,0:T(8,128)S(1)} %constant_dynamic-slice_fusion.3), channel_id=1, source_target_pairs={{0,1},{1,0},{2,3},{3,2},{4,5},{5,4},{6,7},{7,6},{8,9},{9,8},{10,11... | collective-permute-start | bytes 688136 | tf_op jit(solution)/shard_map/ppermute | solution.py:354
  9.3 25.7 %copy-start = (bf16[27,64,64]{2,1,0:T(8,128)(2,1)S(1)}, bf16[27,64,64]{2,1,0:T(8,128)(2,1)}, u32[]{:S(2)}) copy-start(bf16[27,64,64]{2,1,0:T(8,128)(2,1)} %weight.1) | copy-start | bytes 663556
  9.3 5.2 %collective-permute-start.5 = (f32[112,128]{1,0:T(8,128)S(1)}, f32[112,128]{1,0:T(8,128)S(1)}, u32[]{:S(2)}, u32[]{:S(2)}) collective-permute-start(f32[112,128]{1,0:T(8,128)S(1)} %get-tuple-element.40), channel_id=1, source_target_pairs={{0,6},{1,7},{2,4},{3,5},{4,2},{5,3},{6,0},{7,1},{8,14},{9,15},{10,... | collective-permute-start | bytes 172040 | tf_op jit(solution)/shard_map/ppermute | solution.py:354
  12.4 4.2 %collective-permute-start.4 = (f32[112,128]{1,0:T(8,128)S(1)}, f32[112,128]{1,0:T(8,128)S(1)}, u32[]{:S(2)}, u32[]{:S(2)}) collective-permute-start(f32[112,128]{1,0:T(8,128)S(1)} %get-tuple-element.41), channel_id=1, source_target_pairs={{0,4},{1,5},{2,6},{3,7},{4,0},{5,1},{6,2},{7,3},{8,12},{9,13},{10,... | collective-permute-start | bytes 172040 | tf_op jit(solution)/shard_map/ppermute | solution.py:354
  12.4 4.2 %collective-permute-start.3 = (f32[112,128]{1,0:T(8,128)S(1)}, f32[112,128]{1,0:T(8,128)S(1)}, u32[]{:S(2)}, u32[]{:S(2)}) collective-permute-start(f32[112,128]{1,0:T(8,128)S(1)} %get-tuple-element.39), channel_id=1, source_target_pairs={{0,2},{1,3},{2,0},{3,1},{4,6},{5,7},{6,4},{7,5},{8,10},{9,11},{10,... | collective-permute-start | bytes 172040 | tf_op jit(solution)/shard_map/ppermute | solution.py:354
  16.6 6.1 %collective-permute-start.7 = (f32[112,128]{1,0:T(8,128)S(1)}, f32[112,128]{1,0:T(8,128)S(1)}, u32[]{:S(2)}, u32[]{:S(2)}) collective-permute-start(f32[112,128]{1,0:T(8,128)S(1)} %add_add_fusion.1), channel_id=1, source_target_pairs={{0,16},{1,17},{2,18},{3,19},{4,20},{5,21},{6,22},{7,23},{8,24},{9,... | collective-permute-start | bytes 172040 | tf_op jit(solution)/shard_map/ppermute | solution.py:354
  20.5 6.1 %collective-permute-start.8 = (f32[112,128]{1,0:T(8,128)S(1)}, f32[112,128]{1,0:T(8,128)S(1)}, u32[]{:S(2)}, u32[]{:S(2)}) collective-permute-start(f32[112,128]{1,0:T(8,128)S(1)} %add_add_fusion.1), channel_id=1, source_target_pairs={{0,24},{1,25},{2,26},{3,27},{4,28},{5,29},{6,30},{7,31},{8,16},{9,... | collective-permute-start | bytes 172040 | tf_op jit(solution)/shard_map/ppermute | solution.py:354
  21.9 4.8 %collective-permute-start.6 = (f32[112,128]{1,0:T(8,128)S(1)}, f32[112,128]{1,0:T(8,128)S(1)}, u32[]{:S(2)}, u32[]{:S(2)}) collective-permute-start(f32[112,128]{1,0:T(8,128)S(1)} %add_add_fusion.1), channel_id=1, source_target_pairs={{0,8},{1,9},{2,10},{3,11},{4,12},{5,13},{6,14},{7,15},{8,0},{9,1},... | collective-permute-start | bytes 172040 | tf_op jit(solution)/shard_map/ppermute | solution.py:354
  26.7 4.2 %collective-permute-start.10 = (f32[112,128]{1,0:T(8,128)S(1)}, f32[112,128]{1,0:T(8,128)S(1)}, u32[]{:S(2)}, u32[]{:S(2)}) collective-permute-start(f32[112,128]{1,0:T(8,128)S(1)} %add_add_fusion.refs_0_), channel_id=1, source_target_pairs={{0,2},{1,3},{2,0},{3,1},{4,6},{5,7},{6,4},{7,5},{8,10},{9,11},{10,... | collective-permute-start | bytes 172040 | tf_op jit(solution)/shard_map/ppermute | solution.py:354
  27.3 4.2 %collective-permute-start.12 = (f32[112,128]{1,0:T(8,128)S(1)}, f32[112,128]{1,0:T(8,128)S(1)}, u32[]{:S(2)}, u32[]{:S(2)}) collective-permute-start(f32[112,128]{1,0:T(8,128)S(1)} %add_add_fusion.refs_0_), channel_id=1, source_target_pairs={{0,4},{1,5},{2,6},{3,7},{4,0},{5,1},{6,2},{7,3},{8,12},{9,13},{10,... | collective-permute-start | bytes 172040 | tf_op jit(solution)/shard_map/ppermute | solution.py:354
  28.0 5.1 %collective-permute-start.14 = (f32[112,128]{1,0:T(8,128)S(1)}, f32[112,128]{1,0:T(8,128)S(1)}, u32[]{:S(2)}, u32[]{:S(2)}) collective-permute-start(f32[112,128]{1,0:T(8,128)S(1)} %add_add_fusion.refs_0_), channel_id=1, source_target_pairs={{0,6},{1,7},{2,4},{3,5},{4,2},{5,3},{6,0},{7,1},{8,14},{9,15},{10,... | collective-permute-start | bytes 172040 | tf_op jit(solution)/shard_map/ppermute | solution.py:354
  30.2 11.4 %collective-permute-start.9 = (f32[112,128]{1,0:T(8,128)S(1)}, f32[112,128]{1,0:T(8,128)S(1)}, u32[]{:S(2)}, u32[]{:S(2)}) collective-permute-start(f32[112,128]{1,0:T(8,128)S(1)} %add_add_fusion.refs_0_), channel_id=1, source_target_pairs={{0,1},{1,0},{2,3},{3,2},{4,5},{5,4},{6,7},{7,6},{8,9},{9,8},{10,11... | collective-permute-start | bytes 172040 | tf_op jit(solution)/shard_map/ppermute | solution.py:354
  30.9 10.7 %collective-permute-start.11 = (f32[112,128]{1,0:T(8,128)S(1)}, f32[112,128]{1,0:T(8,128)S(1)}, u32[]{:S(2)}, u32[]{:S(2)}) collective-permute-start(f32[112,128]{1,0:T(8,128)S(1)} %collective-permute-done.10.refs_1_), channel_id=1, source_target_pairs={{0,1},{1,0},{2,3},{3,2},{4,5},{5,4},{6,7},{7,6},{8,9},{9,8},{10,11... | collective-permute-start | bytes 172040 | tf_op jit(solution)/shard_map/ppermute | solution.py:354
  31.5 10.2 %collective-permute-start.13 = (f32[112,128]{1,0:T(8,128)S(1)}, f32[112,128]{1,0:T(8,128)S(1)}, u32[]{:S(2)}, u32[]{:S(2)}) collective-permute-start(f32[112,128]{1,0:T(8,128)S(1)} %collective-permute-done.12.refs_2_), channel_id=1, source_target_pairs={{0,1},{1,0},{2,3},{3,2},{4,5},{5,4},{6,7},{7,6},{8,9},{9,8},{10,11... | collective-permute-start | bytes 172040 | tf_op jit(solution)/shard_map/ppermute | solution.py:354
  33.1 8.6 %collective-permute-start.15 = (f32[112,128]{1,0:T(8,128)S(1)}, f32[112,128]{1,0:T(8,128)S(1)}, u32[]{:S(2)}, u32[]{:S(2)}) collective-permute-start(f32[112,128]{1,0:T(8,128)S(1)} %collective-permute-done.14.refs_3_), channel_id=1, source_target_pairs={{0,1},{1,0},{2,3},{3,2},{4,5},{5,4},{6,7},{7,6},{8,9},{9,8},{10,11... | collective-permute-start | bytes 172040 | tf_op jit(solution)/shard_map/ppermute | solution.py:354
  33.1 3.9 %collective-permute-start = (bf16[2,64,128]{2,1,0:T(8,128)(2,1)S(1)}, bf16[2,64,128]{2,1,0:T(8,128)(2,1)S(1)}, u32[]{:S(2)}, u32[]{:S(2)}) collective-permute-start(bf16[2,64,128]{2,1,0:T(8,128)(2,1)S(1)} %get-tuple-element.22.facing.mine), channel_id=1, source_target_pairs={{4,0},{8,4},{12,8},{16,12},{20,16},{24,20},{28,24},{29,28},{25,29}... | collective-permute-start | bytes 98312 | tf_op jit(solution)/shard_map/ppermute | solution.py:440

commit v7 on v6

--- a/solution.py
+++ b/solution.py
@@ -212,8 +212,13 @@
         grad[count + half :, :] = jnp.zeros((rows - count - half, 2 * channels), jnp.float32)
 
 
+def device_place():
+    return lax.axis_index("space") * lax.axis_size("scene") + lax.axis_index("scene")
+
+
 def outer_kernel(
-    scale, facing, other, local, weights, inner, select_y, select_z, shifted, grad, parts, middle
+    scale, groups, facing, other, local, weights, inner, select_y, select_z,
+    shifted, send_far, send_rest, keep_far, keep_rest, parts, middle, grad
 ):
     bricks, channels = other.shape[0], other.shape[1]
     odd = on_odd()
@@ -239,6 +244,15 @@
         term = jnp.concatenate([jnp.where(odd == 1, two, one), jnp.where(odd == 1, one, two)], axis=1)
         grad[at, :] = inner[at, :] + term * scale
     grad[9 * channels :, :] = inner[9 * channels :, :]
+    place = device_place()
+    size = send_far.shape[0]
+    for side, far, rest in ((1 - place % 2, send_far, send_rest), (place % 2, keep_far, keep_rest)):
+        for k in range(groups):
+            at = pl.multiple_of((side * groups + jnp.bitwise_xor(place // 2 % groups, k)) * size, 8)
+            if k == groups - 1:
+                far[...] = grad[pl.ds(at, size), :]
+            else:
+                rest[k * size : (k + 1) * size, :] = grad[pl.ds(at, size), :]
 
 
 def shift_kernel(near, own, select_y, select_z, shifted, parts, middle):
@@ -291,7 +305,7 @@
 
 def unpack_kernel(groups, own, *refs):
     parts, (out, whole, blocks, sem) = refs[:groups], refs[-4:]
-    place = lax.axis_index("space") * lax.axis_size("scene") + lax.axis_index("scene")
+    place = device_place()
     where = place // 2 % groups
     size, channels = parts[0].shape[0], blocks.shape[1]
     for k in range(groups):
@@ -300,36 +314,32 @@
     half, count = groups * size, 9 * channels
 
     def write(low, high):
-        runs = []
-
-        def put(tap, lane, row, rows, first):
-            if not runs or runs[-1][0] + runs[-1][2] not in (tap, tap + 1) or (first == 0) != (
-                runs[-1][0] + runs[-1][2] == tap
-            ):
-                runs.append([tap, sum(run[2] for run in runs), 0])
-            if first == 0:
-                runs[-1][2] += 1
-            at = runs[-1][1] + runs[-1][2] - 1
-            blocks[at, first : first + rows, :] = whole[row : row + rows, lane * channels : (lane + 1) * channels]
-
-        taps = range(low // channels, min(high, count) // channels)
+        copies = []
+
+        def send(tap):
+            n = len(copies)
+            copies.append(pltpu.make_async_copy(blocks.at[n], out.at[tap], sem.at[n]))
+            copies[-1].start()
+
         for lane, base in ((0, 0), (1, 18)):
-            for yz in taps:
-                put(base + yz, lane, yz * channels - low, channels, 0)
+            for yz in range(low // channels, min(high, count) // channels):
+                row = yz * channels - low
+                blocks[len(copies)] = whole[row : row + channels, lane * channels : (lane + 1) * channels]
+                send(base + yz)
         if high > count:
             for lane in range(2):
                 done = 0
                 while done < count // 2:
                     at = lane * (count // 2) + done
-                    rows = min(channels - at % channels, count // 2 - done)
-                    put(9 + at // channels, lane, count - low + done, rows, at % channels)
-                    done += rows
-        copies = [
-            pltpu.make_async_copy(blocks.at[start : start + n], out.at[tap : tap + n], sem.at[i])
-            for i, (tap, start, n) in enumerate(runs)
-        ]
-        for copy in copies:
-            copy.start()
+                    first = at % channels
+                    size = min(channels - first, count // 2 - done)
+                    row = count - low + done
+                    blocks[len(copies), first : first + size, :] = whole[
+                        row : row + size, lane * channels : (lane + 1) * channels
+                    ]
+                    if first + size == channels:
+                        send(9 + at // channels)
+                    done += size
         for copy in copies:
             copy.wait()
 
@@ -354,19 +364,15 @@
     return lax.ppermute(x, AXES, [(i, i ^ bit) for i in range(count)])
 
 
-def all_sum(part, groups):
+def all_sum(send_far, send_rest, keep_far, keep_rest, groups):
     count = lax.axis_size("space") * lax.axis_size("scene")
-    place = lax.axis_index("space") * lax.axis_size("scene") + lax.axis_index("scene")
-    odd, where = place % 2, place // 2 % groups
-    half = part.shape[0] // 2
-    size = half // groups
-    keep = lax.dynamic_slice_in_dim(part, odd * half, half, 0)
-    send = lax.dynamic_slice_in_dim(part, (1 - odd) * half, half, 0)
-    mine = keep + exchange(send, 1)
-    own = lax.dynamic_slice_in_dim(mine, where * size, size, 0)
-    got = []
+    size = send_far.shape[0]
+    far = keep_far + exchange(send_far, 1)
+    rest = keep_rest + exchange(send_rest, 1)
+    mine = [rest[k * size : (k + 1) * size] for k in range(groups - 1)] + [far]
+    own, got = mine[0], []
     for k in range(1, groups):
-        got.append(exchange(lax.dynamic_slice_in_dim(mine, (where ^ k) * size, size, 0), 2 * k))
+        got.append(exchange(mine[k], 2 * k))
     for one in got:
         own = own + one
     bit = 2 * groups
@@ -447,12 +453,14 @@
         [SMEM] + [VMEM] * 3,
         [*parts, scratch(bricks, 3 * channels, 512), scratch(bricks + 1, channels, TILE)],
     )
-    ends_one, grad = call(
-        functools.partial(outer_kernel, scale),
-        [shifted, grads],
+    far = shape(rows // 2 // groups, 2 * channels, dtype=jnp.float32)
+    rest = shape(rows // 2 // groups * (groups - 1), 2 * channels, dtype=jnp.float32)
+    ends_one, *halves = call(
+        functools.partial(outer_kernel, scale, groups),
+        [shifted, far, rest, far, rest],
         (two, got_one, near_ends, weights, grad, *select),
         [VMEM] * 7,
-        ends[1:],
+        [*ends[1:], scratch(rows, 2 * channels, dtype=jnp.float32)],
     )
     table = shape(3 * channels, 9 * channels)
     table_y, table_g = call(tables_kernel, [table, table], (weight,), [VMEM], [])
@@ -467,7 +475,7 @@
     out_g = call(
         backward_kernel, shape(*cotangent.shape), (table_g, inner_g, ends_one, ends_two, present), [VMEM] * 5, []
     )
-    mine, theirs = all_sum(grad, groups)
+    mine, theirs = all_sum(*halves, groups)
     taps = shape(27, channels, channels, dtype=jnp.float32)
 
     def unpack(own, parts, *before):
@@ -479,7 +487,7 @@
             scratch_shapes=[
                 scratch(rows // 2, 2 * channels, dtype=jnp.float32),
                 scratch(14, channels, channels, dtype=jnp.float32),
-                pltpu.SemaphoreType.DMA((3,)),
+                pltpu.SemaphoreType.DMA((14,)),
             ],
             input_output_aliases={groups: 0} if before else {},
             compiler_params=pltpu.CompilerParams(vmem_limit_bytes=16 << 20),

time: 42.8 us -> 42.8 us (level)
  waiting for transfers between devices: 13.9 us -> 14.5 us
  starting transfers between devices: 16.4 us -> 15.8 us
    ppermute x14 -> x15, waiting for transfers between devices: 12.4 us -> 13 us  [exchange(): return lax.ppermute(x, AXES, [(i, i ^ bit) for i in range(count)])]
    ppermute x14 -> x15, starting transfers between devices: 12.8 us -> 12.2 us  [exchange(): return lax.ppermute(x, AXES, [(i, i ^ bit) for i in range(count)])]
  transfers between devices with their start and end apart: 16 -> 17, of which waited for: 10 -> 10; matrix products, arithmetic and copies ran while one was open for 0% -> 0% of each run, Pallas kernels for 20% -> 20%
where the time goes in v7:
time: 42.8 us; the launch traced here: 42.6 us
  starting transfers between devices  15.8 us (37%)
  waiting for transfers between devices  14.5 us (34%)
  Pallas kernels  11.5 us (27%)
  between operations  0.76 us (2%)
    ppermute x15, waiting for transfers between devices, exchange(): return lax.ppermute(x, AXES, [(i, i ^ bit) for i in range(count)])  13 us
    ppermute x15, starting transfers between devices, exchange(): return lax.ppermute(x, AXES, [(i, i ^ bit) for i in range(count)])  12.2 us
    pallas_call x7, Pallas kernels, call(): pl.pallas_call(kernel, out_shape=shapes, in_specs=specs, out_specs=VMEM i...  9.62 us
    ppermute x1, starting transfers between devices, program(): got_one = lax.ppermute(one, AXES, forth)  3.05 us
    pallas_call x2, Pallas kernels, unpack(): pl.pallas_call(functools.partial(unpack_kernel, groups, own), out_shape=t...  1.88 us
    ppermute x1, waiting for transfers between devices, program(): got_two = lax.ppermute(two, AXES, [(b, a) for a, b in forth])  1.46 us
  transfers between devices with their start and end apart: 17, of which 10 were waited for; matrix products, arithmetic and copies ran while one was open for 0% of the time, Pallas kernels for 20%

profile of v7, /device:TPU:0, one launch (start us, length us, event | category | flops | bytes accessed | tf_op | source)
XLA Modules:
  0.0 42.6 jit_solution(9860338729710157384)
XLA Ops:
  0.6 1.1 %shard_map.76 = (bf16[2,64,128]{2,1,0:T(8,128)(2,1)S(1)}, bf16[2,64,128]{2,1,0:T(8,128)(2,1)S(1)}, bf16[3,64,512]{2,1,0:T(8,128)(2,1)S(1)}, bf16[3,64,512]{2,1,0...) custom-call(bf16[1,2,64,512]{3,2,1,0:T(8,128)(2,1)} %features.1, bf16[1,2,64,512]{3,2,1,0:T(8,128)(2,1)} %cotangent.1, ...), custom_call_target="tpu_custom_call" | custom-call | flops 100000000 | bytes 1000000 | tf_op jit(solution)/shard_map/pallas_call | solution.py:407
  1.8 3.1 %collective-permute-start.1 = (bf16[2,64,128]{2,1,0:T(8,128)(2,1)S(1)}, bf16[2,64,128]{2,1,0:T(8,128)(2,1)S(1)}, u32[]{:S(2)}, u32[]{:S(2)}) collective-permute-start(bf16[2,64,128]{2,1,0:T(8,128)(2,1)S(1)} %get-tuple-element.29.mine), channel_id=1, source_target_pairs={{0,4},{4,8},{8,12},{12,16},{16,20},{20,24},{24,28},{28,29},{29,25}... | collective-permute-start | bytes 98312 | tf_op jit(solution)/shard_map/ppermute | solution.py:445
  4.8 2.0 %shard_map.78 = (bf16[2,576,512]{2,1,0:T(8,128)(2,1)S(1)}, f32[896,128]{1,0:T(8,128)S(1)}, bf16[256,384]{1,0:T(8,128)(2,1)S(1)}, bf16[256,384]{1,0:T(8,128)(2,1)...) custom-call(s32[1,2,27]{2,1,0:T(2,128)S(1)} %get-tuple-element.24.near, ...), custom_call_target="tpu_custom_call" | custom-call | flops 100000000 | bytes 1000000 | tf_op jit(solution)/shard_map/pallas_call | solution.py:407
  6.8 0.9 %shard_map.79 = (bf16[2,576,128]{2,1,0:T(8,128)(2,1)S(1)}, f32[112,128]{1,0:T(8,128)S(1)}, f32[336,128]{1,0:T(8,128)S(1)}, f32[112,128]{1,0:T(8,128)S(1)}, f32[336,128]{1,0:T(8,128)S(1)}) custom-call(bf16[2,64,128]{2,1,0:T(8,128)(2,1)S(1)} %get-tuple-element.25.facing.mine, bf16[2,64,128]{2,1,0:T(8,128)(2,1)S(1)} %collective-permute-done.1.other, ...), custom_call_target="tpu_custom_call" | custom-call | flops 100000000 | bytes 1000000 | tf_op jit(solution)/shard_map/pallas_call | solution.py:407
  8.3 1.0 %collective-permute-done.5 = f32[112,128]{1,0:T(8,128)S(1)} collective-permute-done((f32[112,128]{1,0:T(8,128)S(1)}, f32[112,128]{1,0:T(8,128)S(1)}, u32[]{:S(2)}, u32[]{:S(2)}) %collective-permute-start.5) | collective-permute-done | bytes 57376 | tf_op jit(solution)/shard_map/ppermute | solution.py:364
  9.3 3.0 %collective-permute-start.6 = (f32[112,128]{1,0:T(8,128)S(1)}, f32[112,128]{1,0:T(8,128)S(1)}, u32[]{:S(2)}, u32[]{:S(2)}) collective-permute-start(f32[112,128]{1,0:T(8,128)S(1)} %add.27), channel_id=1, source_target_pairs={{0,6},{1,7},{2,4},{3,5},{4,2},{5,3},{6,0},{7,1},{8,14},{9,15},{10,... | collective-permute-start | bytes 172040 | tf_op jit(solution)/shard_map/ppermute | solution.py:364
  12.4 0.6 %collective-permute-start.3 = (f32[112,128]{1,0:T(8,128)S(1)}, f32[112,128]{1,0:T(8,128)S(1)}, u32[]{:S(2)}, u32[]{:S(2)}) collective-permute-start(f32[112,128]{1,0:T(8,128)S(1)} %get-tuple-element.45), channel_id=1, source_target_pairs={{0,2},{1,3},{2,0},{3,1},{4,6},{5,7},{6,4},{7,5},{8,10},{9,11},{10,... | collective-permute-start | bytes 172040 | tf_op jit(solution)/shard_map/ppermute | solution.py:364
  13.0 1.8 %collective-permute-done.6 = f32[112,128]{1,0:T(8,128)S(1)} collective-permute-done((f32[112,128]{1,0:T(8,128)S(1)}, f32[112,128]{1,0:T(8,128)S(1)}, u32[]{:S(2)}, u32[]{:S(2)}) %collective-permute-start.6) | collective-permute-done | bytes 57376 | tf_op jit(solution)/shard_map/ppermute | solution.py:364
  14.8 1.8 %collective-permute-done.3 = f32[112,128]{1,0:T(8,128)S(1)} collective-permute-done((f32[112,128]{1,0:T(8,128)S(1)}, f32[112,128]{1,0:T(8,128)S(1)}, u32[]{:S(2)}, u32[]{:S(2)}) %collective-permute-start.3) | collective-permute-done | bytes 57376 | tf_op jit(solution)/shard_map/ppermute | solution.py:364
  17.2 3.5 %collective-permute-start.9 = (f32[112,128]{1,0:T(8,128)S(1)}, f32[112,128]{1,0:T(8,128)S(1)}, u32[]{:S(2)}, u32[]{:S(2)}) collective-permute-start(f32[112,128]{1,0:T(8,128)S(1)} %fusion.1), channel_id=1, source_target_pairs={{0,24},{1,25},{2,26},{3,27},{4,28},{5,29},{6,30},{7,31},{8,16},{9,... | collective-permute-start | bytes 172040 | tf_op jit(solution)/shard_map/ppermute | solution.py:364
  20.7 0.9 %collective-permute-start.7 = (f32[112,128]{1,0:T(8,128)S(1)}, f32[112,128]{1,0:T(8,128)S(1)}, u32[]{:S(2)}, u32[]{:S(2)}) collective-permute-start(f32[112,128]{1,0:T(8,128)S(1)} %fusion.1), channel_id=1, source_target_pairs={{0,8},{1,9},{2,10},{3,11},{4,12},{5,13},{6,14},{7,15},{8,0},{9,1},... | collective-permute-start | bytes 172040 | tf_op jit(solution)/shard_map/ppermute | solution.py:364
  21.6 2.1 %collective-permute-done.9 = f32[112,128]{1,0:T(8,128)S(1)} collective-permute-done((f32[112,128]{1,0:T(8,128)S(1)}, f32[112,128]{1,0:T(8,128)S(1)}, u32[]{:S(2)}, u32[]{:S(2)}) %collective-permute-start.9) | collective-permute-done | bytes 57376 | tf_op jit(solution)/shard_map/ppermute | solution.py:364
  23.7 2.1 %collective-permute-done.8 = f32[112,128]{1,0:T(8,128)S(1)} collective-permute-done((f32[112,128]{1,0:T(8,128)S(1)}, f32[112,128]{1,0:T(8,128)S(1)}, u32[]{:S(2)}, u32[]{:S(2)}) %collective-permute-start.8) | collective-permute-done | bytes 57376 | tf_op jit(solution)/shard_map/ppermute | solution.py:364
  25.9 2.5 %collective-permute-start.15 = (f32[112,128]{1,0:T(8,128)S(1)}, f32[112,128]{1,0:T(8,128)S(1)}, u32[]{:S(2)}, u32[]{:S(2)}) collective-permute-start(f32[112,128]{1,0:T(8,128)S(1)} %add_add_fusion.refs_0_), channel_id=1, source_target_pairs={{0,6},{1,7},{2,4},{3,5},{4,2},{5,3},{6,0},{7,1},{8,14},{9,15},{10,... | collective-permute-start | bytes 172040 | tf_op jit(solution)/shard_map/ppermute | solution.py:364
  28.3 0.6 %collective-permute-start.13 = (f32[112,128]{1,0:T(8,128)S(1)}, f32[112,128]{1,0:T(8,128)S(1)}, u32[]{:S(2)}, u32[]{:S(2)}) collective-permute-start(f32[112,128]{1,0:T(8,128)S(1)} %add_add_fusion.refs_0_), channel_id=1, source_target_pairs={{0,4},{1,5},{2,6},{3,7},{4,0},{5,1},{6,2},{7,3},{8,12},{9,13},{10,... | collective-permute-start | bytes 172040 | tf_op jit(solution)/shard_map/ppermute | solution.py:364
  29.4 1.7 %collective-permute-done.15.refs_3_ = f32[112,128]{1,0:T(8,128)S(1)} collective-permute-done((f32[112,128]{1,0:T(8,128)S(1)}, f32[112,128]{1,0:T(8,128)S(1)}, u32[]{:S(2)}, u32[]{:S(2)}) %collective-permute-start.15) | collective-permute-done | bytes 57376 | tf_op jit(solution)/shard_map/ppermute | solution.py:364
  31.1 1.4 %collective-permute-done.13.refs_2_ = f32[112,128]{1,0:T(8,128)S(1)} collective-permute-done((f32[112,128]{1,0:T(8,128)S(1)}, f32[112,128]{1,0:T(8,128)S(1)}, u32[]{:S(2)}, u32[]{:S(2)}) %collective-permute-start.13) | collective-permute-done | bytes 57376 | tf_op jit(solution)/shard_map/ppermute | solution.py:364
  32.5 0.6 %collective-permute-done.11.refs_1_ = f32[112,128]{1,0:T(8,128)S(1)} collective-permute-done((f32[112,128]{1,0:T(8,128)S(1)}, f32[112,128]{1,0:T(8,128)S(1)}, u32[]{:S(2)}, u32[]{:S(2)}) %collective-permute-start.11) | collective-permute-done | bytes 57376 | tf_op jit(solution)/shard_map/ppermute | solution.py:364
  33.6 1.5 %shard_map.81.inner = bf16[2,576,512]{2,1,0:T(8,128)(2,1)S(1)} custom-call(s32[1,2,27]{2,1,0:T(2,128)S(1)} %get-tuple-element.24.near, bf16[3,64,512]{2,1,0:T(8,128)(2,1)S(1)} %get-tuple-element.28.gradient.own, bf16[256,384]{1,0:T(8,128)(2,1)S(1)} %get-tuple-element.34.select_y, bf16[256,384]{1,0:T(8,128)(2,1)S(1)} %get-tuple-element.35.select_z), custom_call_target="tpu_custom_call" | custom-call | flops 100000000 | bytes 1000000 | tf_op jit(solution)/shard_map/pallas_call | solution.py:407
  35.6 1.5 %collective-permute-done.other = bf16[2,64,128]{2,1,0:T(8,128)(2,1)S(1)} collective-permute-done((bf16[2,64,128]{2,1,0:T(8,128)(2,1)S(1)}, bf16[2,64,128]{2,1,0:T(8,128)(2,1)S(1)}, u32[]{:S(2)}, u32[]{:S(2)}) %collective-permute-start) | collective-permute-done | bytes 32800 | tf_op jit(solution)/shard_map/ppermute | solution.py:446
  37.0 2.2 %shard_map.80 = (bf16[1,2,64,512]{3,2,1,0:T(8,128)(2,1)}, bf16[2,576,128]{2,1,0:T(8,128)(2,1)S(1)}) custom-call(s32[1,2,27]{2,1,0:T(2,128)S(1)} %get-tuple-element.24.near, bf16[2,64,128]{2,1,0:T(8,128)(2,1)S(1)} %get-tuple-element.25.facing.mine, bf16[2,64,128]{2,1,0:T(8,128)(2,1)S(1)} %collective-permute-done.other, ...), custom_call_target="tpu_custom_call" | custom-call | flops 100000000 | bytes 1000000 | tf_op jit(solution)/shard_map/pallas_call | solution.py:407
  39.3 1.4 %shard_map.82 = bf16[1,2,64,512]{3,2,1,0:T(8,128)(2,1)} custom-call(bf16[192,576]{1,0:T(8,128)(2,1)S(1)} %get-tuple-element.39.table, bf16[2,576,512]{2,1,0:T(8,128)(2,1)S(1)} %shard_map.81.inner, bf16[2,576,128]{2,1,0:T(8,128)(2,1)S(1)} %get-tuple-element.36.ends, bf16[2,576,128]{2,1,0:T(8,128)(2,1)S(1)} %get-tuple-element.40.more_ends, ...), custom_call_target="tpu_custom_call" | custom-call | flops 100000000 | bytes 1000000 | tf_op jit(solution)/shard_map/pallas_call | solution.py:407
  40.7 0.9 %unpack.2.refs_4_ = f32[27,64,64]{2,1,0:T(8,128)} custom-call(f32[112,128]{1,0:T(8,128)S(1)} %add_add_fusion.refs_0_, f32[112,128]{1,0:T(8,128)S(1)} %collective-permute-done.11.refs_1_, f32[112,128]{1,0:T(8,128)S(1)} %collective-permute-done.13.refs_2_, f32[112,128]{1,0:T(8,128)S(1)} %collective-permute-done.15.refs_3_), custom_call_target="tpu_custom_call" | custom-call | flops 1000000 | bytes 1000000 | tf_op jit(solution)/shard_map/unpack/pallas_call | solution.py:482
  41.6 1.0 %unpack.3 = f32[27,64,64]{2,1,0:T(8,128)} custom-call(f32[112,128]{1,0:T(8,128)S(1)} %collective-permute-done.10.refs_0_, f32[112,128]{1,0:T(8,128)S(1)} %collective-permute-done.12.refs_1_, f32[112,128]{1,0:T(8,128)S(1)} %collective-permute-done.14.refs_2_, f32[112,128]{1,0:T(8,128)S(1)} %collective-permute-done.16.refs_3_, ...), custom_call_target="tpu_custom_call", output_to_operand_aliasing={{}: (4, {})} | custom-call | flops 1000000 | bytes 1000000 | tf_op jit(solution)/shard_map/unpack/pallas_call | solution.py:482
  (26 shorter events, 2.7 us)
Async XLA Ops:
  1.8 5.1 %collective-permute-start.1 = (bf16[2,64,128]{2,1,0:T(8,128)(2,1)S(1)}, bf16[2,64,128]{2,1,0:T(8,128)(2,1)S(1)}, u32[]{:S(2)}, u32[]{:S(2)}) collective-permute-start(bf16[2,64,128]{2,1,0:T(8,128)(2,1)S(1)} %get-tuple-element.29.mine), channel_id=1, source_target_pairs={{0,4},{4,8},{8,12},{12,16},{16,20},{20,24},{24,28},{28,29},{29,25}... | collective-permute-start | bytes 98312 | tf_op jit(solution)/shard_map/ppermute | solution.py:445
  7.7 4.6 %collective-permute-start.2 = (f32[336,128]{1,0:T(8,128)S(1)}, f32[336,128]{1,0:T(8,128)S(1)}, u32[]{:S(2)}, u32[]{:S(2)}) collective-permute-start(f32[336,128]{1,0:T(8,128)S(1)} %get-tuple-element.42), channel_id=1, source_target_pairs={{0,1},{1,0},{2,3},{3,2},{4,5},{5,4},{6,7},{7,6},{8,9},{9,8},{10,11... | collective-permute-start | bytes 516104 | tf_op jit(solution)/shard_map/ppermute | solution.py:364
  7.8 1.5 %collective-permute-start.5 = (f32[112,128]{1,0:T(8,128)S(1)}, f32[112,128]{1,0:T(8,128)S(1)}, u32[]{:S(2)}, u32[]{:S(2)}) collective-permute-start(f32[112,128]{1,0:T(8,128)S(1)} %get-tuple-element.44), channel_id=1, source_target_pairs={{0,1},{1,0},{2,3},{3,2},{4,5},{5,4},{6,7},{7,6},{8,9},{9,8},{10,11... | collective-permute-start | bytes 172040 | tf_op jit(solution)/shard_map/ppermute | solution.py:364
  9.3 5.5 %collective-permute-start.6 = (f32[112,128]{1,0:T(8,128)S(1)}, f32[112,128]{1,0:T(8,128)S(1)}, u32[]{:S(2)}, u32[]{:S(2)}) collective-permute-start(f32[112,128]{1,0:T(8,128)S(1)} %add.27), channel_id=1, source_target_pairs={{0,6},{1,7},{2,4},{3,5},{4,2},{5,3},{6,0},{7,1},{8,14},{9,15},{10,... | collective-permute-start | bytes 172040 | tf_op jit(solution)/shard_map/ppermute | solution.py:364
  12.4 22.8 %copy-start = (bf16[27,64,64]{2,1,0:T(8,128)(2,1)S(1)}, bf16[27,64,64]{2,1,0:T(8,128)(2,1)}, u32[]{:S(2)}) copy-start(bf16[27,64,64]{2,1,0:T(8,128)(2,1)} %weight.1) | copy-start | bytes 663556
  12.4 4.2 %collective-permute-start.3 = (f32[112,128]{1,0:T(8,128)S(1)}, f32[112,128]{1,0:T(8,128)S(1)}, u32[]{:S(2)}, u32[]{:S(2)}) collective-permute-start(f32[112,128]{1,0:T(8,128)S(1)} %get-tuple-element.45), channel_id=1, source_target_pairs={{0,2},{1,3},{2,0},{3,1},{4,6},{5,7},{6,4},{7,5},{8,10},{9,11},{10,... | collective-permute-start | bytes 172040 | tf_op jit(solution)/shard_map/ppermute | solution.py:364
  13.0 4.2 %collective-permute-start.4 = (f32[112,128]{1,0:T(8,128)S(1)}, f32[112,128]{1,0:T(8,128)S(1)}, u32[]{:S(2)}, u32[]{:S(2)}) collective-permute-start(f32[112,128]{1,0:T(8,128)S(1)} %get-tuple-element.46), channel_id=1, source_target_pairs={{0,4},{1,5},{2,6},{3,7},{4,0},{5,1},{6,2},{7,3},{8,12},{9,13},{10,... | collective-permute-start | bytes 172040 | tf_op jit(solution)/shard_map/ppermute | solution.py:364
  17.2 6.5 %collective-permute-start.9 = (f32[112,128]{1,0:T(8,128)S(1)}, f32[112,128]{1,0:T(8,128)S(1)}, u32[]{:S(2)}, u32[]{:S(2)}) collective-permute-start(f32[112,128]{1,0:T(8,128)S(1)} %fusion.1), channel_id=1, source_target_pairs={{0,24},{1,25},{2,26},{3,27},{4,28},{5,29},{6,30},{7,31},{8,16},{9,... | collective-permute-start | bytes 172040 | tf_op jit(solution)/shard_map/ppermute | solution.py:364
  20.7 5.1 %collective-permute-start.8 = (f32[112,128]{1,0:T(8,128)S(1)}, f32[112,128]{1,0:T(8,128)S(1)}, u32[]{:S(2)}, u32[]{:S(2)}) collective-permute-start(f32[112,128]{1,0:T(8,128)S(1)} %fusion.1), channel_id=1, source_target_pairs={{0,16},{1,17},{2,18},{3,19},{4,20},{5,21},{6,22},{7,23},{8,24},{9,... | collective-permute-start | bytes 172040 | tf_op jit(solution)/shard_map/ppermute | solution.py:364
  20.7 5.1 %collective-permute-start.7 = (f32[112,128]{1,0:T(8,128)S(1)}, f32[112,128]{1,0:T(8,128)S(1)}, u32[]{:S(2)}, u32[]{:S(2)}) collective-permute-start(f32[112,128]{1,0:T(8,128)S(1)} %fusion.1), channel_id=1, source_target_pairs={{0,8},{1,9},{2,10},{3,11},{4,12},{5,13},{6,14},{7,15},{8,0},{9,1},... | collective-permute-start | bytes 172040 | tf_op jit(solution)/shard_map/ppermute | solution.py:364
  25.9 5.3 %collective-permute-start.15 = (f32[112,128]{1,0:T(8,128)S(1)}, f32[112,128]{1,0:T(8,128)S(1)}, u32[]{:S(2)}, u32[]{:S(2)}) collective-permute-start(f32[112,128]{1,0:T(8,128)S(1)} %add_add_fusion.refs_0_), channel_id=1, source_target_pairs={{0,6},{1,7},{2,4},{3,5},{4,2},{5,3},{6,0},{7,1},{8,14},{9,15},{10,... | collective-permute-start | bytes 172040 | tf_op jit(solution)/shard_map/ppermute | solution.py:364
  28.3 4.2 %collective-permute-start.13 = (f32[112,128]{1,0:T(8,128)S(1)}, f32[112,128]{1,0:T(8,128)S(1)}, u32[]{:S(2)}, u32[]{:S(2)}) collective-permute-start(f32[112,128]{1,0:T(8,128)S(1)} %add_add_fusion.refs_0_), channel_id=1, source_target_pairs={{0,4},{1,5},{2,6},{3,7},{4,0},{5,1},{6,2},{7,3},{8,12},{9,13},{10,... | collective-permute-start | bytes 172040 | tf_op jit(solution)/shard_map/ppermute | solution.py:364
  28.9 4.2 %collective-permute-start.11 = (f32[112,128]{1,0:T(8,128)S(1)}, f32[112,128]{1,0:T(8,128)S(1)}, u32[]{:S(2)}, u32[]{:S(2)}) collective-permute-start(f32[112,128]{1,0:T(8,128)S(1)} %add_add_fusion.refs_0_), channel_id=1, source_target_pairs={{0,2},{1,3},{2,0},{3,1},{4,6},{5,7},{6,4},{7,5},{8,10},{9,11},{10,... | collective-permute-start | bytes 172040 | tf_op jit(solution)/shard_map/ppermute | solution.py:364
  29.4 12.2 %collective-permute-start.10 = (f32[112,128]{1,0:T(8,128)S(1)}, f32[112,128]{1,0:T(8,128)S(1)}, u32[]{:S(2)}, u32[]{:S(2)}) collective-permute-start(f32[112,128]{1,0:T(8,128)S(1)} %add_add_fusion.refs_0_), channel_id=1, source_target_pairs={{0,1},{1,0},{2,3},{3,2},{4,5},{5,4},{6,7},{7,6},{8,9},{9,8},{10,11... | collective-permute-start | bytes 172040 | tf_op jit(solution)/shard_map/ppermute | solution.py:364
  31.1 10.5 %collective-permute-start.16 = (f32[112,128]{1,0:T(8,128)S(1)}, f32[112,128]{1,0:T(8,128)S(1)}, u32[]{:S(2)}, u32[]{:S(2)}) collective-permute-start(f32[112,128]{1,0:T(8,128)S(1)} %collective-permute-done.15.refs_3_), channel_id=1, source_target_pairs={{0,1},{1,0},{2,3},{3,2},{4,5},{5,4},{6,7},{7,6},{8,9},{9,8},{10,11... | collective-permute-start | bytes 172040 | tf_op jit(solution)/shard_map/ppermute | solution.py:364
  32.5 9.1 %collective-permute-start.14 = (f32[112,128]{1,0:T(8,128)S(1)}, f32[112,128]{1,0:T(8,128)S(1)}, u32[]{:S(2)}, u32[]{:S(2)}) collective-permute-start(f32[112,128]{1,0:T(8,128)S(1)} %collective-permute-done.13.refs_2_), channel_id=1, source_target_pairs={{0,1},{1,0},{2,3},{3,2},{4,5},{5,4},{6,7},{7,6},{8,9},{9,8},{10,11... | collective-permute-start | bytes 172040 | tf_op jit(solution)/shard_map/ppermute | solution.py:364
  33.1 8.5 %collective-permute-start.12 = (f32[112,128]{1,0:T(8,128)S(1)}, f32[112,128]{1,0:T(8,128)S(1)}, u32[]{:S(2)}, u32[]{:S(2)}) collective-permute-start(f32[112,128]{1,0:T(8,128)S(1)} %collective-permute-done.11.refs_1_), channel_id=1, source_target_pairs={{0,1},{1,0},{2,3},{3,2},{4,5},{5,4},{6,7},{7,6},{8,9},{9,8},{10,11... | collective-permute-start | bytes 172040 | tf_op jit(solution)/shard_map/ppermute | solution.py:364
  33.1 3.9 %collective-permute-start = (bf16[2,64,128]{2,1,0:T(8,128)(2,1)S(1)}, bf16[2,64,128]{2,1,0:T(8,128)(2,1)S(1)}, u32[]{:S(2)}, u32[]{:S(2)}) collective-permute-start(bf16[2,64,128]{2,1,0:T(8,128)(2,1)S(1)} %get-tuple-element.25.facing.mine), channel_id=1, source_target_pairs={{4,0},{8,4},{12,8},{16,12},{20,16},{24,20},{28,24},{29,28},{25,29}... | collective-permute-start | bytes 98312 | tf_op jit(solution)/shard_map/ppermute | solution.py:446

commit v8 on v7

--- a/solution.py
+++ b/solution.py
@@ -126,6 +126,57 @@
     for b in range(bricks):
         at = {s: place(b, *s) for s in SIDES}
         set_groups(parts, b * channels, channels, lambda c, e: table[at[c, e]])
+
+
+def prepare_ends(near, up, mine, table, local, weights):
+    bricks, channels = mine.shape[0], mine.shape[1]
+    for b in range(bricks):
+        table[b] = mine[b]
+    table[bricks] = jnp.zeros((channels, TILE), jnp.bfloat16)
+    start = (lax.axis_index("space") - 1 + up) * bricks
+    for b in range(bricks):
+        own, other = {}, {}
+        for c, e in SIDES:
+            number = near[0, b, 18 * up + 3 * (c + 1) + e + 1]
+            at = number - start
+            at_own, at_other = at - bricks * (1 - up), at - bricks * up
+            inside = (number >= 0) & (at_own >= 0) & (at_own < bricks)
+            own[c, e] = jnp.where(inside, at_own, bricks)
+            other[c, e] = jnp.where(number >= 0, at_other, -1)
+        set_groups(local, b * channels, channels, lambda c, e: table[own[c, e]])
+        for n in range(bricks):
+            flags = grouped(lambda c, e: jnp.where(other[c, e] == n, 1.0, 0.0), weights.shape[3:])
+            for g in range(4):
+                weights[b, g, n] = jnp.broadcast_to(flags[g], weights.shape[3:]).astype(jnp.bfloat16)
+
+
+def faces_kernel(features, cotangent, mask, near, one, two, own_x, own_g, present, near_out, *rest):
+    (mask_here, *arrays), sems = rest[:3], rest[3]
+    bricks, channels = own_x.shape[0] - 1, own_x.shape[1]
+    copies = [pltpu.make_async_copy(mask, mask_here, sems.at[0])]
+    for b in range(bricks):
+        for side, array in enumerate((features, cotangent)):
+            copies.append(pltpu.make_async_copy(array.at[0, b], arrays[side].at[0, b], sems.at[len(copies)]))
+    copies.append(pltpu.make_async_copy(near, near_out, sems.at[len(copies)]))
+    for copy in copies:
+        copy.start()
+    lower = lane_of((channels, TILE)) < 64
+    odd = on_odd() == 1
+    for own in (own_x, own_g):
+        own[bricks] = jnp.zeros((channels, 512), jnp.bfloat16)
+    copies[0].wait()
+    present[...] = mask_here[0].astype(jnp.float32)
+    for b in range(bricks):
+        there = jnp.broadcast_to(present[b : b + 1, :], (channels, 512)).astype(jnp.bfloat16)
+        for side, own in enumerate((own_x, own_g)):
+            copies[1 + 2 * b + side].wait()
+            own[b] = arrays[side][0, b] * there
+        x, g = own_x[b].astype(jnp.float32), own_g[b].astype(jnp.float32)
+        head = jnp.where(lower, x[:, :TILE], swap_halves(g[:, :TILE])).astype(jnp.bfloat16)
+        tail = jnp.where(lower, swap_halves(g[:, 3 * TILE :]), x[:, 3 * TILE :]).astype(jnp.bfloat16)
+        one[b] = jnp.where(odd, head, tail)
+        two[b] = jnp.where(odd, tail, head)
+    copies[-1].wait()
 
 
 def prepare_ends(near, up, mine, table, local, weights):
@@ -437,7 +488,7 @@
             scratch(*occupancy.shape, dtype=jnp.int32),
             scratch(*features.shape),
             scratch(*features.shape),
-            pltpu.SemaphoreType.DMA((4,)),
+            pltpu.SemaphoreType.DMA((2 * bricks + 2,)),
         ],
         limit=16 << 20,
     )

time: 42.8 us -> 42.8 us (level)
  no operation moved by 1% of the time
where the time goes in v8:
time: 42.8 us; the launch traced here: 42.6 us
  starting transfers between devices  15.8 us (37%)
  waiting for transfers between devices  14.5 us (34%)
  Pallas kernels  11.5 us (27%)
  between operations  0.76 us (2%)
    ppermute x15, waiting for transfers between devices, exchange(): return lax.ppermute(x, AXES, [(i, i ^ bit) for i in range(count)])  13 us
    ppermute x15, starting transfers between devices, exchange(): return lax.ppermute(x, AXES, [(i, i ^ bit) for i in range(count)])  12.2 us
    pallas_call x7, Pallas kernels, call(): pl.pallas_call(kernel, out_shape=shapes, in_specs=specs, out_specs=VMEM i...  9.63 us
    ppermute x1, starting transfers between devices, program(): got_one = lax.ppermute(one, AXES, forth)  3.05 us
    pallas_call x2, Pallas kernels, unpack(): pl.pallas_call(functools.partial(unpack_kernel, groups, own), out_shape=t...  1.88 us
    ppermute x1, waiting for transfers between devices, program(): got_two = lax.ppermute(two, AXES, [(b, a) for a, b in forth])  1.46 us
  transfers between devices with their start and end apart: 17, of which 10 were waited for; matrix products, arithmetic and copies ran while one was open for 0% of the time, Pallas kernels for 20%

profile of v8, /device:TPU:0, one launch (start us, length us, event | category | flops | bytes accessed | tf_op | source)
XLA Modules:
  0.0 42.6 jit_solution(16356053213576971893)
XLA Ops:
  0.6 1.1 %shard_map.76 = (bf16[2,64,128]{2,1,0:T(8,128)(2,1)S(1)}, bf16[2,64,128]{2,1,0:T(8,128)(2,1)S(1)}, bf16[3,64,512]{2,1,0:T(8,128)(2,1)S(1)}, bf16[3,64,512]{2,1,0...) custom-call(bf16[1,2,64,512]{3,2,1,0:T(8,128)(2,1)} %features.1, bf16[1,2,64,512]{3,2,1,0:T(8,128)(2,1)} %cotangent.1, ...), custom_call_target="tpu_custom_call" | custom-call | flops 100000000 | bytes 1000000 | tf_op jit(solution)/shard_map/pallas_call | solution.py:458
  1.8 3.1 %collective-permute-start.1 = (bf16[2,64,128]{2,1,0:T(8,128)(2,1)S(1)}, bf16[2,64,128]{2,1,0:T(8,128)(2,1)S(1)}, u32[]{:S(2)}, u32[]{:S(2)}) collective-permute-start(bf16[2,64,128]{2,1,0:T(8,128)(2,1)S(1)} %get-tuple-element.29.mine), channel_id=1, source_target_pairs={{0,4},{4,8},{8,12},{12,16},{16,20},{20,24},{24,28},{28,29},{29,25}... | collective-permute-start | bytes 98312 | tf_op jit(solution)/shard_map/ppermute | solution.py:496
  4.8 2.0 %shard_map.78 = (bf16[2,576,512]{2,1,0:T(8,128)(2,1)S(1)}, f32[896,128]{1,0:T(8,128)S(1)}, bf16[256,384]{1,0:T(8,128)(2,1)S(1)}, bf16[256,384]{1,0:T(8,128)(2,1)...) custom-call(s32[1,2,27]{2,1,0:T(2,128)S(1)} %get-tuple-element.24.near, ...), custom_call_target="tpu_custom_call" | custom-call | flops 100000000 | bytes 1000000 | tf_op jit(solution)/shard_map/pallas_call | solution.py:458
  6.8 0.9 %shard_map.79 = (bf16[2,576,128]{2,1,0:T(8,128)(2,1)S(1)}, f32[112,128]{1,0:T(8,128)S(1)}, f32[336,128]{1,0:T(8,128)S(1)}, f32[112,128]{1,0:T(8,128)S(1)}, f32[336,128]{1,0:T(8,128)S(1)}) custom-call(bf16[2,64,128]{2,1,0:T(8,128)(2,1)S(1)} %get-tuple-element.25.facing.mine, bf16[2,64,128]{2,1,0:T(8,128)(2,1)S(1)} %collective-permute-done.1.other, ...), custom_call_target="tpu_custom_call" | custom-call | flops 100000000 | bytes 1000000 | tf_op jit(solution)/shard_map/pallas_call | solution.py:458
  8.3 1.0 %collective-permute-done.5 = f32[112,128]{1,0:T(8,128)S(1)} collective-permute-done((f32[112,128]{1,0:T(8,128)S(1)}, f32[112,128]{1,0:T(8,128)S(1)}, u32[]{:S(2)}, u32[]{:S(2)}) %collective-permute-start.5) | collective-permute-done | bytes 57376 | tf_op jit(solution)/shard_map/ppermute | solution.py:415
  9.3 3.0 %collective-permute-start.6 = (f32[112,128]{1,0:T(8,128)S(1)}, f32[112,128]{1,0:T(8,128)S(1)}, u32[]{:S(2)}, u32[]{:S(2)}) collective-permute-start(f32[112,128]{1,0:T(8,128)S(1)} %add.27), channel_id=1, source_target_pairs={{0,6},{1,7},{2,4},{3,5},{4,2},{5,3},{6,0},{7,1},{8,14},{9,15},{10,... | collective-permute-start | bytes 172040 | tf_op jit(solution)/shard_map/ppermute | solution.py:415
  12.4 0.6 %collective-permute-start.3 = (f32[112,128]{1,0:T(8,128)S(1)}, f32[112,128]{1,0:T(8,128)S(1)}, u32[]{:S(2)}, u32[]{:S(2)}) collective-permute-start(f32[112,128]{1,0:T(8,128)S(1)} %get-tuple-element.45), channel_id=1, source_target_pairs={{0,2},{1,3},{2,0},{3,1},{4,6},{5,7},{6,4},{7,5},{8,10},{9,11},{10,... | collective-permute-start | bytes 172040 | tf_op jit(solution)/shard_map/ppermute | solution.py:415
  13.0 1.8 %collective-permute-done.6 = f32[112,128]{1,0:T(8,128)S(1)} collective-permute-done((f32[112,128]{1,0:T(8,128)S(1)}, f32[112,128]{1,0:T(8,128)S(1)}, u32[]{:S(2)}, u32[]{:S(2)}) %collective-permute-start.6) | collective-permute-done | bytes 57376 | tf_op jit(solution)/shard_map/ppermute | solution.py:415
  14.9 1.8 %collective-permute-done.3 = f32[112,128]{1,0:T(8,128)S(1)} collective-permute-done((f32[112,128]{1,0:T(8,128)S(1)}, f32[112,128]{1,0:T(8,128)S(1)}, u32[]{:S(2)}, u32[]{:S(2)}) %collective-permute-start.3) | collective-permute-done | bytes 57376 | tf_op jit(solution)/shard_map/ppermute | solution.py:415
  17.2 3.6 %collective-permute-start.9 = (f32[112,128]{1,0:T(8,128)S(1)}, f32[112,128]{1,0:T(8,128)S(1)}, u32[]{:S(2)}, u32[]{:S(2)}) collective-permute-start(f32[112,128]{1,0:T(8,128)S(1)} %fusion.1), channel_id=1, source_target_pairs={{0,24},{1,25},{2,26},{3,27},{4,28},{5,29},{6,30},{7,31},{8,16},{9,... | collective-permute-start | bytes 172040 | tf_op jit(solution)/shard_map/ppermute | solution.py:415
  20.7 0.9 %collective-permute-start.7 = (f32[112,128]{1,0:T(8,128)S(1)}, f32[112,128]{1,0:T(8,128)S(1)}, u32[]{:S(2)}, u32[]{:S(2)}) collective-permute-start(f32[112,128]{1,0:T(8,128)S(1)} %fusion.1), channel_id=1, source_target_pairs={{0,8},{1,9},{2,10},{3,11},{4,12},{5,13},{6,14},{7,15},{8,0},{9,1},... | collective-permute-start | bytes 172040 | tf_op jit(solution)/shard_map/ppermute | solution.py:415
  21.6 2.1 %collective-permute-done.9 = f32[112,128]{1,0:T(8,128)S(1)} collective-permute-done((f32[112,128]{1,0:T(8,128)S(1)}, f32[112,128]{1,0:T(8,128)S(1)}, u32[]{:S(2)}, u32[]{:S(2)}) %collective-permute-start.9) | collective-permute-done | bytes 57376 | tf_op jit(solution)/shard_map/ppermute | solution.py:415
  23.7 2.1 %collective-permute-done.8 = f32[112,128]{1,0:T(8,128)S(1)} collective-permute-done((f32[112,128]{1,0:T(8,128)S(1)}, f32[112,128]{1,0:T(8,128)S(1)}, u32[]{:S(2)}, u32[]{:S(2)}) %collective-permute-start.8) | collective-permute-done | bytes 57376 | tf_op jit(solution)/shard_map/ppermute | solution.py:415
  25.9 2.5 %collective-permute-start.15 = (f32[112,128]{1,0:T(8,128)S(1)}, f32[112,128]{1,0:T(8,128)S(1)}, u32[]{:S(2)}, u32[]{:S(2)}) collective-permute-start(f32[112,128]{1,0:T(8,128)S(1)} %add_add_fusion.refs_0_), channel_id=1, source_target_pairs={{0,6},{1,7},{2,4},{3,5},{4,2},{5,3},{6,0},{7,1},{8,14},{9,15},{10,... | collective-permute-start | bytes 172040 | tf_op jit(solution)/shard_map/ppermute | solution.py:415
  28.3 0.6 %collective-permute-start.13 = (f32[112,128]{1,0:T(8,128)S(1)}, f32[112,128]{1,0:T(8,128)S(1)}, u32[]{:S(2)}, u32[]{:S(2)}) collective-permute-start(f32[112,128]{1,0:T(8,128)S(1)} %add_add_fusion.refs_0_), channel_id=1, source_target_pairs={{0,4},{1,5},{2,6},{3,7},{4,0},{5,1},{6,2},{7,3},{8,12},{9,13},{10,... | collective-permute-start | bytes 172040 | tf_op jit(solution)/shard_map/ppermute | solution.py:415
  29.4 1.7 %collective-permute-done.15.refs_3_ = f32[112,128]{1,0:T(8,128)S(1)} collective-permute-done((f32[112,128]{1,0:T(8,128)S(1)}, f32[112,128]{1,0:T(8,128)S(1)}, u32[]{:S(2)}, u32[]{:S(2)}) %collective-permute-start.15) | collective-permute-done | bytes 57376 | tf_op jit(solution)/shard_map/ppermute | solution.py:415
  31.1 1.4 %collective-permute-done.13.refs_2_ = f32[112,128]{1,0:T(8,128)S(1)} collective-permute-done((f32[112,128]{1,0:T(8,128)S(1)}, f32[112,128]{1,0:T(8,128)S(1)}, u32[]{:S(2)}, u32[]{:S(2)}) %collective-permute-start.13) | collective-permute-done | bytes 57376 | tf_op jit(solution)/shard_map/ppermute | solution.py:415
  32.5 0.6 %collective-permute-done.11.refs_1_ = f32[112,128]{1,0:T(8,128)S(1)} collective-permute-done((f32[112,128]{1,0:T(8,128)S(1)}, f32[112,128]{1,0:T(8,128)S(1)}, u32[]{:S(2)}, u32[]{:S(2)}) %collective-permute-start.11) | collective-permute-done | bytes 57376 | tf_op jit(solution)/shard_map/ppermute | solution.py:415
  33.6 1.5 %shard_map.81.inner = bf16[2,576,512]{2,1,0:T(8,128)(2,1)S(1)} custom-call(s32[1,2,27]{2,1,0:T(2,128)S(1)} %get-tuple-element.24.near, bf16[3,64,512]{2,1,0:T(8,128)(2,1)S(1)} %get-tuple-element.28.gradient.own, bf16[256,384]{1,0:T(8,128)(2,1)S(1)} %get-tuple-element.34.select_y, bf16[256,384]{1,0:T(8,128)(2,1)S(1)} %get-tuple-element.35.select_z), custom_call_target="tpu_custom_call" | custom-call | flops 100000000 | bytes 1000000 | tf_op jit(solution)/shard_map/pallas_call | solution.py:458
  35.6 1.5 %collective-permute-done.other = bf16[2,64,128]{2,1,0:T(8,128)(2,1)S(1)} collective-permute-done((bf16[2,64,128]{2,1,0:T(8,128)(2,1)S(1)}, bf16[2,64,128]{2,1,0:T(8,128)(2,1)S(1)}, u32[]{:S(2)}, u32[]{:S(2)}) %collective-permute-start) | collective-permute-done | bytes 32800 | tf_op jit(solution)/shard_map/ppermute | solution.py:497
  37.0 2.2 %shard_map.80 = (bf16[1,2,64,512]{3,2,1,0:T(8,128)(2,1)}, bf16[2,576,128]{2,1,0:T(8,128)(2,1)S(1)}) custom-call(s32[1,2,27]{2,1,0:T(2,128)S(1)} %get-tuple-element.24.near, bf16[2,64,128]{2,1,0:T(8,128)(2,1)S(1)} %get-tuple-element.25.facing.mine, bf16[2,64,128]{2,1,0:T(8,128)(2,1)S(1)} %collective-permute-done.other, ...), custom_call_target="tpu_custom_call" | custom-call | flops 100000000 | bytes 1000000 | tf_op jit(solution)/shard_map/pallas_call | solution.py:458
  39.3 1.4 %shard_map.82 = bf16[1,2,64,512]{3,2,1,0:T(8,128)(2,1)} custom-call(bf16[192,576]{1,0:T(8,128)(2,1)S(1)} %get-tuple-element.39.table, bf16[2,576,512]{2,1,0:T(8,128)(2,1)S(1)} %shard_map.81.inner, bf16[2,576,128]{2,1,0:T(8,128)(2,1)S(1)} %get-tuple-element.36.ends, bf16[2,576,128]{2,1,0:T(8,128)(2,1)S(1)} %get-tuple-element.40.more_ends, ...), custom_call_target="tpu_custom_call" | custom-call | flops 100000000 | bytes 1000000 | tf_op jit(solution)/shard_map/pallas_call | solution.py:458
  40.7 0.9 %unpack.2.refs_4_ = f32[27,64,64]{2,1,0:T(8,128)} custom-call(f32[112,128]{1,0:T(8,128)S(1)} %add_add_fusion.refs_0_, f32[112,128]{1,0:T(8,128)S(1)} %collective-permute-done.11.refs_1_, f32[112,128]{1,0:T(8,128)S(1)} %collective-permute-done.13.refs_2_, f32[112,128]{1,0:T(8,128)S(1)} %collective-permute-done.15.refs_3_), custom_call_target="tpu_custom_call" | custom-call | flops 1000000 | bytes 1000000 | tf_op jit(solution)/shard_map/unpack/pallas_call | solution.py:533
  41.7 1.0 %unpack.3 = f32[27,64,64]{2,1,0:T(8,128)} custom-call(f32[112,128]{1,0:T(8,128)S(1)} %collective-permute-done.10.refs_0_, f32[112,128]{1,0:T(8,128)S(1)} %collective-permute-done.12.refs_1_, f32[112,128]{1,0:T(8,128)S(1)} %collective-permute-done.14.refs_2_, f32[112,128]{1,0:T(8,128)S(1)} %collective-permute-done.16.refs_3_, ...), custom_call_target="tpu_custom_call", output_to_operand_aliasing={{}: (4, {})} | custom-call | flops 1000000 | bytes 1000000 | tf_op jit(solution)/shard_map/unpack/pallas_call | solution.py:533
  (26 shorter events, 2.7 us)
Async XLA Ops:
  1.8 5.1 %collective-permute-start.1 = (bf16[2,64,128]{2,1,0:T(8,128)(2,1)S(1)}, bf16[2,64,128]{2,1,0:T(8,128)(2,1)S(1)}, u32[]{:S(2)}, u32[]{:S(2)}) collective-permute-start(bf16[2,64,128]{2,1,0:T(8,128)(2,1)S(1)} %get-tuple-element.29.mine), channel_id=1, source_target_pairs={{0,4},{4,8},{8,12},{12,16},{16,20},{20,24},{24,28},{28,29},{29,25}... | collective-permute-start | bytes 98312 | tf_op jit(solution)/shard_map/ppermute | solution.py:496
  7.8 4.6 %collective-permute-start.2 = (f32[336,128]{1,0:T(8,128)S(1)}, f32[336,128]{1,0:T(8,128)S(1)}, u32[]{:S(2)}, u32[]{:S(2)}) collective-permute-start(f32[336,128]{1,0:T(8,128)S(1)} %get-tuple-element.42), channel_id=1, source_target_pairs={{0,1},{1,0},{2,3},{3,2},{4,5},{5,4},{6,7},{7,6},{8,9},{9,8},{10,11... | collective-permute-start | bytes 516104 | tf_op jit(solution)/shard_map/ppermute | solution.py:415
  7.8 1.5 %collective-permute-start.5 = (f32[112,128]{1,0:T(8,128)S(1)}, f32[112,128]{1,0:T(8,128)S(1)}, u32[]{:S(2)}, u32[]{:S(2)}) collective-permute-start(f32[112,128]{1,0:T(8,128)S(1)} %get-tuple-element.44), channel_id=1, source_target_pairs={{0,1},{1,0},{2,3},{3,2},{4,5},{5,4},{6,7},{7,6},{8,9},{9,8},{10,11... | collective-permute-start | bytes 172040 | tf_op jit(solution)/shard_map/ppermute | solution.py:415
  9.3 5.5 %collective-permute-start.6 = (f32[112,128]{1,0:T(8,128)S(1)}, f32[112,128]{1,0:T(8,128)S(1)}, u32[]{:S(2)}, u32[]{:S(2)}) collective-permute-start(f32[112,128]{1,0:T(8,128)S(1)} %add.27), channel_id=1, source_target_pairs={{0,6},{1,7},{2,4},{3,5},{4,2},{5,3},{6,0},{7,1},{8,14},{9,15},{10,... | collective-permute-start | bytes 172040 | tf_op jit(solution)/shard_map/ppermute | solution.py:415
  12.4 22.8 %copy-start = (bf16[27,64,64]{2,1,0:T(8,128)(2,1)S(1)}, bf16[27,64,64]{2,1,0:T(8,128)(2,1)}, u32[]{:S(2)}) copy-start(bf16[27,64,64]{2,1,0:T(8,128)(2,1)} %weight.1) | copy-start | bytes 663556
  12.4 4.2 %collective-permute-start.3 = (f32[112,128]{1,0:T(8,128)S(1)}, f32[112,128]{1,0:T(8,128)S(1)}, u32[]{:S(2)}, u32[]{:S(2)}) collective-permute-start(f32[112,128]{1,0:T(8,128)S(1)} %get-tuple-element.45), channel_id=1, source_target_pairs={{0,2},{1,3},{2,0},{3,1},{4,6},{5,7},{6,4},{7,5},{8,10},{9,11},{10,... | collective-permute-start | bytes 172040 | tf_op jit(solution)/shard_map/ppermute | solution.py:415
  13.0 4.2 %collective-permute-start.4 = (f32[112,128]{1,0:T(8,128)S(1)}, f32[112,128]{1,0:T(8,128)S(1)}, u32[]{:S(2)}, u32[]{:S(2)}) collective-permute-start(f32[112,128]{1,0:T(8,128)S(1)} %get-tuple-element.46), channel_id=1, source_target_pairs={{0,4},{1,5},{2,6},{3,7},{4,0},{5,1},{6,2},{7,3},{8,12},{9,13},{10,... | collective-permute-start | bytes 172040 | tf_op jit(solution)/shard_map/ppermute | solution.py:415
  17.2 6.6 %collective-permute-start.9 = (f32[112,128]{1,0:T(8,128)S(1)}, f32[112,128]{1,0:T(8,128)S(1)}, u32[]{:S(2)}, u32[]{:S(2)}) collective-permute-start(f32[112,128]{1,0:T(8,128)S(1)} %fusion.1), channel_id=1, source_target_pairs={{0,24},{1,25},{2,26},{3,27},{4,28},{5,29},{6,30},{7,31},{8,16},{9,... | collective-permute-start | bytes 172040 | tf_op jit(solution)/shard_map/ppermute | solution.py:415
  20.7 5.1 %collective-permute-start.8 = (f32[112,128]{1,0:T(8,128)S(1)}, f32[112,128]{1,0:T(8,128)S(1)}, u32[]{:S(2)}, u32[]{:S(2)}) collective-permute-start(f32[112,128]{1,0:T(8,128)S(1)} %fusion.1), channel_id=1, source_target_pairs={{0,16},{1,17},{2,18},{3,19},{4,20},{5,21},{6,22},{7,23},{8,24},{9,... | collective-permute-start | bytes 172040 | tf_op jit(solution)/shard_map/ppermute | solution.py:415
  20.7 5.1 %collective-permute-start.7 = (f32[112,128]{1,0:T(8,128)S(1)}, f32[112,128]{1,0:T(8,128)S(1)}, u32[]{:S(2)}, u32[]{:S(2)}) collective-permute-start(f32[112,128]{1,0:T(8,128)S(1)} %fusion.1), channel_id=1, source_target_pairs={{0,8},{1,9},{2,10},{3,11},{4,12},{5,13},{6,14},{7,15},{8,0},{9,1},... | collective-permute-start | bytes 172040 | tf_op jit(solution)/shard_map/ppermute | solution.py:415
  25.9 5.3 %collective-permute-start.15 = (f32[112,128]{1,0:T(8,128)S(1)}, f32[112,128]{1,0:T(8,128)S(1)}, u32[]{:S(2)}, u32[]{:S(2)}) collective-permute-start(f32[112,128]{1,0:T(8,128)S(1)} %add_add_fusion.refs_0_), channel_id=1, source_target_pairs={{0,6},{1,7},{2,4},{3,5},{4,2},{5,3},{6,0},{7,1},{8,14},{9,15},{10,... | collective-permute-start | bytes 172040 | tf_op jit(solution)/shard_map/ppermute | solution.py:415
  28.3 4.2 %collective-permute-start.13 = (f32[112,128]{1,0:T(8,128)S(1)}, f32[112,128]{1,0:T(8,128)S(1)}, u32[]{:S(2)}, u32[]{:S(2)}) collective-permute-start(f32[112,128]{1,0:T(8,128)S(1)} %add_add_fusion.refs_0_), channel_id=1, source_target_pairs={{0,4},{1,5},{2,6},{3,7},{4,0},{5,1},{6,2},{7,3},{8,12},{9,13},{10,... | collective-permute-start | bytes 172040 | tf_op jit(solution)/shard_map/ppermute | solution.py:415
  28.9 4.2 %collective-permute-start.11 = (f32[112,128]{1,0:T(8,128)S(1)}, f32[112,128]{1,0:T(8,128)S(1)}, u32[]{:S(2)}, u32[]{:S(2)}) collective-permute-start(f32[112,128]{1,0:T(8,128)S(1)} %add_add_fusion.refs_0_), channel_id=1, source_target_pairs={{0,2},{1,3},{2,0},{3,1},{4,6},{5,7},{6,4},{7,5},{8,10},{9,11},{10,... | collective-permute-start | bytes 172040 | tf_op jit(solution)/shard_map/ppermute | solution.py:415
  29.4 12.2 %collective-permute-start.10 = (f32[112,128]{1,0:T(8,128)S(1)}, f32[112,128]{1,0:T(8,128)S(1)}, u32[]{:S(2)}, u32[]{:S(2)}) collective-permute-start(f32[112,128]{1,0:T(8,128)S(1)} %add_add_fusion.refs_0_), channel_id=1, source_target_pairs={{0,1},{1,0},{2,3},{3,2},{4,5},{5,4},{6,7},{7,6},{8,9},{9,8},{10,11... | collective-permute-start | bytes 172040 | tf_op jit(solution)/shard_map/ppermute | solution.py:415
  31.1 10.5 %collective-permute-start.16 = (f32[112,128]{1,0:T(8,128)S(1)}, f32[112,128]{1,0:T(8,128)S(1)}, u32[]{:S(2)}, u32[]{:S(2)}) collective-permute-start(f32[112,128]{1,0:T(8,128)S(1)} %collective-permute-done.15.refs_3_), channel_id=1, source_target_pairs={{0,1},{1,0},{2,3},{3,2},{4,5},{5,4},{6,7},{7,6},{8,9},{9,8},{10,11... | collective-permute-start | bytes 172040 | tf_op jit(solution)/shard_map/ppermute | solution.py:415
  32.5 9.1 %collective-permute-start.14 = (f32[112,128]{1,0:T(8,128)S(1)}, f32[112,128]{1,0:T(8,128)S(1)}, u32[]{:S(2)}, u32[]{:S(2)}) collective-permute-start(f32[112,128]{1,0:T(8,128)S(1)} %collective-permute-done.13.refs_2_), channel_id=1, source_target_pairs={{0,1},{1,0},{2,3},{3,2},{4,5},{5,4},{6,7},{7,6},{8,9},{9,8},{10,11... | collective-permute-start | bytes 172040 | tf_op jit(solution)/shard_map/ppermute | solution.py:415
  33.1 8.5 %collective-permute-start.12 = (f32[112,128]{1,0:T(8,128)S(1)}, f32[112,128]{1,0:T(8,128)S(1)}, u32[]{:S(2)}, u32[]{:S(2)}) collective-permute-start(f32[112,128]{1,0:T(8,128)S(1)} %collective-permute-done.11.refs_1_), channel_id=1, source_target_pairs={{0,1},{1,0},{2,3},{3,2},{4,5},{5,4},{6,7},{7,6},{8,9},{9,8},{10,11... | collective-permute-start | bytes 172040 | tf_op jit(solution)/shard_map/ppermute | solution.py:415
  33.1 3.9 %collective-permute-start = (bf16[2,64,128]{2,1,0:T(8,128)(2,1)S(1)}, bf16[2,64,128]{2,1,0:T(8,128)(2,1)S(1)}, u32[]{:S(2)}, u32[]{:S(2)}) collective-permute-start(bf16[2,64,128]{2,1,0:T(8,128)(2,1)S(1)} %get-tuple-element.25.facing.mine), channel_id=1, source_target_pairs={{4,0},{8,4},{12,8},{16,12},{20,16},{24,20},{28,24},{29,28},{25,29}... | collective-permute-start | bytes 98312 | tf_op jit(solution)/shard_map/ppermute | solution.py:497

commit v9 on v8

--- a/solution.py
+++ b/solution.py
@@ -267,6 +267,11 @@
     return lax.axis_index("space") * lax.axis_size("scene") + lax.axis_index("scene")
 
 
+def device_half():
+    place = device_place()
+    return jnp.bitwise_xor(place, place // 2) % 2
+
+
 def outer_kernel(
     scale, groups, facing, other, local, weights, inner, select_y, select_z,
     shifted, send_far, send_rest, keep_far, keep_rest, parts, middle, grad
@@ -297,7 +302,7 @@
     grad[9 * channels :, :] = inner[9 * channels :, :]
     place = device_place()
     size = send_far.shape[0]
-    for side, far, rest in ((1 - place % 2, send_far, send_rest), (place % 2, keep_far, keep_rest)):
+    for side, far, rest in ((1 - device_half(), send_far, send_rest), (device_half(), keep_far, keep_rest)):
         for k in range(groups):
             at = pl.multiple_of((side * groups + jnp.bitwise_xor(place // 2 % groups, k)) * size, 8)
             if k == groups - 1:
@@ -394,7 +399,7 @@
         for copy in copies:
             copy.wait()
 
-    lower = (place % 2 == 0) == own
+    lower = (device_half() == 0) == own
     pl.when(lower)(lambda: write(0, half))
     pl.when(jnp.logical_not(lower))(lambda: write(half, 2 * half))
 
@@ -423,7 +428,7 @@
     mine = [rest[k * size : (k + 1) * size] for k in range(groups - 1)] + [far]
     own, got = mine[0], []
     for k in range(1, groups):
-        got.append(exchange(mine[k], 2 * k))
+        got.append(exchange(mine[k], 2 * k + k % 2))
     for one in got:
         own = own + one
     bit = 2 * groups
@@ -438,7 +443,7 @@
         bit *= wide
     chunks = [own]
     for k in range(1, groups):
-        chunks.append(exchange(own, 2 * k))
+        chunks.append(exchange(own, 2 * k + k % 2))
     theirs = []
     for k in range(groups):
         theirs.append(exchange(chunks[k], 1))

time: 42.8 us -> 42.1 us (0.984)
  starting transfers between devices: 15.8 us -> 15.2 us
    ppermute x15, waiting for transfers between devices: 13 us -> 12.4 us  [exchange(): return lax.ppermute(x, AXES, [(i, i ^ bit) for i in range(count)])]
  transfers between devices with their start and end apart: 17 -> 17, of which waited for: 10 -> 9; matrix products, arithmetic and copies ran while one was open for 0% -> 0% of each run, Pallas kernels for 20% -> 20%
where the time goes in v9:
time: 42.1 us; the launch traced here: 41.9 us
  starting transfers between devices  15.2 us (36%)
  waiting for transfers between devices  14.3 us (34%)
  Pallas kernels  11.5 us (27%)
  between operations  0.77 us (2%)
    ppermute x15, waiting for transfers between devices, exchange(): return lax.ppermute(x, AXES, [(i, i ^ bit) for i in range(count)])  12.4 us
    ppermute x15, starting transfers between devices, exchange(): return lax.ppermute(x, AXES, [(i, i ^ bit) for i in range(count)])  12 us
    pallas_call x7, Pallas kernels, call(): pl.pallas_call(kernel, out_shape=shapes, in_specs=specs, out_specs=VMEM i...  9.63 us
    ppermute x1, starting transfers between devices, program(): got_one = lax.ppermute(one, AXES, forth)  3.05 us
    pallas_call x2, Pallas kernels, unpack(): pl.pallas_call(functools.partial(unpack_kernel, groups, own), out_shape=t...  1.88 us
    ppermute x1, waiting for transfers between devices, program(): got_two = lax.ppermute(two, AXES, [(b, a) for a, b in forth])  1.85 us
  transfers between devices with their start and end apart: 17, of which 9 were waited for; matrix products, arithmetic and copies ran while one was open for 0% of the time, Pallas kernels for 20%

profile of v9, /device:TPU:0, one launch (start us, length us, event | category | flops | bytes accessed | tf_op | source)
XLA Modules:
  0.0 41.9 jit_solution(7368209903358171032)
XLA Ops:
  0.6 1.1 %shard_map.76 = (bf16[2,64,128]{2,1,0:T(8,128)(2,1)S(1)}, bf16[2,64,128]{2,1,0:T(8,128)(2,1)S(1)}, bf16[3,64,512]{2,1,0:T(8,128)(2,1)S(1)}, bf16[3,64,512]{2,1,0...) custom-call(bf16[1,2,64,512]{3,2,1,0:T(8,128)(2,1)} %features.1, bf16[1,2,64,512]{3,2,1,0:T(8,128)(2,1)} %cotangent.1, ...), custom_call_target="tpu_custom_call" | custom-call | flops 100000000 | bytes 1000000 | tf_op jit(solution)/shard_map/pallas_call | solution.py:463
  1.8 3.1 %collective-permute-start.1 = (bf16[2,64,128]{2,1,0:T(8,128)(2,1)S(1)}, bf16[2,64,128]{2,1,0:T(8,128)(2,1)S(1)}, u32[]{:S(2)}, u32[]{:S(2)}) collective-permute-start(bf16[2,64,128]{2,1,0:T(8,128)(2,1)S(1)} %get-tuple-element.29.mine), channel_id=1, source_target_pairs={{0,4},{4,8},{8,12},{12,16},{16,20},{20,24},{24,28},{28,29},{29,25}... | collective-permute-start | bytes 98312 | tf_op jit(solution)/shard_map/ppermute | solution.py:501
  4.8 2.0 %shard_map.78 = (bf16[2,576,512]{2,1,0:T(8,128)(2,1)S(1)}, f32[896,128]{1,0:T(8,128)S(1)}, bf16[256,384]{1,0:T(8,128)(2,1)S(1)}, bf16[256,384]{1,0:T(8,128)(2,1)...) custom-call(s32[1,2,27]{2,1,0:T(2,128)S(1)} %get-tuple-element.24.near, ...), custom_call_target="tpu_custom_call" | custom-call | flops 100000000 | bytes 1000000 | tf_op jit(solution)/shard_map/pallas_call | solution.py:463
  6.8 0.9 %shard_map.79 = (bf16[2,576,128]{2,1,0:T(8,128)(2,1)S(1)}, f32[112,128]{1,0:T(8,128)S(1)}, f32[336,128]{1,0:T(8,128)S(1)}, f32[112,128]{1,0:T(8,128)S(1)}, f32[336,128]{1,0:T(8,128)S(1)}) custom-call(bf16[2,64,128]{2,1,0:T(8,128)(2,1)S(1)} %get-tuple-element.25.facing.mine, bf16[2,64,128]{2,1,0:T(8,128)(2,1)S(1)} %collective-permute-done.1.other, ...), custom_call_target="tpu_custom_call" | custom-call | flops 100000000 | bytes 1000000 | tf_op jit(solution)/shard_map/pallas_call | solution.py:463
  7.8 0.5 %collective-permute-start.5 = (f32[112,128]{1,0:T(8,128)S(1)}, f32[112,128]{1,0:T(8,128)S(1)}, u32[]{:S(2)}, u32[]{:S(2)}) collective-permute-start(f32[112,128]{1,0:T(8,128)S(1)} %get-tuple-element.44), channel_id=1, source_target_pairs={{0,1},{1,0},{2,3},{3,2},{4,5},{5,4},{6,7},{7,6},{8,9},{9,8},{10,11... | collective-permute-start | bytes 172040 | tf_op jit(solution)/shard_map/ppermute | solution.py:420
  8.3 1.0 %collective-permute-done.5 = f32[112,128]{1,0:T(8,128)S(1)} collective-permute-done((f32[112,128]{1,0:T(8,128)S(1)}, f32[112,128]{1,0:T(8,128)S(1)}, u32[]{:S(2)}, u32[]{:S(2)}) %collective-permute-start.5) | collective-permute-done | bytes 57376 | tf_op jit(solution)/shard_map/ppermute | solution.py:420
  9.3 2.9 %collective-permute-start.6 = (f32[112,128]{1,0:T(8,128)S(1)}, f32[112,128]{1,0:T(8,128)S(1)}, u32[]{:S(2)}, u32[]{:S(2)}) collective-permute-start(f32[112,128]{1,0:T(8,128)S(1)} %add.27), channel_id=1, source_target_pairs={{0,7},{1,6},{2,5},{3,4},{4,3},{5,2},{6,1},{7,0},{8,15},{9,14},{10,... | collective-permute-start | bytes 172040 | tf_op jit(solution)/shard_map/ppermute | solution.py:420
  12.9 1.6 %collective-permute-done.6 = f32[112,128]{1,0:T(8,128)S(1)} collective-permute-done((f32[112,128]{1,0:T(8,128)S(1)}, f32[112,128]{1,0:T(8,128)S(1)}, u32[]{:S(2)}, u32[]{:S(2)}) %collective-permute-start.6) | collective-permute-done | bytes 57376 | tf_op jit(solution)/shard_map/ppermute | solution.py:420
  14.5 1.6 %collective-permute-done.3 = f32[112,128]{1,0:T(8,128)S(1)} collective-permute-done((f32[112,128]{1,0:T(8,128)S(1)}, f32[112,128]{1,0:T(8,128)S(1)}, u32[]{:S(2)}, u32[]{:S(2)}) %collective-permute-start.3) | collective-permute-done | bytes 57376 | tf_op jit(solution)/shard_map/ppermute | solution.py:420
  16.1 0.8 %collective-permute-done.4 = f32[112,128]{1,0:T(8,128)S(1)} collective-permute-done((f32[112,128]{1,0:T(8,128)S(1)}, f32[112,128]{1,0:T(8,128)S(1)}, u32[]{:S(2)}, u32[]{:S(2)}) %collective-permute-start.4) | collective-permute-done | bytes 57376 | tf_op jit(solution)/shard_map/ppermute | solution.py:420
  16.9 3.8 %collective-permute-start.9 = (f32[112,128]{1,0:T(8,128)S(1)}, f32[112,128]{1,0:T(8,128)S(1)}, u32[]{:S(2)}, u32[]{:S(2)}) collective-permute-start(f32[112,128]{1,0:T(8,128)S(1)} %fusion.1), channel_id=1, source_target_pairs={{0,24},{1,25},{2,26},{3,27},{4,28},{5,29},{6,30},{7,31},{8,16},{9,... | collective-permute-start | bytes 172040 | tf_op jit(solution)/shard_map/ppermute | solution.py:420
  20.7 0.6 %collective-permute-start.7 = (f32[112,128]{1,0:T(8,128)S(1)}, f32[112,128]{1,0:T(8,128)S(1)}, u32[]{:S(2)}, u32[]{:S(2)}) collective-permute-start(f32[112,128]{1,0:T(8,128)S(1)} %fusion.1), channel_id=1, source_target_pairs={{0,8},{1,9},{2,10},{3,11},{4,12},{5,13},{6,14},{7,15},{8,0},{9,1},... | collective-permute-start | bytes 172040 | tf_op jit(solution)/shard_map/ppermute | solution.py:420
  21.4 2.0 %collective-permute-done.9 = f32[112,128]{1,0:T(8,128)S(1)} collective-permute-done((f32[112,128]{1,0:T(8,128)S(1)}, f32[112,128]{1,0:T(8,128)S(1)}, u32[]{:S(2)}, u32[]{:S(2)}) %collective-permute-start.9) | collective-permute-done | bytes 57376 | tf_op jit(solution)/shard_map/ppermute | solution.py:420
  23.3 2.4 %collective-permute-done.8 = f32[112,128]{1,0:T(8,128)S(1)} collective-permute-done((f32[112,128]{1,0:T(8,128)S(1)}, f32[112,128]{1,0:T(8,128)S(1)}, u32[]{:S(2)}, u32[]{:S(2)}) %collective-permute-start.8) | collective-permute-done | bytes 57376 | tf_op jit(solution)/shard_map/ppermute | solution.py:420
  25.9 1.6 %collective-permute-start.13 = (f32[112,128]{1,0:T(8,128)S(1)}, f32[112,128]{1,0:T(8,128)S(1)}, u32[]{:S(2)}, u32[]{:S(2)}) collective-permute-start(f32[112,128]{1,0:T(8,128)S(1)} %add_add_fusion.refs_0_), channel_id=1, source_target_pairs={{0,4},{1,5},{2,6},{3,7},{4,0},{5,1},{6,2},{7,3},{8,12},{9,13},{10,... | collective-permute-start | bytes 172040 | tf_op jit(solution)/shard_map/ppermute | solution.py:420
  27.5 1.3 %collective-permute-start.11 = (f32[112,128]{1,0:T(8,128)S(1)}, f32[112,128]{1,0:T(8,128)S(1)}, u32[]{:S(2)}, u32[]{:S(2)}) collective-permute-start(f32[112,128]{1,0:T(8,128)S(1)} %add_add_fusion.refs_0_), channel_id=1, source_target_pairs={{0,3},{1,2},{2,1},{3,0},{4,7},{5,6},{6,5},{7,4},{8,11},{9,10},{10,... | collective-permute-start | bytes 172040 | tf_op jit(solution)/shard_map/ppermute | solution.py:420
  28.8 2.0 %collective-permute-done.15.refs_3_ = f32[112,128]{1,0:T(8,128)S(1)} collective-permute-done((f32[112,128]{1,0:T(8,128)S(1)}, f32[112,128]{1,0:T(8,128)S(1)}, u32[]{:S(2)}, u32[]{:S(2)}) %collective-permute-start.15) | collective-permute-done | bytes 57376 | tf_op jit(solution)/shard_map/ppermute | solution.py:420
  30.8 1.0 %collective-permute-done.13.refs_2_ = f32[112,128]{1,0:T(8,128)S(1)} collective-permute-done((f32[112,128]{1,0:T(8,128)S(1)}, f32[112,128]{1,0:T(8,128)S(1)}, u32[]{:S(2)}, u32[]{:S(2)}) %collective-permute-start.13) | collective-permute-done | bytes 57376 | tf_op jit(solution)/shard_map/ppermute | solution.py:420
  32.5 1.5 %shard_map.81.inner = bf16[2,576,512]{2,1,0:T(8,128)(2,1)S(1)} custom-call(s32[1,2,27]{2,1,0:T(2,128)S(1)} %get-tuple-element.24.near, bf16[3,64,512]{2,1,0:T(8,128)(2,1)S(1)} %get-tuple-element.28.gradient.own, bf16[256,384]{1,0:T(8,128)(2,1)S(1)} %get-tuple-element.34.select_y, bf16[256,384]{1,0:T(8,128)(2,1)S(1)} %get-tuple-element.35.select_z), custom_call_target="tpu_custom_call" | custom-call | flops 100000000 | bytes 1000000 | tf_op jit(solution)/shard_map/pallas_call | solution.py:463
  34.4 1.9 %collective-permute-done.other = bf16[2,64,128]{2,1,0:T(8,128)(2,1)S(1)} collective-permute-done((bf16[2,64,128]{2,1,0:T(8,128)(2,1)S(1)}, bf16[2,64,128]{2,1,0:T(8,128)(2,1)S(1)}, u32[]{:S(2)}, u32[]{:S(2)}) %collective-permute-start) | collective-permute-done | bytes 32800 | tf_op jit(solution)/shard_map/ppermute | solution.py:502
  36.3 2.2 %shard_map.80 = (bf16[1,2,64,512]{3,2,1,0:T(8,128)(2,1)}, bf16[2,576,128]{2,1,0:T(8,128)(2,1)S(1)}) custom-call(s32[1,2,27]{2,1,0:T(2,128)S(1)} %get-tuple-element.24.near, bf16[2,64,128]{2,1,0:T(8,128)(2,1)S(1)} %get-tuple-element.25.facing.mine, bf16[2,64,128]{2,1,0:T(8,128)(2,1)S(1)} %collective-permute-done.other, ...), custom_call_target="tpu_custom_call" | custom-call | flops 100000000 | bytes 1000000 | tf_op jit(solution)/shard_map/pallas_call | solution.py:463
  38.5 1.4 %shard_map.82 = bf16[1,2,64,512]{3,2,1,0:T(8,128)(2,1)} custom-call(bf16[192,576]{1,0:T(8,128)(2,1)S(1)} %get-tuple-element.39.table, bf16[2,576,512]{2,1,0:T(8,128)(2,1)S(1)} %shard_map.81.inner, bf16[2,576,128]{2,1,0:T(8,128)(2,1)S(1)} %get-tuple-element.36.ends, bf16[2,576,128]{2,1,0:T(8,128)(2,1)S(1)} %get-tuple-element.40.more_ends, ...), custom_call_target="tpu_custom_call" | custom-call | flops 100000000 | bytes 1000000 | tf_op jit(solution)/shard_map/pallas_call | solution.py:463
  39.9 0.9 %unpack.2.refs_4_ = f32[27,64,64]{2,1,0:T(8,128)} custom-call(f32[112,128]{1,0:T(8,128)S(1)} %add_add_fusion.refs_0_, f32[112,128]{1,0:T(8,128)S(1)} %collective-permute-done.11.refs_1_, f32[112,128]{1,0:T(8,128)S(1)} %collective-permute-done.13.refs_2_, f32[112,128]{1,0:T(8,128)S(1)} %collective-permute-done.15.refs_3_), custom_call_target="tpu_custom_call" | custom-call | flops 1000000 | bytes 1000000 | tf_op jit(solution)/shard_map/unpack/pallas_call | solution.py:538
  40.9 1.0 %unpack.3 = f32[27,64,64]{2,1,0:T(8,128)} custom-call(f32[112,128]{1,0:T(8,128)S(1)} %collective-permute-done.10.refs_0_, f32[112,128]{1,0:T(8,128)S(1)} %collective-permute-done.12.refs_1_, f32[112,128]{1,0:T(8,128)S(1)} %collective-permute-done.14.refs_2_, f32[112,128]{1,0:T(8,128)S(1)} %collective-permute-done.16.refs_3_, ...), custom_call_target="tpu_custom_call", output_to_operand_aliasing={{}: (4, {})} | custom-call | flops 1000000 | bytes 1000000 | tf_op jit(solution)/shard_map/unpack/pallas_call | solution.py:538
  (26 shorter events, 2.0 us)
Async XLA Ops:
  1.8 5.1 %collective-permute-start.1 = (bf16[2,64,128]{2,1,0:T(8,128)(2,1)S(1)}, bf16[2,64,128]{2,1,0:T(8,128)(2,1)S(1)}, u32[]{:S(2)}, u32[]{:S(2)}) collective-permute-start(bf16[2,64,128]{2,1,0:T(8,128)(2,1)S(1)} %get-tuple-element.29.mine), channel_id=1, source_target_pairs={{0,4},{4,8},{8,12},{12,16},{16,20},{20,24},{24,28},{28,29},{29,25}... | collective-permute-start | bytes 98312 | tf_op jit(solution)/shard_map/ppermute | solution.py:501
  7.8 4.4 %collective-permute-start.2 = (f32[336,128]{1,0:T(8,128)S(1)}, f32[336,128]{1,0:T(8,128)S(1)}, u32[]{:S(2)}, u32[]{:S(2)}) collective-permute-start(f32[336,128]{1,0:T(8,128)S(1)} %get-tuple-element.42), channel_id=1, source_target_pairs={{0,1},{1,0},{2,3},{3,2},{4,5},{5,4},{6,7},{7,6},{8,9},{9,8},{10,11... | collective-permute-start | bytes 516104 | tf_op jit(solution)/shard_map/ppermute | solution.py:420
  7.8 1.5 %collective-permute-start.5 = (f32[112,128]{1,0:T(8,128)S(1)}, f32[112,128]{1,0:T(8,128)S(1)}, u32[]{:S(2)}, u32[]{:S(2)}) collective-permute-start(f32[112,128]{1,0:T(8,128)S(1)} %get-tuple-element.44), channel_id=1, source_target_pairs={{0,1},{1,0},{2,3},{3,2},{4,5},{5,4},{6,7},{7,6},{8,9},{9,8},{10,11... | collective-permute-start | bytes 172040 | tf_op jit(solution)/shard_map/ppermute | solution.py:420
  9.3 5.2 %collective-permute-start.6 = (f32[112,128]{1,0:T(8,128)S(1)}, f32[112,128]{1,0:T(8,128)S(1)}, u32[]{:S(2)}, u32[]{:S(2)}) collective-permute-start(f32[112,128]{1,0:T(8,128)S(1)} %add.27), channel_id=1, source_target_pairs={{0,7},{1,6},{2,5},{3,4},{4,3},{5,2},{6,1},{7,0},{8,15},{9,14},{10,... | collective-permute-start | bytes 172040 | tf_op jit(solution)/shard_map/ppermute | solution.py:420
  12.2 21.8 %copy-start = (bf16[27,64,64]{2,1,0:T(8,128)(2,1)S(1)}, bf16[27,64,64]{2,1,0:T(8,128)(2,1)}, u32[]{:S(2)}) copy-start(bf16[27,64,64]{2,1,0:T(8,128)(2,1)} %weight.1) | copy-start | bytes 663556
  12.2 3.9 %collective-permute-start.3 = (f32[112,128]{1,0:T(8,128)S(1)}, f32[112,128]{1,0:T(8,128)S(1)}, u32[]{:S(2)}, u32[]{:S(2)}) collective-permute-start(f32[112,128]{1,0:T(8,128)S(1)} %get-tuple-element.45), channel_id=1, source_target_pairs={{0,3},{1,2},{2,1},{3,0},{4,7},{5,6},{6,5},{7,4},{8,11},{9,10},{10,... | collective-permute-start | bytes 172040 | tf_op jit(solution)/shard_map/ppermute | solution.py:420
  12.7 4.2 %collective-permute-start.4 = (f32[112,128]{1,0:T(8,128)S(1)}, f32[112,128]{1,0:T(8,128)S(1)}, u32[]{:S(2)}, u32[]{:S(2)}) collective-permute-start(f32[112,128]{1,0:T(8,128)S(1)} %get-tuple-element.46), channel_id=1, source_target_pairs={{0,4},{1,5},{2,6},{3,7},{4,0},{5,1},{6,2},{7,3},{8,12},{9,13},{10,... | collective-permute-start | bytes 172040 | tf_op jit(solution)/shard_map/ppermute | solution.py:420
  16.9 6.4 %collective-permute-start.9 = (f32[112,128]{1,0:T(8,128)S(1)}, f32[112,128]{1,0:T(8,128)S(1)}, u32[]{:S(2)}, u32[]{:S(2)}) collective-permute-start(f32[112,128]{1,0:T(8,128)S(1)} %fusion.1), channel_id=1, source_target_pairs={{0,24},{1,25},{2,26},{3,27},{4,28},{5,29},{6,30},{7,31},{8,16},{9,... | collective-permute-start | bytes 172040 | tf_op jit(solution)/shard_map/ppermute | solution.py:420
  20.7 5.1 %collective-permute-start.8 = (f32[112,128]{1,0:T(8,128)S(1)}, f32[112,128]{1,0:T(8,128)S(1)}, u32[]{:S(2)}, u32[]{:S(2)}) collective-permute-start(f32[112,128]{1,0:T(8,128)S(1)} %fusion.1), channel_id=1, source_target_pairs={{0,16},{1,17},{2,18},{3,19},{4,20},{5,21},{6,22},{7,23},{8,24},{9,... | collective-permute-start | bytes 172040 | tf_op jit(solution)/shard_map/ppermute | solution.py:420
  20.7 5.1 %collective-permute-start.7 = (f32[112,128]{1,0:T(8,128)S(1)}, f32[112,128]{1,0:T(8,128)S(1)}, u32[]{:S(2)}, u32[]{:S(2)}) collective-permute-start(f32[112,128]{1,0:T(8,128)S(1)} %fusion.1), channel_id=1, source_target_pairs={{0,8},{1,9},{2,10},{3,11},{4,12},{5,13},{6,14},{7,15},{8,0},{9,1},... | collective-permute-start | bytes 172040 | tf_op jit(solution)/shard_map/ppermute | solution.py:420
  25.8 5.0 %collective-permute-start.15 = (f32[112,128]{1,0:T(8,128)S(1)}, f32[112,128]{1,0:T(8,128)S(1)}, u32[]{:S(2)}, u32[]{:S(2)}) collective-permute-start(f32[112,128]{1,0:T(8,128)S(1)} %add_add_fusion.refs_0_), channel_id=1, source_target_pairs={{0,7},{1,6},{2,5},{3,4},{4,3},{5,2},{6,1},{7,0},{8,15},{9,14},{10,... | collective-permute-start | bytes 172040 | tf_op jit(solution)/shard_map/ppermute | solution.py:420
  25.9 6.0 %collective-permute-start.13 = (f32[112,128]{1,0:T(8,128)S(1)}, f32[112,128]{1,0:T(8,128)S(1)}, u32[]{:S(2)}, u32[]{:S(2)}) collective-permute-start(f32[112,128]{1,0:T(8,128)S(1)} %add_add_fusion.refs_0_), channel_id=1, source_target_pairs={{0,4},{1,5},{2,6},{3,7},{4,0},{5,1},{6,2},{7,3},{8,12},{9,13},{10,... | collective-permute-start | bytes 172040 | tf_op jit(solution)/shard_map/ppermute | solution.py:420
  27.5 4.4 %collective-permute-start.11 = (f32[112,128]{1,0:T(8,128)S(1)}, f32[112,128]{1,0:T(8,128)S(1)}, u32[]{:S(2)}, u32[]{:S(2)}) collective-permute-start(f32[112,128]{1,0:T(8,128)S(1)} %add_add_fusion.refs_0_), channel_id=1, source_target_pairs={{0,3},{1,2},{2,1},{3,0},{4,7},{5,6},{6,5},{7,4},{8,11},{9,10},{10,... | collective-permute-start | bytes 172040 | tf_op jit(solution)/shard_map/ppermute | solution.py:420
  28.8 12.1 %collective-permute-start.10 = (f32[112,128]{1,0:T(8,128)S(1)}, f32[112,128]{1,0:T(8,128)S(1)}, u32[]{:S(2)}, u32[]{:S(2)}) collective-permute-start(f32[112,128]{1,0:T(8,128)S(1)} %add_add_fusion.refs_0_), channel_id=1, source_target_pairs={{0,1},{1,0},{2,3},{3,2},{4,5},{5,4},{6,7},{7,6},{8,9},{9,8},{10,11... | collective-permute-start | bytes 172040 | tf_op jit(solution)/shard_map/ppermute | solution.py:420
  30.8 10.1 %collective-permute-start.16 = (f32[112,128]{1,0:T(8,128)S(1)}, f32[112,128]{1,0:T(8,128)S(1)}, u32[]{:S(2)}, u32[]{:S(2)}) collective-permute-start(f32[112,128]{1,0:T(8,128)S(1)} %collective-permute-done.15.refs_3_), channel_id=1, source_target_pairs={{0,1},{1,0},{2,3},{3,2},{4,5},{5,4},{6,7},{7,6},{8,9},{9,8},{10,11... | collective-permute-start | bytes 172040 | tf_op jit(solution)/shard_map/ppermute | solution.py:420
  31.9 9.0 %collective-permute-start.14 = (f32[112,128]{1,0:T(8,128)S(1)}, f32[112,128]{1,0:T(8,128)S(1)}, u32[]{:S(2)}, u32[]{:S(2)}) collective-permute-start(f32[112,128]{1,0:T(8,128)S(1)} %collective-permute-done.13.refs_2_), channel_id=1, source_target_pairs={{0,1},{1,0},{2,3},{3,2},{4,5},{5,4},{6,7},{7,6},{8,9},{9,8},{10,11... | collective-permute-start | bytes 172040 | tf_op jit(solution)/shard_map/ppermute | solution.py:420
  32.0 8.9 %collective-permute-start.12 = (f32[112,128]{1,0:T(8,128)S(1)}, f32[112,128]{1,0:T(8,128)S(1)}, u32[]{:S(2)}, u32[]{:S(2)}) collective-permute-start(f32[112,128]{1,0:T(8,128)S(1)} %collective-permute-done.11.refs_1_), channel_id=1, source_target_pairs={{0,1},{1,0},{2,3},{3,2},{4,5},{5,4},{6,7},{7,6},{8,9},{9,8},{10,11... | collective-permute-start | bytes 172040 | tf_op jit(solution)/shard_map/ppermute | solution.py:420
  32.4 3.9 %collective-permute-start = (bf16[2,64,128]{2,1,0:T(8,128)(2,1)S(1)}, bf16[2,64,128]{2,1,0:T(8,128)(2,1)S(1)}, u32[]{:S(2)}, u32[]{:S(2)}) collective-permute-start(bf16[2,64,128]{2,1,0:T(8,128)(2,1)S(1)} %get-tuple-element.25.facing.mine), channel_id=1, source_target_pairs={{4,0},{8,4},{12,8},{16,12},{20,16},{24,20},{28,24},{29,28},{25,29}... | collective-permute-start | bytes 98312 | tf_op jit(solution)/shard_map/ppermute | solution.py:502
